TPU v7x, 256 devices: a whole 4x4x8 slice. The times are simulated.
256 devices in a mesh: gx: 32 (over x, z), gy: 4 (over y), gz: 2 (over core).
Axes of the slice: x: 4, y: 4, z: 8, core: 2. Of those that a mesh axis runs over, the one named last changes fastest.
Arguments:
- offsets: float32 [3, 32, 8, 16, 128], P(None, 'gx', 'gy', 'gz'), may hold values from 0 to 1
- counts: int32 [32, 8, 16], P('gx', 'gy', 'gz'), may hold values from 32 to 128
- correction: float32 [32, 8, 16, 128], P('gx', 'gy', 'gz'), may hold values from 0.25 to 1.75
- dirichlet: float32 [32, 8, 16, 128], P('gx', 'gy', 'gz'), may hold values from 0.05 to 1
- right_side: float32 [32, 8, 16, 128], P('gx', 'gy', 'gz'), may hold values from -15 to 15
- deflation: float32 [64, 32, 8, 16, 128], P(None, 'gx', 'gy', 'gz'), may hold values from -0.5 to 0.5
- coarse_inverse: float32 [16384, 16384], P(('gx', 'gy', 'gz')), may hold values from -1 to 2.5, as said below
Outputs:
- pressure: float32 [32, 8, 16, 128], P('gx', 'gy', 'gz')
- residual: float32 [32, 8, 16, 128], P('gx', 'gy', 'gz')
- direction: float32 [32, 8, 16, 128], P('gx', 'gy', 'gz')
Inputs may be any that keep to these rules, and one draw needn't show every extreme that they name: coarse_inverse is symmetric and positive definite.
All inputs are finite; a program needn't handle non-finite values.
Results may differ from a plain program's by a relative error of at most 0.0003.
Values sent between devices are 32-bit elements; how exact they have to be, the bound alone decides.
No kernel may reach another device: no remote copies, remote signals or barrier semaphores. Data moves between devices by JAX's collectives and lax.ppermute only.
A program may use at most 64 MiB of HBM per device.

v0:
```python
import jax
import jax.numpy as jnp
from jax import lax
from jax.sharding import PartitionSpec as P

SLOTS = 128
ITERS = 2


def extended(x, sides, width):
    for axis, dim in sides:
        size, length = (lax.axis_size(axis), x.shape[dim])
        up = [(i, (i + 1) % size) for i in range(size - 1)]
        down = [(j, i) for i, j in up]
        last = lax.slice_in_dim(x, length - width, length, axis=dim)
        leading = lax.slice_in_dim(x, 0, width, axis=dim)
        before = lax.ppermute(last, axis, up)
        after = lax.ppermute(leading, axis, down)
        x = jnp.concatenate([before, x, after], axis=dim)
    return x


def pair_weights(centre, beside, shifts):
    delta_first = beside[0][..., None, :] + shifts[0] - centre[0][..., :, None]
    delta_second = beside[1][..., None, :] + shifts[1] - centre[1][..., :, None]
    delta_third = beside[2][..., None, :] + shifts[2] - centre[2][..., :, None]
    squared = delta_first * delta_first + delta_second * delta_second + delta_third * delta_third
    radius = jnp.sqrt(squared)
    falloff = jnp.maximum(1.0 - radius, 0.0)
    weight = 20.0 * squared * falloff * falloff * falloff / (squared + 0.01) / SLOTS
    weight = weight * centre[3][..., :, None] * beside[3][..., None, :]
    return weight * (0.5 * (centre[4][..., :, None] + beside[4][..., None, :]))


def neighbour_sum(padded_geometry, padded_field):
    centre = padded_geometry[:, 1:-1, 1:-1, 1:-1, :]
    extent = centre.shape
    blank_sum = jnp.zeros(extent[1:], jnp.float32)

    def visit(offset_index, running):
        offset_index = jnp.asarray(offset_index).astype(jnp.int32)
        first_shift = offset_index // 9
        second_shift = offset_index // 3 % 3
        third_shift = offset_index % 3
        zero_start = jnp.zeros((), jnp.int32)
        beside = lax.dynamic_slice(
            padded_geometry,
            (zero_start, first_shift, second_shift, third_shift, zero_start),
            extent,
        )
        shifts = (
            (first_shift - 1).astype(jnp.float32),
            (second_shift - 1).astype(jnp.float32),
            (third_shift - 1).astype(jnp.float32),
        )
        weight = pair_weights(centre, beside, shifts)
        if padded_field is None:
            return running + jnp.sum(weight, -1)
        beside_field = lax.dynamic_slice(
            padded_field, (first_shift, second_shift, third_shift, zero_start), extent[1:]
        )
        centre_field = padded_field[1:-1, 1:-1, 1:-1, :]
        return running + jnp.sum(
            weight * (centre_field[..., :, None] - beside_field[..., None, :]), -1
        )

    return lax.fori_loop(0, 27, visit, blank_sum)


def per_device(offsets, counts, correction, dirichlet, right_side, deflation, coarse_inverse):
    slot_index = jnp.arange(SLOTS, dtype=jnp.int32)
    live_mask = (slot_index < counts[..., None]).astype(jnp.float32)
    geometry = jnp.concatenate([offsets, live_mask[None], correction[None]], 0)
    padded_geometry = extended(geometry, (("gx", 1), ("gy", 2), ("gz", 3)), 1)
    diagonal = dirichlet + neighbour_sum(padded_geometry, None)
    flat_basis = deflation.reshape(deflation.shape[0], -1)

    def apply_matrix(field):
        padded_field = extended(field, (("gx", 0), ("gy", 1), ("gz", 2)), 1)
        return live_mask * dirichlet * field + neighbour_sum(padded_geometry, padded_field)

    def precondition(current):
        coefficient = jnp.dot(flat_basis, current.reshape(-1), precision=lax.Precision.HIGHEST)
        coarse_value = jnp.dot(
            coarse_inverse,
            lax.all_gather(coefficient, ("gx", "gy", "gz"), axis=0, tiled=True),
            precision=lax.Precision.HIGHEST,
        )
        lifted = jnp.dot(coarse_value, flat_basis, precision=lax.Precision.HIGHEST).reshape(
            current.shape
        )
        return live_mask * (current / diagonal + lifted)

    residual = right_side * live_mask
    pressure = jnp.zeros_like(residual)

    def global_inner(left_field, right_field):
        return lax.psum(jnp.sum(left_field * right_field), ("gx", "gy", "gz"))

    smoothed = precondition(residual)
    direction = smoothed
    inner_now = global_inner(residual, smoothed)

    def iterate(step_number, state_tuple):
        pressure, residual, direction, inner_now = state_tuple
        product_field = apply_matrix(direction)
        step_size = inner_now / lax.psum(jnp.sum(direction * product_field), ("gx", "gy", "gz"))
        pressure = pressure + step_size * direction
        residual = residual - step_size * product_field
        smoothed = precondition(residual)
        inner_next = global_inner(residual, smoothed)
        direction = smoothed + inner_next / inner_now * direction
        return (pressure, residual, direction, inner_next)

    pressure, residual, direction, inner_now = lax.fori_loop(
        0, ITERS, iterate, (pressure, residual, direction, inner_now)
    )
    return (pressure, residual, direction)


def solution(mesh):
    in_specs = (
        P(None, "gx", "gy", "gz", None),
        P("gx", "gy", "gz"),
        P("gx", "gy", "gz", None),
        P("gx", "gy", "gz", None),
        P("gx", "gy", "gz", None),
        P(None, "gx", "gy", "gz", None),
        P(("gx", "gy", "gz"), None),
    )
    out_specs = (P("gx", "gy", "gz", None), P("gx", "gy", "gz", None), P("gx", "gy", "gz", None))
    return jax.shard_map(
        per_device, mesh=mesh, in_specs=in_specs, out_specs=out_specs, check_vma=False
    )
```

profile of v0, /device:TPU:1, one launch (start us, length us, event | category | flops | bytes accessed | tf_op | source)
XLA Modules:
  0.0 1402.0 jit_solution(15801425661661029320)
XLA Ops:
  10.0 5.0 collective-permute-start.6
  21.8 4.0 collective-permute-start.8
  25.8 238.6 %all-reduce.8.cloned.1.call-done = f32[16384]{0:T(1024)} async-done(((f32[16384]{0:T(1024)}), f32[16384]{0:T(1024)}) %all-reduce.8.cloned.1.call-update) | async-done | bytes 65552
  264.4 5.6 convolution_bitcast_fusion.2
  275.0 63.1 %while.63 = (s32[]{:T(128)}, f32[1,2,8,128]{3,2,1,0:T(8,128)S(1)}, f32[5,3,4,10,128]{4,3,2,1,0:T(8,128)S(1)}, f32[3,1,2,8,128]{4,3,2,1,0:T(8,128)S(1)}, f32[1,2,...) while((s32[]{:T(128)}, f32[1,2,8,128]{3,2,1,0:T(8,128)S(1)}, ...), condition=%wide.region_2.3_spmd.clone, body=%wide.region_0.2_spmd.clone.sunk | while | flops 5779502 | bytes 254675 | solution.py:67
  338.8 75.3 %psum.29 = f32[]{:T(128)} all-reduce(f32[]{:T(128)} %get-tuple-element.808), channel_id=1, replica_groups=mesh['gx'=32,'gy'=4,'gz'=2] {'gx','gy','gz'}, use_global_device_ids=true, to_apply=%region_4.5 | all-reduce | flops 1 | bytes 8 | tf_op jit(solution)/shard_map/psum | solution.py:98
  414.1 980.7 %while.65 = (s32[]{:T(128)}, f32[1,2,8,128]{3,2,1,0:T(8,128)S(1)}, f32[1,2,8,128]{3,2,1,0:T(8,128)S(1)}, f32[1,2,8,128]{3,2,1,0:T(8,128)S(1)}, f32[]{:T(128)}, /...) while((s32[]{:T(128)}, f32[1,2,8,128]{3,2,1,0:T(8,128)S(1)}, ...), condition=%wide.region_13.14_spmd.clone, body=%wide.region_5.13_spmd.clone.sunk | while | flops 22165556 | bytes 6994874 | solution.py:115
  414.1 3.7 collective-permute-start
  419.1 3.1 collective-permute-done.1
  423.4 4.0 collective-permute-start.3
  428.3 5.3 collective-permute-start.4
  436.6 71.3 %while.66 = (s32[]{:T(128)}, f32[1,2,8,128]{3,2,1,0:T(8,128)S(1)}, f32[5,3,4,10,128]{4,3,2,1,0:T(8,128)S(1)}, f32[3,1,2,8,128]{4,3,2,1,0:T(8,128)S(1)}, f32[1,2,...) while((s32[]{:T(128)}, f32[1,2,8,128]{3,2,1,0:T(8,128)S(1)}, ...), condition=%wide.region_8.8_spmd.clone, body=%wide.region_6.7_spmd.clone.sunk | while | flops 6301742 | bytes 295599 | solution.py:67
  436.8 2.4 fusion.68
  439.5 2.4 fusion.68
  442.1 2.4 fusion.68
  444.7 2.4 fusion.68
  447.4 2.4 fusion.68
  450.0 2.4 fusion.68
  452.7 2.4 fusion.68
  455.3 2.4 fusion.68
  457.9 2.4 fusion.68
  460.6 2.4 fusion.68
  463.2 2.4 fusion.68
  465.9 2.4 fusion.68
  468.5 2.4 fusion.68
  471.2 2.4 fusion.68
  473.8 2.4 fusion.68
  476.4 2.4 fusion.68
  479.1 2.4 fusion.68
  481.7 2.4 fusion.68
  484.4 2.4 fusion.68
  487.0 2.4 fusion.68
  489.6 2.4 fusion.68
  492.3 2.4 fusion.68
  494.9 2.4 fusion.68
  502.8 2.4 fusion.68
  508.6 75.5 %psum.34 = f32[]{:T(128)} all-reduce(f32[]{:T(128)} %multiply_reduce_fusion.5), channel_id=1, replica_groups=mesh['gx'=32,'gy'=4,'gz'=2] {'gx','gy','gz'}, use_global_device_ids=true, to_apply=%region_10.10 | all-reduce | flops 1 | bytes 8 | tf_op jit(solution)/shard_map/while/body/eval_jaxpr/psum | solution.py:107
  586.2 236.4 %all-reduce.10.cloned.1.call-done = f32[16384]{0:T(1024)} async-done(((f32[16384]{0:T(1024)}), f32[16384]{0:T(1024)}) %all-reduce.10.cloned.1.call-update) | async-done | bytes 65552 | tf_op jit(solution)/shard_map/while
  822.6 5.6 convolution_bitcast_fusion.7
  829.2 74.5 %psum.35 = f32[]{:T(128)} all-reduce(f32[]{:T(128)} %multiply_reduce_fusion.6), channel_id=1, replica_groups=mesh['gx'=32,'gy'=4,'gz'=2] {'gx','gy','gz'}, use_global_device_ids=true, to_apply=%region_12.12 | all-reduce | flops 1 | bytes 8 | tf_op jit(solution)/shard_map/while/body/eval_jaxpr/psum | solution.py:98
  904.4 3.7 collective-permute-start
  909.4 3.1 collective-permute-done.1
  913.8 4.0 collective-permute-start.3
  918.6 5.3 collective-permute-start.4
  927.0 71.3 %while.66 = (s32[]{:T(128)}, f32[1,2,8,128]{3,2,1,0:T(8,128)S(1)}, f32[5,3,4,10,128]{4,3,2,1,0:T(8,128)S(1)}, f32[3,1,2,8,128]{4,3,2,1,0:T(8,128)S(1)}, f32[1,2,...) while((s32[]{:T(128)}, f32[1,2,8,128]{3,2,1,0:T(8,128)S(1)}, ...), condition=%wide.region_8.8_spmd.clone, body=%wide.region_6.7_spmd.clone.sunk | while | flops 6301742 | bytes 295599 | solution.py:67
  929.8 2.4 fusion.68
  932.4 2.4 fusion.68
  937.7 2.4 fusion.68
  945.6 2.4 fusion.68
  950.9 2.4 fusion.68
  953.6 2.4 fusion.68
  958.8 2.4 fusion.68
  961.5 2.4 fusion.68
  966.8 2.4 fusion.68
  972.0 2.4 fusion.68
  974.7 2.4 fusion.68
  980.0 2.4 fusion.68
  982.6 2.4 fusion.68
  987.9 2.4 fusion.68
  995.8 2.4 fusion.68
  998.9 75.3 %psum.34 = f32[]{:T(128)} all-reduce(f32[]{:T(128)} %multiply_reduce_fusion.5), channel_id=1, replica_groups=mesh['gx'=32,'gy'=4,'gz'=2] {'gx','gy','gz'}, use_global_device_ids=true, to_apply=%region_10.10 | all-reduce | flops 1 | bytes 8 | tf_op jit(solution)/shard_map/while/body/eval_jaxpr/psum | solution.py:107
  1076.4 236.6 %all-reduce.10.cloned.1.call-done = f32[16384]{0:T(1024)} async-done(((f32[16384]{0:T(1024)}), f32[16384]{0:T(1024)}) %all-reduce.10.cloned.1.call-update) | async-done | bytes 65552 | tf_op jit(solution)/shard_map/while
  1313.0 5.6 convolution_bitcast_fusion.7
  1319.6 74.5 %psum.35 = f32[]{:T(128)} all-reduce(f32[]{:T(128)} %multiply_reduce_fusion.6), channel_id=1, replica_groups=mesh['gx'=32,'gy'=4,'gz'=2] {'gx','gy','gz'}, use_global_device_ids=true, to_apply=%region_12.12 | all-reduce | flops 1 | bytes 8 | tf_op jit(solution)/shard_map/while/body/eval_jaxpr/psum | solution.py:98
  (387 shorter events, 133.2 us)
Async XLA Ops:
  7.2 262.9 %copy-start.7 = (f32[1,2,8,128]{3,2,1,0:T(8,128)S(1)}, f32[1,2,8,128]{3,2,1,0:T(8,128)}, u32[]{:S(2)}) copy-start(f32[1,2,8,128]{3,2,1,0:T(8,128)} %param.15) | copy-start | bytes 24580
  7.2 262.9 %copy-start = (f32[3,1,2,8,128]{4,3,2,1,0:T(8,128)S(1)}, f32[3,1,2,8,128]{4,3,2,1,0:T(8,128)}, u32[]{:S(2)}) copy-start(f32[3,1,2,8,128]{4,3,2,1,0:T(8,128)} %param.13) | copy-start | bytes 73732
  7.2 257.2 %all-reduce.8.cloned.1.call-start = ((), (), s32[]{:S(2)}) async-start(), calls=%async_computation | async-start | bytes 131072
  8.7 11.0 collective-permute-start.7
  10.0 9.7 collective-permute-start.6
  17.7 0.6 copy-start.5
  18.4 256.6 %copy-start.4 = (s32[1,2,8]{2,1,0:T(2,128)S(1)}, s32[1,2,8]{2,1,0:T(2,128)}, u32[]{:S(2)}) copy-start(s32[1,2,8]{2,1,0:T(2,128)} %param.14) | copy-start | bytes 196
  20.5 249.5 %collective-permute-start.9 = (f32[5,3,1,8,128]{4,3,2,1,0:T(8,128)S(1)}, f32[5,3,1,8,128]{4,3,2,1,0:T(8,128)S(1)}, u32[]{:S(2)}, u32[]{:S(2)}) collective-permute-start(f32[5,3,1,8,128]{4,3,2,1,0:T(8,128)S(1)} %get-tuple-element.846), channel_id=1, source_target_pairs={{2,0},{4,2},{6,4},{3,1},{5,3},{7,5},{10,8},{12,10},{14,12},{11,9},... | collective-permute-start | bytes 184328 | tf_op jit(solution)/shard_map/ppermute | solution.py:18
  21.8 248.2 %collective-permute-start.8 = (f32[5,3,1,8,128]{4,3,2,1,0:T(8,128)S(1)}, f32[5,3,1,8,128]{4,3,2,1,0:T(8,128)S(1)}, u32[]{:S(2)}, u32[]{:S(2)}) collective-permute-start(f32[5,3,1,8,128]{4,3,2,1,0:T(8,128)S(1)} %get-tuple-element.845), channel_id=1, source_target_pairs={{0,2},{2,4},{4,6},{1,3},{3,5},{5,7},{8,10},{10,12},{12,14},{9,11},... | collective-permute-start | bytes 184328 | tf_op jit(solution)/shard_map/ppermute | solution.py:17
  264.4 73.7 %copy-start.8 = (f32[1,2,8,128]{3,2,1,0:T(8,128)S(1)}, f32[1,2,8,128]{3,2,1,0:T(8,128)}, u32[]{:S(2)}) copy-start(f32[1,2,8,128]{3,2,1,0:T(8,128)} %param.17) | copy-start | bytes 24580
  264.4 73.7 %copy-start.9 = (f32[1,2,8,128]{3,2,1,0:T(8,128)S(1)}, f32[1,2,8,128]{3,2,1,0:T(8,128)}, u32[]{:S(2)}) copy-start(f32[1,2,8,128]{3,2,1,0:T(8,128)} %param.16) | copy-start | bytes 24580
  270.1 3.5 collective-permute-start.11
  271.8 3.1 collective-permute-start.10
  414.1 408.5 %all-reduce.10.cloned.1.call-start = ((), (), s32[]{:S(2)}) async-start(), calls=%async_computation.1 | async-start | bytes 131072 | tf_op jit(solution)/shard_map/while
  414.1 5.0 collective-permute-start
  417.7 4.4 collective-permute-start.1
  422.1 5.3 collective-permute-start.2
  423.4 4.8 collective-permute-start.3
  428.3 7.3 collective-permute-start.4
  433.6 3.1 collective-permute-start.5
  585.5 0.6 copy-start.1
  904.4 408.6 %all-reduce.10.cloned.1.call-start = ((), (), s32[]{:S(2)}) async-start(), calls=%async_computation.1 | async-start | bytes 131072 | tf_op jit(solution)/shard_map/while
  904.4 5.0 collective-permute-start
  908.1 4.4 collective-permute-start.1
  912.5 5.3 collective-permute-start.2
  913.8 4.8 collective-permute-start.3
  918.6 7.3 collective-permute-start.4
  923.9 3.1 collective-permute-start.5
  1075.7 0.6 copy-start.1
  1394.8 0.6 copy-start.2
  1394.8 0.6 copy-start.3
  1394.8 0.6 copy-start.6
Sparse Core Ops, SparseCore 0:
  18.5 245.8 all-reduce.7
  586.3 236.1 all-reduce.9
  1076.5 236.4 all-reduce.9
where the time goes:
time: 1400 us
  waiting for transfers between devices  723 us (52%)
  blocking collectives  375 us (27%)
  other arithmetic  202 us (14%)
  starting transfers between devices  48.2 us (3%)
  matrix products  20.6 us (1%)
  loops' own time  15.2 us (1%)
    while x4, waiting for transfers between devices  473 us
    unnamed x2, waiting for transfers between devices  239 us
    psum x3, blocking collectives, global_inner(): return lax.psum(jnp.sum(left_field * right_field), ('gx', 'gy', 'gz'))  224 us
    psum x2, blocking collectives, iterate(): lax.psum(jnp.sum(direction * product_field), ('gx', 'gy', 'gz'))  151 us
    reduce_sum x54, other arithmetic, visit(): jnp.sum(weight * (centre_field[..., :, None] - beside_field[..., None, :]...  132 us
    reduce_sum x27, other arithmetic, visit(): return running + jnp.sum(weight, -1)  56.9 us
    ppermute x9, starting transfers between devices, extended(): before = lax.ppermute(last, axis, up)  28.2 us
  transfers between devices with their start and end apart: 21, of which 10 were waited for; matrix products, arithmetic and copies ran while one was open for 1% of the time, Pallas kernels for 0%

commit v1 on v0

v1 whole, which is shorter than its diff:
```python
import jax
import jax.numpy as jnp
from jax import lax
from jax.experimental import pallas as pl
from jax.experimental.pallas import tpu as pltpu
from jax.sharding import PartitionSpec as P

SLOTS = 128
FAR = 1000.0

VM = pl.BlockSpec(memory_space=pltpu.VMEM)
SM = pl.BlockSpec(memory_space=pltpu.SMEM)


def f32(*shape):
    return jax.ShapeDtypeStruct(shape, jnp.float32)


def call(kernel, outs, ins, scratch=(), limit=None):
    return pl.pallas_call(
        kernel,
        out_shape=outs,
        in_specs=ins,
        out_specs=jax.tree.map(lambda _: VM, outs),
        scratch_shapes=scratch,
        compiler_params=pltpu.CompilerParams(vmem_limit_bytes=limit),
    )


def project(basis_ref, field, part_ref, second):
    for k in range(64):
        prod = basis_ref[k, 0] * field[0] + basis_ref[k, 1] * field[1]
        part_ref[k : k + 1, :] = jnp.sum(prod, axis=0, keepdims=True)
    row = jnp.sum(part_ref[...].T, axis=0, keepdims=True)
    both = jnp.concatenate([row, row], axis=1)
    lane = lax.broadcasted_iota(jnp.int32, (1, SLOTS), 1)
    return jnp.where((lane >= 64) == (second == 1), both, 0.0)


def inner_row(pairs):
    lane = lax.broadcasted_iota(jnp.int32, (1, SLOTS), 1)
    row = jnp.zeros((1, SLOTS), jnp.float32)
    for at, (left, right) in enumerate(pairs):
        total = jnp.sum(left * right)
        row = jnp.where(lane == at, total, row)
    return row


def prepare_kernel(second_ref, counts_ref, right_ref, basis_ref, live_ref, residual_ref, payload_ref, part_ref):
    slot = lax.broadcasted_iota(jnp.int32, (1, SLOTS), 1)
    for y in range(2):
        for z in range(8):
            live_ref[y, z : z + 1, :] = jnp.where(slot < counts_ref[y * 8 + z], 1.0, 0.0)
    residual_ref[...] = right_ref[...] * live_ref[...]
    payload_ref[...] = project(basis_ref, residual_ref[...], part_ref, second_ref[0])


def assemble(own, before, after, below, above, across, second, put):
    for x, block in enumerate((before, own, after)):
        for y in range(4):
            if y == 0:
                rows = below(x)
            elif y == 3:
                rows = above(x)
            else:
                rows = block(y - 1)
            for z in range(8):
                put(x, y, z + 1, rows[z : z + 1])
            row = across(x * 4 + y)
            put(x, y, 0, jnp.where(second == 1, row, 0.0))
            put(x, y, 9, jnp.where(second == 0, row, 0.0))


def weights_kernel(
    second_ref, counts_ref, own_ref, before_ref, after_ref, below_ref, above_ref, across_ref,
    live_ref, dirichlet_ref, weight_ref, diagonal_ref, inverse_ref, near_ref, mine_ref, sums_ref,
):
    second = second_ref[0]
    tile = (8, SLOTS)
    for f in range(4):
        def put(x, y, z, row, f=f):
            if f == 3:
                near_ref[3, x, y, z] = jnp.broadcast_to(row, tile)
            else:
                near_ref[f, x, y, z] = jnp.broadcast_to(row + float((x, y, z)[f]), tile)

        assemble(
            lambda y: own_ref[f, y], lambda y: before_ref[f, y], lambda y: after_ref[f, y],
            lambda x: below_ref[f, x], lambda x: above_ref[f, x],
            lambda at: across_ref[f, at : at + 1], second, put,
        )
    dead = near_ref[3] == 0.0
    near_ref[0] = jnp.where(dead, FAR, near_ref[0])

    def one_cell(cell, _):
        y, z = cell // 8, cell % 8
        groups = (counts_ref[cell] + 7) // 8
        for f in range(4):
            row = near_ref[f, 1, y + 1, z + 1]
            if f == 0:
                row = jnp.where(near_ref[3, 1, y + 1, z + 1] == 0.0, -FAR, row)
            mine_ref[f] = jnp.broadcast_to(row.T[:, 0:1], (SLOTS, SLOTS))
        sums_ref[...] = jnp.zeros((SLOTS, SLOTS), jnp.float32)

        def one_group(group, _):
            here = pl.ds(pl.multiple_of(group * 8, 8), 8)
            mx, my, mz, mc = (mine_ref[f, here, :] for f in range(4))
            total = jnp.zeros(tile, jnp.float32)
            for at in range(27):
                a, b, c = at // 9, at // 3 % 3, at % 3
                dx = near_ref[0, a, y + b, z + c] - mx
                dy = near_ref[1, a, y + b, z + c] - my
                dz = near_ref[2, a, y + b, z + c] - mz
                square = dx * dx + dy * dy + dz * dz
                radius = square * lax.rsqrt(jnp.maximum(square, 1e-30))
                fall = jnp.maximum(1.0 - radius, 0.0)
                weight = (square * fall) * (fall * fall) / (square + 0.01)
                weight = weight * (near_ref[3, a, y + b, z + c] + mc)
                weight_ref[cell, group, at] = weight
                total = total + weight
            sums_ref[here, :] = total
            return 0

        lax.fori_loop(0, groups, one_group, 0)
        sums = jnp.sum(sums_ref[...].T, axis=0, keepdims=True)
        diagonal_ref[y, pl.ds(z, 1), :] = sums
        return 0

    lax.fori_loop(0, 16, one_cell, 0)
    sums = diagonal_ref[...]
    inverse_ref[...] = live_ref[...] / (dirichlet_ref[...] + sums)
    diagonal_ref[...] = live_ref[...] * dirichlet_ref[...] + sums


def coarse_lift(values_ref, coarse_ref, basis_ref, part_ref):
    total = jnp.zeros((64, SLOTS), jnp.float32)
    for t in range(128):
        total = total + coarse_ref[:, t * SLOTS : (t + 1) * SLOTS] * values_ref[t : t + 1, :]
    part_ref[...] = jnp.broadcast_to(jnp.sum(total, axis=1, keepdims=True), (64, SLOTS))
    sums = [[jnp.zeros((8, SLOTS), jnp.float32) for _ in range(2)] for _ in range(2)]
    for k in range(64):
        scale = jnp.broadcast_to(part_ref[k : k + 1, :], (8, SLOTS))
        for y in range(2):
            sums[k % 2][y] = sums[k % 2][y] + scale * basis_ref[k, y]
    return jnp.stack([sums[0][y] + sums[1][y] for y in range(2)])


def total_of(gathered_ref, at):
    rows = gathered_ref[pl.ds(1, 128, stride=2), :]
    lane = lax.broadcasted_iota(jnp.int32, rows.shape, 1)
    return jnp.sum(jnp.where(lane == at, rows, 0.0))


def first_smooth_kernel(gathered_ref, coarse_ref, basis_ref, live_ref, residual_ref, inverse_ref, smoothed_ref, part_ref):
    lifted = coarse_lift(gathered_ref, coarse_ref, basis_ref, part_ref)
    smoothed_ref[...] = residual_ref[...] * inverse_ref[...] + live_ref[...] * lifted


def second_smooth_kernel(
    gathered_ref, coefficient_ref, coarse_ref, basis_ref, live_ref, residual_ref, inverse_ref,
    smoothed_ref, image_ref, new_coefficient_ref, new_residual_ref, new_smoothed_ref, part_ref,
):
    step = total_of(gathered_ref, 0) / total_of(gathered_ref, 1)
    new_coefficient_ref[...] = coefficient_ref[...] - step * gathered_ref[pl.ds(0, 128, stride=2), :]
    lifted = coarse_lift(new_coefficient_ref, coarse_ref, basis_ref, part_ref)
    residual = residual_ref[...] - step * image_ref[...]
    new_residual_ref[...] = residual
    new_smoothed_ref[...] = residual * inverse_ref[...] + live_ref[...] * lifted


def third_smooth_kernel(
    gathered_ref, before_ref, coefficient_ref, coarse_ref, basis_ref, live_ref, residual_ref, inverse_ref,
    first_ref, first_image_ref, smoothed_ref, image_ref,
    pressure_ref, new_residual_ref, new_smoothed_ref, direction_ref, payload_ref, values_ref, part_ref,
):
    inner_first, curve_first = total_of(before_ref, 0), total_of(before_ref, 1)
    inner, curve = total_of(gathered_ref, 0), total_of(gathered_ref, 1)
    cross = total_of(gathered_ref, 2) + total_of(gathered_ref, 3)
    step_first = inner_first / curve_first
    ratio = inner / inner_first
    step = inner / (curve + ratio * (cross + ratio * curve_first))
    values_ref[...] = coefficient_ref[...] - step * (
        gathered_ref[pl.ds(0, 128, stride=2), :] + ratio * before_ref[pl.ds(0, 128, stride=2), :]
    )
    lifted = coarse_lift(values_ref, coarse_ref, basis_ref, part_ref)
    direction = smoothed_ref[...] + ratio * first_ref[...]
    direction_ref[...] = direction
    pressure_ref[...] = step_first * first_ref[...] + step * direction
    residual = residual_ref[...] - step * (image_ref[...] + ratio * first_image_ref[...])
    new_residual_ref[...] = residual
    smoothed = residual * inverse_ref[...] + live_ref[...] * lifted
    new_smoothed_ref[...] = smoothed
    payload_ref[...] = inner_row([(residual, smoothed), (residual_ref[...], smoothed_ref[...])])


def image_kernel(
    second_ref, counts_ref, weight_ref, own_ref, before_ref, after_ref, below_ref, above_ref, across_ref,
    diagonal_ref, residual_ref, basis_ref, *rest,
):
    olds, (image_ref, payload_ref, near_ref, sums_ref, part_ref) = rest[:-5], rest[-5:]
    second = second_ref[0]
    tile = (8, SLOTS)

    def put(x, y, z, row):
        near_ref[x, y, z] = jnp.broadcast_to(row, tile)

    assemble(
        lambda y: own_ref[y], lambda y: before_ref[y], lambda y: after_ref[y],
        lambda x: below_ref[x], lambda x: above_ref[x],
        lambda at: across_ref[at : at + 1], second, put,
    )

    def one_cell(cell, _):
        y, z = cell // 8, cell % 8
        groups = (counts_ref[cell] + 7) // 8
        sums_ref[...] = jnp.zeros((SLOTS, SLOTS), jnp.float32)

        def one_group(group, _):
            parts = [jnp.zeros(tile, jnp.float32) for _ in range(3)]
            for at in range(27):
                a, b, c = at // 9, at // 3 % 3, at % 3
                parts[at % 3] = parts[at % 3] + weight_ref[cell, group, at] * near_ref[a, y + b, z + c]
            sums_ref[pl.ds(pl.multiple_of(group * 8, 8), 8), :] = parts[0] + parts[1] + parts[2]
            return 0

        lax.fori_loop(0, groups, one_group, 0)
        image_ref[y, pl.ds(z, 1), :] = jnp.sum(sums_ref[...].T, axis=0, keepdims=True)
        return 0

    lax.fori_loop(0, 16, one_cell, 0)
    own = own_ref[...]
    image = diagonal_ref[...] * own - image_ref[...]
    image_ref[...] = image
    payload_ref[0:1, :] = project(basis_ref, image, part_ref, second)
    pairs = [(residual_ref[...], own), (own, image)]
    if olds:
        first_ref, first_image_ref = olds
        pairs += [(own, first_image_ref[...]), (first_ref[...], image)]
    payload_ref[1:2, :] = inner_row(pairs)


def steps(axis):
    size = lax.axis_size(axis)
    up = [(i, i + 1) for i in range(size - 1)]
    return up, [(j, i) for i, j in up]


def around(field, second):
    up, down = steps("gx")
    before = lax.ppermute(field, "gx", up)
    after = lax.ppermute(field, "gx", down)
    three = jnp.stack([before, field, after], axis=-4)
    up, down = steps("gy")
    below = lax.ppermute(three[..., :, 1, :, :], "gy", up)
    above = lax.ppermute(three[..., :, 0, :, :], "gy", down)
    full = jnp.concatenate([below[..., :, None, :, :], three, above[..., :, None, :, :]], axis=-3)
    face = jnp.where(second == 0, full[..., 7, :], full[..., 0, :])
    face = face.reshape(face.shape[:-3] + (12, SLOTS))
    across = lax.ppermute(face, "gz", [(0, 1), (1, 0)])
    return before, after, below, above, across


def gather(payload):
    both = payload + lax.ppermute(payload, "gz", [(0, 1), (1, 0)])
    rows = payload.shape[0]
    spread = jnp.broadcast_to(both[None], (128, rows, SLOTS))
    got = lax.all_to_all(spread, ("gx", "gy"), 0, 0, tiled=True)
    return got.reshape(128 * rows, SLOTS)


def per_device(offsets, counts, correction, dirichlet, right_side, deflation, coarse_inverse):
    second = lax.axis_index("gz").astype(jnp.int32)
    second_ref = second.reshape(1)
    cell_counts = counts.reshape(16)
    block = lambda x: x.reshape(2, 8, SLOTS)
    offsets = offsets.reshape(3, 2, 8, SLOTS)
    dirichlet, right_side = block(dirichlet), block(right_side)
    basis = deflation.reshape(64, 2, 8, SLOTS)
    cells = f32(2, 8, SLOTS)

    live, residual, payload = call(
        prepare_kernel, (cells, cells, f32(1, SLOTS)), [SM, SM, VM, VM], [pltpu.VMEM((64, SLOTS), jnp.float32)]
    )(second_ref, cell_counts, right_side, basis)
    scaled = (block(correction) * live) * (10.0 / SLOTS)
    geometry = jnp.concatenate([offsets, scaled[None]], 0)
    halo = around(geometry, second)
    coefficient = gather(payload)
    part = pltpu.VMEM((64, SLOTS), jnp.float32)

    weight, diagonal, inverse = call(
        weights_kernel,
        (f32(16, 16, 27, 8, SLOTS), cells, cells),
        [SM, SM] + [VM] * 8,
        [
            pltpu.VMEM((4, 3, 4, 10, 8, SLOTS), jnp.float32),
            pltpu.VMEM((4, SLOTS, SLOTS), jnp.float32),
            pltpu.VMEM((SLOTS, SLOTS), jnp.float32),
        ],
        limit=56 * 2**20,
    )(second_ref, cell_counts, geometry, *halo, live, dirichlet)

    def image_of(field, residual, *olds):
        return call(
            image_kernel,
            (cells, f32(2, SLOTS)),
            [SM, SM] + [VM] * (10 + len(olds)),
            [
                pltpu.VMEM((3, 4, 10, 8, SLOTS), jnp.float32),
                pltpu.VMEM((SLOTS, SLOTS), jnp.float32),
                part,
            ],
            limit=56 * 2**20,
        )(second_ref, cell_counts, weight, field, *around(field, second), diagonal, residual, basis, *olds)

    smoothed = call(first_smooth_kernel, cells, [VM] * 6, [part])(
        coefficient, coarse_inverse, basis, live, residual, inverse
    )
    image, payload = image_of(smoothed, residual)
    gathered_first = gather(payload)
    coefficient, residual, second_smoothed = call(
        second_smooth_kernel, (f32(128, SLOTS), cells, cells), [VM] * 9, [part]
    )(gathered_first, coefficient, coarse_inverse, basis, live, residual, inverse, smoothed, image)
    second_image, payload = image_of(second_smoothed, residual, smoothed, image)
    gathered = gather(payload)
    pressure, residual, third_smoothed, direction, payload = call(
        third_smooth_kernel,
        (cells, cells, cells, cells, f32(1, SLOTS)),
        [VM] * 12,
        [pltpu.VMEM((128, SLOTS), jnp.float32), part],
    )(
        gathered, gathered_first, coefficient, coarse_inverse, basis, live, residual, inverse,
        smoothed, image, second_smoothed, second_image,
    )
    totals = jnp.sum(gather(payload), axis=0)
    direction = third_smoothed + totals[0] / totals[1] * direction
    shape = (1, 2, 8, SLOTS)
    return pressure.reshape(shape), residual.reshape(shape), direction.reshape(shape)


def solution(mesh):
    field = P("gx", "gy", "gz", None)
    in_specs = (
        P(None, "gx", "gy", "gz", None),
        P("gx", "gy", "gz"),
        field,
        field,
        field,
        P(None, "gx", "gy", "gz", None),
        P(("gx", "gy", "gz"), None),
    )
    return jax.shard_map(per_device, mesh=mesh, in_specs=in_specs, out_specs=(field,) * 3, check_vma=False)
```

time: 1400 us -> 232 us (0.17)
  waiting for transfers between devices: 723 us -> 8.66 us
  blocking collectives: 375 us -> 66.6 us
  other arithmetic: 202 us -> 7.72 us
  Pallas kernels: 0 us -> 77.9 us
  matrix products: 20.6 us -> 0 us
  loops' own time: 15.2 us -> 0 us
    while x4 -> x0, waiting for transfers between devices: 473 us -> none
    psum x5 -> x0, blocking collectives: 375 us -> none  [the longest x3 224 us: global_inner(): return lax.psum(jnp.sum(left_field * right_field), ('gx', 'gy', 'gz'))]
    unnamed x2 -> x0, waiting for transfers between devices: 239 us -> none
    reduce_sum x86 -> x1, other arithmetic: 192 us -> 0.03 us  [per_device(): totals = jnp.sum(gather(payload), axis=0)]
    pallas_call x0 -> x7, Pallas kernels: none -> 77.9 us  [the longest x1 34 us: per_device(): call(weights_kernel, (f32(16, 16, 27, 8, SLOTS), cells, cells), [SM, SM]...]
    all_to_all x0 -> x3, blocking collectives: none -> 66.6 us  [gather(): got = lax.all_to_all(spread, ('gx', 'gy'), 0, 0, tiled=True)]
    dot_general x9 -> x0, matrix products: 20.6 us -> none  [the longest x3 16.7 us: precondition(): jnp.dot(coarse_inverse, lax.all_gather(coefficient, ('gx', 'gy', 'gz'), a...]
    another operation x4 -> x0, loops' own time: 15.2 us -> none  [the longest x3 10.9 us: neighbour_sum(): return lax.fori_loop(0, 27, visit, blank_sum)]
  transfers between devices with their start and end apart: 21 -> 20, of which waited for: 10 -> 9; matrix products, arithmetic and copies ran while one was open for 1% -> 1% of each run, Pallas kernels for 0% -> 15%
where the time goes in v1:
time: 232 us; the launch traced here: 231 us
  Pallas kernels  77.9 us (34%)
  blocking collectives  66.6 us (29%)
  starting transfers between devices  60.1 us (26%)
  waiting for transfers between devices  8.66 us (4%)
  other arithmetic  7.72 us (3%)
  local copies, waits for them, and re-layouts  7.65 us (3%)
    all_to_all x3, blocking collectives, gather(): got = lax.all_to_all(spread, ('gx', 'gy'), 0, 0, tiled=True)  66.6 us
    pallas_call x1, Pallas kernels, per_device(): call(weights_kernel, (f32(16, 16, 27, 8, SLOTS), cells, cells), [SM, SM]...  34 us
    pallas_call x2, Pallas kernels, image_of(): call(image_kernel, (cells, f32(2, SLOTS)), [SM, SM] + [VM] * (10 + len(ol...  31 us
    all_to_all x1, starting transfers between devices, gather(): got = lax.all_to_all(spread, ('gx', 'gy'), 0, 0, tiled=True)  15 us
    ppermute x3, starting transfers between devices, around(): before = lax.ppermute(field, 'gx', up)  13 us
    ppermute x3, starting transfers between devices, around(): below = lax.ppermute(three[..., :, 1, :, :], 'gy', up)  12 us
    ppermute x3, starting transfers between devices, around(): across = lax.ppermute(face, 'gz', [(0, 1), (1, 0)])  7.64 us
    ppermute x4, starting transfers between devices, gather(): both = payload + lax.ppermute(payload, 'gz', [(0, 1), (1, 0)])  4.85 us
  transfers between devices with their start and end apart: 20, of which 9 were waited for; matrix products, arithmetic and copies ran while one was open for 1% of the time, Pallas kernels for 15%

profile of v1, /device:TPU:1, one launch (start us, length us, event | category | flops | bytes accessed | tf_op | source)
XLA Modules:
  0.0 230.8 jit_solution(7431305935891764473)
XLA Ops:
  0.6 1.3 reshape.71.counts_ref
  1.9 0.7 copy.60
  2.7 1.9 shard_map.94
  4.5 0.7 fusion.1
  5.2 1.3 collective-permute-start.1
  6.5 5.0 %collective-permute-start = (f32[4,2,8,128]{3,2,0,1:T(8,128)S(1)}, f32[4,2,8,128]{3,2,0,1:T(8,128)S(1)}, u32[]{:S(2)}, u32[]{:S(2)}) collective-permute-start(f32[4,2,8,128]{3,2,0,1:T(8,128)S(1)} %get-tuple-element.42), channel_id=1, source_target_pairs={{0,8},{8,16},{16,24},{24,32},{32,40},{40,48},{48,56},{56,64},{64,7... | collective-permute-start | bytes 98312 | tf_op jit(solution)/shard_map/ppermute | solution.py:250
  11.5 2.8 %collective-permute-start.5 = (f32[1,128]{1,0:T(1,128)}, f32[1,128]{1,0:T(1,128)S(1)}, u32[]{:S(2)}, u32[]{:S(2)}) collective-permute-start(f32[1,128]{1,0:T(1,128)} %get-tuple-element.23), channel_id=1, source_target_pairs={{0,1},{1,0},{2,3},{3,2},{4,5},{5,4},{6,7},{7,6},{8,9},{9,8},{10,11... | collective-permute-start | bytes 1544 | tf_op jit(solution)/shard_map/ppermute | solution.py:264
  14.4 1.3 collective-permute-start.3
  15.7 4.0 %collective-permute-start.2 = (f32[4,3,8,128]{3,2,1,0:T(8,128)S(1)}, f32[4,3,8,128]{3,2,1,0:T(8,128)S(1)}, u32[]{:S(2)}, u32[]{:S(2)}) collective-permute-start(f32[4,3,8,128]{3,2,1,0:T(8,128)S(1)} %get-tuple-element.40), channel_id=1, source_target_pairs={{0,2},{2,4},{4,6},{1,3},{3,5},{5,7},{8,10},{10,12},{12,14},{9,11},... | collective-permute-start | bytes 147464 | tf_op jit(solution)/shard_map/ppermute | solution.py:254
  19.7 0.0 collective-permute-done.5
  19.7 0.7 add_bitcast_fusion.2
  20.4 0.7 broadcast_in_dim.53
  21.0 15.0 %all-to-all-start = ((f32[128,1,128]{2,1,0:T(1,128)}), f32[128,1,128]{2,1,0:T(1,128)S(1)}, u32[]{:S(2)}, u32[]{:S(2)}) async-start(f32[128,1,128]{2,1,0:T(1,128)} %broadcast_in_dim.53), calls=%async_computation | async-start | bytes 131072 | tf_op jit(solution)/shard_map/all_to_all | solution.py:267
  36.0 0.0 collective-permute-done.3.above_ref
  36.1 2.9 %collective-permute-start.4 = (f32[4,12,128]{2,1,0:T(8,128)S(1)}, f32[4,12,128]{2,1,0:T(8,128)S(1)}, u32[]{:S(2)}, u32[]{:S(2)}) collective-permute-start(f32[4,12,128]{2,1,0:T(8,128)S(1)} %copy.52), channel_id=1, source_target_pairs={{0,1},{1,0},{2,3},{3,2},{4,5},{5,4},{6,7},{7,6},{8,9},{9,8},{10,11... | collective-permute-start | bytes 73736 | tf_op jit(solution)/shard_map/ppermute | solution.py:259
  39.0 0.6 copy.53.own_ref
  39.6 0.6 copy.55.after_ref
  40.2 0.6 copy.54.before_ref
  40.8 0.0 collective-permute-done.4.across_ref
  40.8 0.6 copy-done.11
  41.4 34.0 %shard_map.95 = (f32[16,16,27,8,128]{4,3,2,1,0:T(8,128)}, f32[2,8,128]{2,1,0:T(8,128)}, f32[2,8,128]{2,1,0:T(8,128)}) custom-call(s32[1]{0:T(128)} %bitcast.second_ref, s32[16]{0:T(128)} %reshape.71.counts_ref, f32[4,2,8,128]{3,2,1,0:T(8,128)} %copy.53.own_ref, f32[4,2,8,128]{3,2,1,0:T(8,128)} %copy.54.before_ref, f32[4,2,8,128]{3,2,1,0:T(8,128)} %copy.55.after_ref, ...), custom_call_target="tpu_custom_call" | custom-call | tf_op jit(solution)/shard_map/pallas_call | solution.py:290
  75.5 0.0 all-to-all-done
  75.5 0.6 copy-done
  76.1 3.5 %shard_map.96.own_ref.smoothed_ref.rest_0_.first_ref = f32[2,8,128]{2,1,0:T(8,128)} custom-call(f32[128,128]{1,0:T(8,128)} %bitcast.73, f32[64,16384]{1,0:T(8,128)} %coarse_ref.5, f32[64,2,8,128]{3,2,1,0:T(8,128)} %bitcast.66, f32[2,8,128]{2,1,0:T(8,128)} %get-tuple-element.21.live_ref, f32[2,8,128]{2,1,0:T(8,128)} %get-tuple-element.24.residual_ref, ...), custom_call_target="tpu_custom_call" | custom-call | tf_op jit(solution)/shard_map/pallas_call | solution.py:315
  79.5 1.3 collective-permute-start.7
  80.8 4.0 %collective-permute-start.6 = (f32[2,8,128]{2,1,0:T(8,128)}, f32[2,8,128]{2,1,0:T(8,128)S(1)}, u32[]{:S(2)}, u32[]{:S(2)}) collective-permute-start(f32[2,8,128]{2,1,0:T(8,128)} %shard_map.96.own_ref.smoothed_ref.rest_0_.first_ref), channel_id=1, source_target_pairs={{0,8},{8,16},{16,24},{24,32},{32,40},{40,48},{48,56},{56,64},{64,7... | collective-permute-start | bytes 24584 | tf_op jit(solution)/shard_map/ppermute | solution.py:250
  84.8 0.0 collective-permute-done.7.after_ref
  84.8 1.0 collective-permute-done.6.before_ref
  85.8 0.7 pad_maximum_fusion.6
  86.5 1.3 collective-permute-start.9
  87.8 4.0 %collective-permute-start.8 = (f32[3,8,128]{2,1,0:T(8,128)S(1)}, f32[3,8,128]{2,1,0:T(8,128)S(1)}, u32[]{:S(2)}, u32[]{:S(2)}) collective-permute-start(f32[3,8,128]{2,1,0:T(8,128)S(1)} %get-tuple-element.46), channel_id=1, source_target_pairs={{0,2},{2,4},{4,6},{1,3},{3,5},{5,7},{8,10},{10,12},{12,14},{9,11},... | collective-permute-start | bytes 36872 | tf_op jit(solution)/shard_map/ppermute | solution.py:254
  91.8 0.8 collective-permute-done.8.below_ref
  92.6 0.8 broadcast_select_fusion.2
  93.4 0.6 collective-permute-start.10
  94.0 0.8 collective-permute-done.10.across_ref
  94.8 0.6 copy-done.13
  95.4 15.4 %shard_map.97 = (f32[2,8,128]{2,1,0:T(8,128)}, f32[2,128]{1,0:T(2,128)}) custom-call(s32[1]{0:T(128)} %bitcast.second_ref, s32[16]{0:T(128)} %reshape.71.counts_ref, f32[16,16,27,8,128]{4,3,2,1,0:T(8,128)} %get-tuple-element.22.weight_ref, f32[2,8,128]{2,1,0:T(8,128)} %shard_map.96.own_ref.smoothed_ref.rest_0_.first_ref, f32[2,8,128]{2,1,0:T(8,128)} %copy-done.6, ...), custom_call_target="tpu_custom_call" | custom-call | tf_op jit(solution)/shard_map/pallas_call | solution.py:303
  110.8 0.0 collective-permute-start.11
  110.8 1.2 collective-permute-done.11
  112.1 0.7 add.16
  112.8 28.2 %all_to_all.20 = f32[128,2,128]{2,1,0:T(2,128)} all-to-all(f32[128,2,128]{2,1,0:T(2,128)S(1)} %broadcast_in_dim.56), channel_id=1, replica_groups=mesh['gx'=32,'gy'=4,'gz'=2] {'gx','gy'}, dimensions={0} | all-to-all | bytes 262144 | tf_op jit(solution)/shard_map/all_to_all | solution.py:267
  141.0 3.7 %shard_map.98 = (f32[128,128]{1,0:T(8,128)}, f32[2,8,128]{2,1,0:T(8,128)}, f32[2,8,128]{2,1,0:T(8,128)}) custom-call(f32[256,128]{1,0:T(8,128)} %bitcast.71, f32[128,128]{1,0:T(8,128)} %bitcast.74, f32[64,16384]{1,0:T(8,128)} %coarse_ref.5, f32[64,2,8,128]{3,2,1,0:T(8,128)} %bitcast.68, f32[2,8,128]{2,1,0:T(8,128)} %get-tuple-element.21.live_ref, ...), custom_call_target="tpu_custom_call" | custom-call | tf_op jit(solution)/shard_map/pallas_call | solution.py:320
  144.7 1.3 collective-permute-start.13
  146.0 4.0 %collective-permute-start.12 = (f32[2,8,128]{2,1,0:T(8,128)}, f32[2,8,128]{2,1,0:T(8,128)S(1)}, u32[]{:S(2)}, u32[]{:S(2)}) collective-permute-start(f32[2,8,128]{2,1,0:T(8,128)} %get-tuple-element.29.own_ref.smoothed_ref), channel_id=1, source_target_pairs={{0,8},{8,16},{16,24},{24,32},{32,40},{40,48},{48,56},{56,64},{64,7... | collective-permute-start | bytes 24584 | tf_op jit(solution)/shard_map/ppermute | solution.py:250
  150.0 1.0 collective-permute-done.12.before_ref
  151.0 0.7 pad_maximum_fusion.7
  151.7 1.3 collective-permute-start.15
  153.0 4.0 %collective-permute-start.14 = (f32[3,8,128]{2,1,0:T(8,128)S(1)}, f32[3,8,128]{2,1,0:T(8,128)S(1)}, u32[]{:S(2)}, u32[]{:S(2)}) collective-permute-start(f32[3,8,128]{2,1,0:T(8,128)S(1)} %get-tuple-element.44), channel_id=1, source_target_pairs={{0,2},{2,4},{4,6},{1,3},{3,5},{5,7},{8,10},{10,12},{12,14},{9,11},... | collective-permute-start | bytes 36872 | tf_op jit(solution)/shard_map/ppermute | solution.py:254
  157.0 0.8 collective-permute-done.14.below_ref
  157.8 0.8 broadcast_select_fusion.1
  158.6 4.2 %collective-permute-start.16 = (f32[12,128]{1,0:T(8,128)S(1)}, f32[12,128]{1,0:T(8,128)S(1)}, u32[]{:S(2)}, u32[]{:S(2)}) collective-permute-start(f32[12,128]{1,0:T(8,128)S(1)} %select_n.39), channel_id=1, source_target_pairs={{0,1},{1,0},{2,3},{3,2},{4,5},{5,4},{6,7},{7,6},{8,9},{9,8},{10,11... | collective-permute-start | bytes 18440 | tf_op jit(solution)/shard_map/ppermute | solution.py:259
  162.8 0.8 collective-permute-done.16.across_ref
  163.6 0.6 copy-done.12
  164.2 15.5 %shard_map.99 = (f32[2,8,128]{2,1,0:T(8,128)}, f32[2,128]{1,0:T(2,128)}) custom-call(s32[1]{0:T(128)} %bitcast.second_ref, s32[16]{0:T(128)} %reshape.71.counts_ref, f32[16,16,27,8,128]{4,3,2,1,0:T(8,128)} %get-tuple-element.22.weight_ref, f32[2,8,128]{2,1,0:T(8,128)} %get-tuple-element.29.own_ref.smoothed_ref, f32[2,8,128]{2,1,0:T(8,128)} %copy-done.4, ...), custom_call_target="tpu_custom_call" | custom-call | tf_op jit(solution)/shard_map/pallas_call | solution.py:303
  179.7 1.2 collective-permute-done.17
  181.0 0.7 add.17
  181.7 22.3 %all_to_all.21 = f32[128,2,128]{2,1,0:T(2,128)} all-to-all(f32[128,2,128]{2,1,0:T(2,128)S(1)} %broadcast_in_dim.59), channel_id=1, replica_groups=mesh['gx'=32,'gy'=4,'gz'=2] {'gx','gy'}, dimensions={0} | all-to-all | bytes 262144 | tf_op jit(solution)/shard_map/all_to_all | solution.py:267
  204.0 3.8 %shard_map.100 = (f32[2,8,128]{2,1,0:T(8,128)}, f32[2,8,128]{2,1,0:T(8,128)}, f32[2,8,128]{2,1,0:T(8,128)}, f32[2,8,128]{2,1,0:T(8,128)}, f32[1,128]{1,0:T(1,128)}) custom-call(f32[256,128]{1,0:T(8,128)} %bitcast.75, f32[256,128]{1,0:T(8,128)} %bitcast.72, f32[128,128]{1,0:T(8,128)} %get-tuple-element.32.coefficient_ref, f32[64,16384]{1,0:T(8,128)} %coarse_ref.5, ...), custom_call_target="tpu_custom_call" | custom-call | tf_op jit(solution)/shard_map/pallas_call | solution.py:325
  207.8 2.0 collective-permute-start.18
  209.8 1.0 collective-permute-done.18
  210.8 0.6 add_bitcast_fusion.1
  211.5 16.1 %all_to_all.22 = f32[128,1,128]{2,1,0:T(1,128)S(1)} all-to-all(f32[128,1,128]{2,1,0:T(1,128)S(1)} %broadcast_in_dim.61), channel_id=1, replica_groups=mesh['gx'=32,'gy'=4,'gz'=2] {'gx','gy'}, dimensions={0} | all-to-all | bytes 131072 | tf_op jit(solution)/shard_map/all_to_all | solution.py:267
  227.7 0.6 fusion.3
  229.5 1.3 add_bitcast_fusion
  (47 shorter events, 0.3 us)
Async XLA Ops:
  5.2 9.1 %collective-permute-start.1 = (f32[4,2,8,128]{3,2,0,1:T(8,128)S(1)}, f32[4,2,8,128]{3,2,0,1:T(8,128)S(1)}, u32[]{:S(2)}, u32[]{:S(2)}) collective-permute-start(f32[4,2,8,128]{3,2,0,1:T(8,128)S(1)} %get-tuple-element.42), channel_id=1, source_target_pairs={{8,0},{16,8},{24,16},{32,24},{40,32},{48,40},{56,48},{64,56},{72,6... | collective-permute-start | bytes 98312 | tf_op jit(solution)/shard_map/ppermute | solution.py:251
  6.5 7.8 %collective-permute-start = (f32[4,2,8,128]{3,2,0,1:T(8,128)S(1)}, f32[4,2,8,128]{3,2,0,1:T(8,128)S(1)}, u32[]{:S(2)}, u32[]{:S(2)}) collective-permute-start(f32[4,2,8,128]{3,2,0,1:T(8,128)S(1)} %get-tuple-element.42), channel_id=1, source_target_pairs={{0,8},{8,16},{16,24},{24,32},{32,40},{40,48},{48,56},{56,64},{64,7... | collective-permute-start | bytes 98312 | tf_op jit(solution)/shard_map/ppermute | solution.py:250
  11.5 8.2 %collective-permute-start.5 = (f32[1,128]{1,0:T(1,128)}, f32[1,128]{1,0:T(1,128)S(1)}, u32[]{:S(2)}, u32[]{:S(2)}) collective-permute-start(f32[1,128]{1,0:T(1,128)} %get-tuple-element.23), channel_id=1, source_target_pairs={{0,1},{1,0},{2,3},{3,2},{4,5},{5,4},{6,7},{7,6},{8,9},{9,8},{10,11... | collective-permute-start | bytes 1544 | tf_op jit(solution)/shard_map/ppermute | solution.py:264
  14.4 21.6 %collective-permute-start.3 = (f32[4,3,8,128]{3,2,1,0:T(8,128)S(1)}, f32[4,3,8,128]{3,2,1,0:T(8,128)S(1)}, u32[]{:S(2)}, u32[]{:S(2)}) collective-permute-start(f32[4,3,8,128]{3,2,1,0:T(8,128)S(1)} %get-tuple-element.39), channel_id=1, source_target_pairs={{2,0},{4,2},{6,4},{3,1},{5,3},{7,5},{10,8},{12,10},{14,12},{11,9},... | collective-permute-start | bytes 147464 | tf_op jit(solution)/shard_map/ppermute | solution.py:255
  15.7 20.3 %collective-permute-start.2 = (f32[4,3,8,128]{3,2,1,0:T(8,128)S(1)}, f32[4,3,8,128]{3,2,1,0:T(8,128)S(1)}, u32[]{:S(2)}, u32[]{:S(2)}) collective-permute-start(f32[4,3,8,128]{3,2,1,0:T(8,128)S(1)} %get-tuple-element.40), channel_id=1, source_target_pairs={{0,2},{2,4},{4,6},{1,3},{3,5},{5,7},{8,10},{10,12},{12,14},{9,11},... | collective-permute-start | bytes 147464 | tf_op jit(solution)/shard_map/ppermute | solution.py:254
  21.0 54.4 %all-to-all-start = ((f32[128,1,128]{2,1,0:T(1,128)}), f32[128,1,128]{2,1,0:T(1,128)S(1)}, u32[]{:S(2)}, u32[]{:S(2)}) async-start(f32[128,1,128]{2,1,0:T(1,128)} %broadcast_in_dim.53), calls=%async_computation | async-start | bytes 131072 | tf_op jit(solution)/shard_map/all_to_all | solution.py:267
  36.0 4.8 %copy-start.1 = (f32[4,3,8,128]{3,2,1,0:T(8,128)}, f32[4,3,8,128]{3,2,1,0:T(8,128)S(1)}, u32[]{:S(2)}) copy-start(f32[4,3,8,128]{3,2,1,0:T(8,128)S(1)} %collective-permute-done.3.above_ref) | copy-start | bytes 147460
  36.0 4.8 %copy-start.2 = (f32[4,3,8,128]{3,2,1,0:T(8,128)}, f32[4,3,8,128]{3,2,1,0:T(8,128)S(1)}, u32[]{:S(2)}) copy-start(f32[4,3,8,128]{3,2,1,0:T(8,128)S(1)} %collective-permute-done.2.below_ref) | copy-start | bytes 147460
  36.1 4.7 %collective-permute-start.4 = (f32[4,12,128]{2,1,0:T(8,128)S(1)}, f32[4,12,128]{2,1,0:T(8,128)S(1)}, u32[]{:S(2)}, u32[]{:S(2)}) collective-permute-start(f32[4,12,128]{2,1,0:T(8,128)S(1)} %copy.52), channel_id=1, source_target_pairs={{0,1},{1,0},{2,3},{3,2},{4,5},{5,4},{6,7},{7,6},{8,9},{9,8},{10,11... | collective-permute-start | bytes 73736 | tf_op jit(solution)/shard_map/ppermute | solution.py:259
  40.8 0.6 copy-start.11
  75.5 0.6 copy-start
  79.5 5.3 %collective-permute-start.7 = (f32[2,8,128]{2,1,0:T(8,128)}, f32[2,8,128]{2,1,0:T(8,128)S(1)}, u32[]{:S(2)}, u32[]{:S(2)}) collective-permute-start(f32[2,8,128]{2,1,0:T(8,128)} %shard_map.96.own_ref.smoothed_ref.rest_0_.first_ref), channel_id=1, source_target_pairs={{8,0},{16,8},{24,16},{32,24},{40,32},{48,40},{56,48},{64,56},{72,6... | collective-permute-start | bytes 24584 | tf_op jit(solution)/shard_map/ppermute | solution.py:251
  80.8 5.0 %collective-permute-start.6 = (f32[2,8,128]{2,1,0:T(8,128)}, f32[2,8,128]{2,1,0:T(8,128)S(1)}, u32[]{:S(2)}, u32[]{:S(2)}) collective-permute-start(f32[2,8,128]{2,1,0:T(8,128)} %shard_map.96.own_ref.smoothed_ref.rest_0_.first_ref), channel_id=1, source_target_pairs={{0,8},{8,16},{16,24},{24,32},{32,40},{40,48},{48,56},{56,64},{64,7... | collective-permute-start | bytes 24584 | tf_op jit(solution)/shard_map/ppermute | solution.py:250
  84.8 10.0 %copy-start.5 = (f32[2,8,128]{2,1,0:T(8,128)}, f32[2,8,128]{2,1,0:T(8,128)S(1)}, u32[]{:S(2)}) copy-start(f32[2,8,128]{2,1,0:T(8,128)S(1)} %collective-permute-done.7.after_ref) | copy-start | bytes 24580
  85.8 9.0 %copy-start.6 = (f32[2,8,128]{2,1,0:T(8,128)}, f32[2,8,128]{2,1,0:T(8,128)S(1)}, u32[]{:S(2)}) copy-start(f32[2,8,128]{2,1,0:T(8,128)S(1)} %collective-permute-done.6.before_ref) | copy-start | bytes 24580
  86.5 5.3 %collective-permute-start.9 = (f32[3,8,128]{2,1,0:T(8,128)S(1)}, f32[3,8,128]{2,1,0:T(8,128)S(1)}, u32[]{:S(2)}, u32[]{:S(2)}) collective-permute-start(f32[3,8,128]{2,1,0:T(8,128)S(1)} %get-tuple-element.45), channel_id=1, source_target_pairs={{2,0},{4,2},{6,4},{3,1},{5,3},{7,5},{10,8},{12,10},{14,12},{11,9},... | collective-permute-start | bytes 36872 | tf_op jit(solution)/shard_map/ppermute | solution.py:255
  87.8 4.8 %collective-permute-start.8 = (f32[3,8,128]{2,1,0:T(8,128)S(1)}, f32[3,8,128]{2,1,0:T(8,128)S(1)}, u32[]{:S(2)}, u32[]{:S(2)}) collective-permute-start(f32[3,8,128]{2,1,0:T(8,128)S(1)} %get-tuple-element.46), channel_id=1, source_target_pairs={{0,2},{2,4},{4,6},{1,3},{3,5},{5,7},{8,10},{10,12},{12,14},{9,11},... | collective-permute-start | bytes 36872 | tf_op jit(solution)/shard_map/ppermute | solution.py:254
  91.8 3.0 %copy-start.7 = (f32[3,8,128]{2,1,0:T(8,128)}, f32[3,8,128]{2,1,0:T(8,128)S(1)}, u32[]{:S(2)}) copy-start(f32[3,8,128]{2,1,0:T(8,128)S(1)} %collective-permute-done.9.above_ref) | copy-start | bytes 36868
  92.6 2.2 copy-start.8
  93.4 1.4 collective-permute-start.10
  94.8 0.6 copy-start.13
  110.8 1.2 collective-permute-start.11
  144.7 5.3 %collective-permute-start.13 = (f32[2,8,128]{2,1,0:T(8,128)}, f32[2,8,128]{2,1,0:T(8,128)S(1)}, u32[]{:S(2)}, u32[]{:S(2)}) collective-permute-start(f32[2,8,128]{2,1,0:T(8,128)} %get-tuple-element.29.own_ref.smoothed_ref), channel_id=1, source_target_pairs={{8,0},{16,8},{24,16},{32,24},{40,32},{48,40},{56,48},{64,56},{72,6... | collective-permute-start | bytes 24584 | tf_op jit(solution)/shard_map/ppermute | solution.py:251
  146.0 5.0 %collective-permute-start.12 = (f32[2,8,128]{2,1,0:T(8,128)}, f32[2,8,128]{2,1,0:T(8,128)S(1)}, u32[]{:S(2)}, u32[]{:S(2)}) collective-permute-start(f32[2,8,128]{2,1,0:T(8,128)} %get-tuple-element.29.own_ref.smoothed_ref), channel_id=1, source_target_pairs={{0,8},{8,16},{16,24},{24,32},{32,40},{40,48},{48,56},{56,64},{64,7... | collective-permute-start | bytes 24584 | tf_op jit(solution)/shard_map/ppermute | solution.py:250
  150.0 13.6 %copy-start.3 = (f32[2,8,128]{2,1,0:T(8,128)}, f32[2,8,128]{2,1,0:T(8,128)S(1)}, u32[]{:S(2)}) copy-start(f32[2,8,128]{2,1,0:T(8,128)S(1)} %collective-permute-done.13.after_ref) | copy-start | bytes 24580
  151.0 12.6 %copy-start.4 = (f32[2,8,128]{2,1,0:T(8,128)}, f32[2,8,128]{2,1,0:T(8,128)S(1)}, u32[]{:S(2)}) copy-start(f32[2,8,128]{2,1,0:T(8,128)S(1)} %collective-permute-done.12.before_ref) | copy-start | bytes 24580
  151.7 5.3 %collective-permute-start.15 = (f32[3,8,128]{2,1,0:T(8,128)S(1)}, f32[3,8,128]{2,1,0:T(8,128)S(1)}, u32[]{:S(2)}, u32[]{:S(2)}) collective-permute-start(f32[3,8,128]{2,1,0:T(8,128)S(1)} %get-tuple-element.43), channel_id=1, source_target_pairs={{2,0},{4,2},{6,4},{3,1},{5,3},{7,5},{10,8},{12,10},{14,12},{11,9},... | collective-permute-start | bytes 36872 | tf_op jit(solution)/shard_map/ppermute | solution.py:255
  153.0 4.8 %collective-permute-start.14 = (f32[3,8,128]{2,1,0:T(8,128)S(1)}, f32[3,8,128]{2,1,0:T(8,128)S(1)}, u32[]{:S(2)}, u32[]{:S(2)}) collective-permute-start(f32[3,8,128]{2,1,0:T(8,128)S(1)} %get-tuple-element.44), channel_id=1, source_target_pairs={{0,2},{2,4},{4,6},{1,3},{3,5},{5,7},{8,10},{10,12},{12,14},{9,11},... | collective-permute-start | bytes 36872 | tf_op jit(solution)/shard_map/ppermute | solution.py:254
  157.0 6.6 %copy-start.9 = (f32[3,8,128]{2,1,0:T(8,128)}, f32[3,8,128]{2,1,0:T(8,128)S(1)}, u32[]{:S(2)}) copy-start(f32[3,8,128]{2,1,0:T(8,128)S(1)} %collective-permute-done.15.above_ref) | copy-start | bytes 36868
  157.8 5.8 %copy-start.10 = (f32[3,8,128]{2,1,0:T(8,128)}, f32[3,8,128]{2,1,0:T(8,128)S(1)}, u32[]{:S(2)}) copy-start(f32[3,8,128]{2,1,0:T(8,128)S(1)} %collective-permute-done.14.below_ref) | copy-start | bytes 36868
  158.6 5.0 %collective-permute-start.16 = (f32[12,128]{1,0:T(8,128)S(1)}, f32[12,128]{1,0:T(8,128)S(1)}, u32[]{:S(2)}, u32[]{:S(2)}) collective-permute-start(f32[12,128]{1,0:T(8,128)S(1)} %select_n.39), channel_id=1, source_target_pairs={{0,1},{1,0},{2,3},{3,2},{4,5},{5,4},{6,7},{7,6},{8,9},{9,8},{10,11... | collective-permute-start | bytes 18440 | tf_op jit(solution)/shard_map/ppermute | solution.py:259
  163.6 0.6 copy-start.12
  179.7 1.2 collective-permute-start.17
  207.8 3.0 %collective-permute-start.18 = (f32[1,128]{1,0:T(1,128)}, f32[1,128]{1,0:T(1,128)S(1)}, u32[]{:S(2)}, u32[]{:S(2)}) collective-permute-start(f32[1,128]{1,0:T(1,128)} %get-tuple-element.37), channel_id=1, source_target_pairs={{0,1},{1,0},{2,3},{3,2},{4,5},{5,4},{6,7},{7,6},{8,9},{9,8},{10,11... | collective-permute-start | bytes 1544 | tf_op jit(solution)/shard_map/ppermute | solution.py:264

commit v2 on v1

--- a/solution.py
+++ b/solution.py
@@ -7,16 +7,18 @@
 
 SLOTS = 128
 FAR = 1000.0
+LIMIT = 4 * 2**20
 
 VM = pl.BlockSpec(memory_space=pltpu.VMEM)
 SM = pl.BlockSpec(memory_space=pltpu.SMEM)
+ANY = pl.BlockSpec(memory_space=pl.ANY)
 
 
 def f32(*shape):
     return jax.ShapeDtypeStruct(shape, jnp.float32)
 
 
-def call(kernel, outs, ins, scratch=(), limit=None):
+def call(kernel, outs, ins, scratch=(), limit=LIMIT):
     return pl.pallas_call(
         kernel,
         out_shape=outs,
@@ -46,13 +48,70 @@
     return row
 
 
-def prepare_kernel(second_ref, counts_ref, right_ref, basis_ref, live_ref, residual_ref, payload_ref, part_ref):
+def fetch(pairs, sems):
+    copies = [pltpu.make_async_copy(src, dst, sems.at[at]) for at, (src, dst) in enumerate(pairs)]
+    for copy in copies:
+        copy.start()
+    return copies
+
+
+def prepare_kernel(
+    second_ref, counts_hbm, offsets_hbm, correction_hbm, right_hbm, dirichlet_hbm, basis_hbm,
+    geometry_ref, live_ref, residual_ref, payload_ref, counts_ref, dirichlet_ref, basis_ref,
+    counts_smem, offsets_ref, correction_ref, right_ref, part_ref, sems,
+):
+    copies = fetch(
+        (
+            (counts_hbm, counts_smem), (counts_hbm, counts_ref), (offsets_hbm, offsets_ref),
+            (correction_hbm, correction_ref), (right_hbm, right_ref), (dirichlet_hbm, dirichlet_ref),
+            (basis_hbm, basis_ref),
+        ),
+        sems,
+    )
+    for copy in copies[:-1]:
+        copy.wait()
     slot = lax.broadcasted_iota(jnp.int32, (1, SLOTS), 1)
     for y in range(2):
         for z in range(8):
-            live_ref[y, z : z + 1, :] = jnp.where(slot < counts_ref[y * 8 + z], 1.0, 0.0)
-    residual_ref[...] = right_ref[...] * live_ref[...]
+            live_ref[y, z : z + 1, :] = jnp.where(slot < counts_smem[0, y, z], 1.0, 0.0)
+    live = live_ref[...]
+    geometry_ref[0:3] = offsets_ref[...]
+    geometry_ref[3] = correction_ref[...] * live * (10.0 / SLOTS)
+    residual_ref[...] = right_ref[...] * live
+    copies[-1].wait()
     payload_ref[...] = project(basis_ref, residual_ref[...], part_ref, second_ref[0])
+
+
+def side_faces_kernel(before_ref, field_ref, after_ref, up_ref, down_ref):
+    for f in range(field_ref.shape[0]):
+        for x, ref in enumerate((before_ref, field_ref, after_ref)):
+            up_ref[f, x] = ref[f, 1]
+            down_ref[f, x] = ref[f, 0]
+
+
+def top_face_kernel(second_ref, before_ref, field_ref, after_ref, below_ref, above_ref, face_ref):
+    second = second_ref[0]
+
+    def pick(rows):
+        return jnp.where(second == 0, rows[7:8], rows[0:1])
+
+    for f in range(field_ref.shape[0]):
+        for x, ref in enumerate((before_ref, field_ref, after_ref)):
+            for y, rows in enumerate((below_ref[f, x], ref[f, 0], ref[f, 1], above_ref[f, x])):
+                face_ref[f, x * 4 + y : x * 4 + y + 1, :] = pick(rows)
+
+
+def spread_kernel(mine_ref, theirs_ref, spread_ref):
+    rows = mine_ref[...] + theirs_ref[...]
+    spread_ref[...] = jnp.broadcast_to(rows[None], spread_ref.shape)
+
+
+def finish_kernel(gathered_ref, smoothed_ref, direction_ref, out_ref):
+    rows = gathered_ref[...]
+    lane = lax.broadcasted_iota(jnp.int32, rows.shape, 1)
+    inner = jnp.sum(jnp.where(lane == 0, rows, 0.0))
+    before = jnp.sum(jnp.where(lane == 1, rows, 0.0))
+    out_ref[...] = smoothed_ref[...] + inner / before * direction_ref[...]
 
 
 def assemble(own, before, after, below, above, across, second, put):
@@ -71,10 +130,18 @@
             put(x, y, 9, jnp.where(second == 0, row, 0.0))
 
 
+def row_sums(sums_ref, out_ref):
+    for cell in range(16):
+        out_ref[cell // 8, cell % 8 : cell % 8 + 1, :] = jnp.sum(sums_ref[cell].T, axis=0, keepdims=True)
+
+
 def weights_kernel(
     second_ref, counts_ref, own_ref, before_ref, after_ref, below_ref, above_ref, across_ref,
-    live_ref, dirichlet_ref, weight_ref, diagonal_ref, inverse_ref, near_ref, mine_ref, sums_ref,
+    live_ref, dirichlet_ref, coarse_hbm,
+    weight_a, weight_b, weight_c, diagonal_ref, inverse_ref, coarse_ref, near_ref, mine_ref, sums_ref, sems,
 ):
+    copies = fetch(((coarse_hbm, coarse_ref),), sems)
+    weight_refs = (weight_a, weight_b, weight_c)
     second = second_ref[0]
     tile = (8, SLOTS)
     for f in range(4):
@@ -92,44 +159,65 @@
     dead = near_ref[3] == 0.0
     near_ref[0] = jnp.where(dead, FAR, near_ref[0])
 
-    def one_cell(cell, _):
-        y, z = cell // 8, cell % 8
-        groups = (counts_ref[cell] + 7) // 8
-        for f in range(4):
-            row = near_ref[f, 1, y + 1, z + 1]
-            if f == 0:
-                row = jnp.where(near_ref[3, 1, y + 1, z + 1] == 0.0, -FAR, row)
-            mine_ref[f] = jnp.broadcast_to(row.T[:, 0:1], (SLOTS, SLOTS))
-        sums_ref[...] = jnp.zeros((SLOTS, SLOTS), jnp.float32)
-
-        def one_group(group, _):
-            here = pl.ds(pl.multiple_of(group * 8, 8), 8)
-            mx, my, mz, mc = (mine_ref[f, here, :] for f in range(4))
-            total = jnp.zeros(tile, jnp.float32)
+    cell_row = lax.broadcasted_iota(jnp.int32, (16, SLOTS), 0)
+    scale = own_ref[3].reshape(16, SLOTS)
+    fields = (
+        jnp.where(scale == 0.0, -FAR, own_ref[0].reshape(16, SLOTS) + 1.0),
+        own_ref[1].reshape(16, SLOTS) + jnp.where(cell_row >= 8, 2.0, 1.0),
+        own_ref[2].reshape(16, SLOTS) + (jnp.where(cell_row >= 8, cell_row - 8, cell_row) + 1).astype(jnp.float32),
+        scale,
+    )
+    for f, field in enumerate(fields):
+        columns = field.T
+        for cell in range(16):
+            mine_ref[cell, f] = jnp.broadcast_to(columns[:, cell : cell + 1], (SLOTS, SLOTS))
+
+    def one_cell(y, z):
+        cell = y * 8 + z
+        groups = (counts_ref[0, y, z] + 7) >> 3
+
+        def some_groups(first, count):
+            spots = [pl.ds(pl.multiple_of((first + g) * 8, 8), 8) for g in range(count)]
+            mine = [[mine_ref[cell, f, spot, :] for f in range(4)] for spot in spots]
+            totals = [jnp.zeros(tile, jnp.float32) for _ in spots]
             for at in range(27):
                 a, b, c = at // 9, at // 3 % 3, at % 3
-                dx = near_ref[0, a, y + b, z + c] - mx
-                dy = near_ref[1, a, y + b, z + c] - my
-                dz = near_ref[2, a, y + b, z + c] - mz
-                square = dx * dx + dy * dy + dz * dz
-                radius = square * lax.rsqrt(jnp.maximum(square, 1e-30))
-                fall = jnp.maximum(1.0 - radius, 0.0)
-                weight = (square * fall) * (fall * fall) / (square + 0.01)
-                weight = weight * (near_ref[3, a, y + b, z + c] + mc)
-                weight_ref[cell, group, at] = weight
-                total = total + weight
-            sums_ref[here, :] = total
+                near = [near_ref[f, a, y + b, z + c] for f in range(4)]
+                for g in range(count):
+                    dx, dy, dz = (near[f] - mine[g][f] for f in range(3))
+                    square = dx * dx + dy * dy + dz * dz
+                    radius = square * lax.rsqrt(jnp.maximum(square, 1e-30))
+                    fall = jnp.maximum(1.0 - radius, 0.0)
+                    weight = (square * fall) * (fall * fall) / (square + 0.01)
+                    weight = weight * (near[3] + mine[g][3])
+                    weight_refs[a][cell, first + g, at % 9] = weight
+                    totals[g] = totals[g] + weight
+            for g in range(count):
+                sums_ref[cell, spots[g], :] = totals[g]
+
+        def two_groups(pair, _):
+            some_groups(pair * 2, 2)
             return 0
 
-        lax.fori_loop(0, groups, one_group, 0)
-        sums = jnp.sum(sums_ref[...].T, axis=0, keepdims=True)
-        diagonal_ref[y, pl.ds(z, 1), :] = sums
-        return 0
-
-    lax.fori_loop(0, 16, one_cell, 0)
-    sums = diagonal_ref[...]
-    inverse_ref[...] = live_ref[...] / (dirichlet_ref[...] + sums)
-    diagonal_ref[...] = live_ref[...] * dirichlet_ref[...] + sums
+        lax.fori_loop(0, groups >> 1, two_groups, 0)
+
+        @pl.when((groups & 1) == 1)
+        def _():
+            some_groups(groups - 1, 1)
+
+    for y in range(2):
+        def cell_of(z, _, y=y):
+            one_cell(y, z)
+            return 0
+
+        lax.fori_loop(0, 8, cell_of, 0)
+
+    row_sums(sums_ref, diagonal_ref)
+    live = live_ref[...]
+    sums = jnp.where(live == 0.0, 0.0, diagonal_ref[...])
+    inverse_ref[...] = live / (dirichlet_ref[...] + sums)
+    diagonal_ref[...] = live * dirichlet_ref[...] + sums
+    copies[0].wait()
 
 
 def coarse_lift(values_ref, coarse_ref, basis_ref, part_ref):
@@ -194,9 +282,10 @@
 
 
 def image_kernel(
-    second_ref, counts_ref, weight_ref, own_ref, before_ref, after_ref, below_ref, above_ref, across_ref,
-    diagonal_ref, residual_ref, basis_ref, *rest,
+    second_ref, counts_ref, weight_a, weight_b, weight_c, own_ref, before_ref, after_ref, below_ref, above_ref,
+    across_ref, live_ref, diagonal_ref, residual_ref, basis_ref, *rest,
 ):
+    weight_refs = (weight_a, weight_b, weight_c)
     olds, (image_ref, payload_ref, near_ref, sums_ref, part_ref) = rest[:-5], rest[-5:]
     second = second_ref[0]
     tile = (8, SLOTS)
@@ -210,26 +299,33 @@
         lambda at: across_ref[at : at + 1], second, put,
     )
 
-    def one_cell(cell, _):
-        y, z = cell // 8, cell % 8
-        groups = (counts_ref[cell] + 7) // 8
-        sums_ref[...] = jnp.zeros((SLOTS, SLOTS), jnp.float32)
-
-        def one_group(group, _):
-            parts = [jnp.zeros(tile, jnp.float32) for _ in range(3)]
+    def one_cell(y, z):
+        cell = y * 8 + z
+
+        def two_groups(pair, _):
+            parts = [[jnp.zeros(tile, jnp.float32) for _ in range(3)] for _ in range(2)]
             for at in range(27):
                 a, b, c = at // 9, at // 3 % 3, at % 3
-                parts[at % 3] = parts[at % 3] + weight_ref[cell, group, at] * near_ref[a, y + b, z + c]
-            sums_ref[pl.ds(pl.multiple_of(group * 8, 8), 8), :] = parts[0] + parts[1] + parts[2]
+                near = near_ref[a, y + b, z + c]
+                for g in range(2):
+                    parts[g][at % 3] = parts[g][at % 3] + weight_refs[a][cell, pair * 2 + g, at % 9] * near
+            for g in range(2):
+                spot = pl.ds(pl.multiple_of((pair * 2 + g) * 8, 8), 8)
+                sums_ref[cell, spot, :] = parts[g][0] + parts[g][1] + parts[g][2]
             return 0
 
-        lax.fori_loop(0, groups, one_group, 0)
-        image_ref[y, pl.ds(z, 1), :] = jnp.sum(sums_ref[...].T, axis=0, keepdims=True)
-        return 0
-
-    lax.fori_loop(0, 16, one_cell, 0)
+        lax.fori_loop(0, (counts_ref[0, y, z] + 15) >> 4, two_groups, 0)
+
+    for y in range(2):
+        def cell_of(z, _, y=y):
+            one_cell(y, z)
+            return 0
+
+        lax.fori_loop(0, 8, cell_of, 0)
+
+    row_sums(sums_ref, image_ref)
     own = own_ref[...]
-    image = diagonal_ref[...] * own - image_ref[...]
+    image = jnp.where(live_ref[...] == 0.0, 0.0, diagonal_ref[...] * own - image_ref[...])
     image_ref[...] = image
     payload_ref[0:1, :] = project(basis_ref, image, part_ref, second)
     pairs = [(residual_ref[...], own), (own, image)]
@@ -246,80 +342,90 @@
 
 
 def around(field, second):
+    count = field.shape[0]
     up, down = steps("gx")
     before = lax.ppermute(field, "gx", up)
     after = lax.ppermute(field, "gx", down)
-    three = jnp.stack([before, field, after], axis=-4)
+    side = f32(count, 3, 8, SLOTS)
+    upper, lower = call(side_faces_kernel, (side, side), [VM] * 3)(before, field, after)
     up, down = steps("gy")
-    below = lax.ppermute(three[..., :, 1, :, :], "gy", up)
-    above = lax.ppermute(three[..., :, 0, :, :], "gy", down)
-    full = jnp.concatenate([below[..., :, None, :, :], three, above[..., :, None, :, :]], axis=-3)
-    face = jnp.where(second == 0, full[..., 7, :], full[..., 0, :])
-    face = face.reshape(face.shape[:-3] + (12, SLOTS))
+    below = lax.ppermute(upper, "gy", up)
+    above = lax.ppermute(lower, "gy", down)
+    face = call(top_face_kernel, f32(count, 12, SLOTS), [SM] + [VM] * 5)(second, before, field, after, below, above)
     across = lax.ppermute(face, "gz", [(0, 1), (1, 0)])
     return before, after, below, above, across
 
 
 def gather(payload):
-    both = payload + lax.ppermute(payload, "gz", [(0, 1), (1, 0)])
+    theirs = lax.ppermute(payload, "gz", [(0, 1), (1, 0)])
     rows = payload.shape[0]
-    spread = jnp.broadcast_to(both[None], (128, rows, SLOTS))
+    spread = call(spread_kernel, f32(128, rows, SLOTS), [VM] * 2)(payload, theirs)
     got = lax.all_to_all(spread, ("gx", "gy"), 0, 0, tiled=True)
     return got.reshape(128 * rows, SLOTS)
 
 
 def per_device(offsets, counts, correction, dirichlet, right_side, deflation, coarse_inverse):
     second = lax.axis_index("gz").astype(jnp.int32)
-    second_ref = second.reshape(1)
-    cell_counts = counts.reshape(16)
+    second = second.reshape(1)
     block = lambda x: x.reshape(2, 8, SLOTS)
     offsets = offsets.reshape(3, 2, 8, SLOTS)
-    dirichlet, right_side = block(dirichlet), block(right_side)
+    dirichlet, right_side, correction = block(dirichlet), block(right_side), block(correction)
     basis = deflation.reshape(64, 2, 8, SLOTS)
     cells = f32(2, 8, SLOTS)
 
-    live, residual, payload = call(
-        prepare_kernel, (cells, cells, f32(1, SLOTS)), [SM, SM, VM, VM], [pltpu.VMEM((64, SLOTS), jnp.float32)]
-    )(second_ref, cell_counts, right_side, basis)
-    scaled = (block(correction) * live) * (10.0 / SLOTS)
-    geometry = jnp.concatenate([offsets, scaled[None]], 0)
+    onchip = lambda x: pltpu.with_memory_space_constraint(x, pltpu.VMEM)
+    outside = lambda x: pltpu.with_memory_space_constraint(x, pltpu.HBM)
+    vmem = lambda *shape: pltpu.VMEM(shape, jnp.float32)
+    part = vmem(64, SLOTS)
+
+    geometry, live, residual, payload, counts, dirichlet, basis = call(
+        prepare_kernel,
+        (
+            f32(4, 2, 8, SLOTS), cells, cells, f32(1, SLOTS),
+            pltpu.VMEM((1, 2, 8), jnp.int32), vmem(2, 8, SLOTS), vmem(64, 2, 8, SLOTS),
+        ),
+        [SM] + [ANY] * 6,
+        [
+            pltpu.SMEM((1, 2, 8), jnp.int32), vmem(3, 2, 8, SLOTS), vmem(2, 8, SLOTS), vmem(2, 8, SLOTS), part,
+            pltpu.SemaphoreType.DMA((7,)),
+        ],
+    )(second, *map(outside, (counts, offsets, correction, right_side, dirichlet, basis)))
+    counts, dirichlet, basis = onchip(counts), onchip(dirichlet), onchip(basis)
     halo = around(geometry, second)
     coefficient = gather(payload)
-    part = pltpu.VMEM((64, SLOTS), jnp.float32)
-
-    weight, diagonal, inverse = call(
+    coefficient, geometry = lax.optimization_barrier((coefficient, geometry))
+
+    *weights, diagonal, inverse, coarse = call(
         weights_kernel,
-        (f32(16, 16, 27, 8, SLOTS), cells, cells),
-        [SM, SM] + [VM] * 8,
+        (*(vmem(16, 16, 9, 8, SLOTS),) * 3, cells, cells, vmem(64, 128 * SLOTS)),
+        [SM, SM] + [VM] * 8 + [ANY],
         [
-            pltpu.VMEM((4, 3, 4, 10, 8, SLOTS), jnp.float32),
-            pltpu.VMEM((4, SLOTS, SLOTS), jnp.float32),
-            pltpu.VMEM((SLOTS, SLOTS), jnp.float32),
+            vmem(4, 3, 4, 10, 8, SLOTS), vmem(16, 4, SLOTS, SLOTS), vmem(16, SLOTS, SLOTS),
+            pltpu.SemaphoreType.DMA((1,)),
         ],
-        limit=56 * 2**20,
-    )(second_ref, cell_counts, geometry, *halo, live, dirichlet)
+        limit=8 * 2**20,
+    )(second, counts, geometry, *halo, live, dirichlet, outside(coarse_inverse))
+    weights, coarse = [onchip(x) for x in weights], onchip(coarse)
 
     def image_of(field, residual, *olds):
         return call(
             image_kernel,
             (cells, f32(2, SLOTS)),
-            [SM, SM] + [VM] * (10 + len(olds)),
-            [
-                pltpu.VMEM((3, 4, 10, 8, SLOTS), jnp.float32),
-                pltpu.VMEM((SLOTS, SLOTS), jnp.float32),
-                part,
-            ],
-            limit=56 * 2**20,
-        )(second_ref, cell_counts, weight, field, *around(field, second), diagonal, residual, basis, *olds)
+            [SM, SM] + [VM] * (13 + len(olds)),
+            [vmem(3, 4, 10, 8, SLOTS), vmem(16, SLOTS, SLOTS), part],
+        )(
+            second, counts, *weights, field, *(piece[0] for piece in around(field[None], second)),
+            live, diagonal, residual, basis, *olds,
+        )
 
     smoothed = call(first_smooth_kernel, cells, [VM] * 6, [part])(
-        coefficient, coarse_inverse, basis, live, residual, inverse
+        coefficient, coarse, basis, live, residual, inverse
     )
     image, payload = image_of(smoothed, residual)
     gathered_first = gather(payload)
     coefficient, residual, second_smoothed = call(
         second_smooth_kernel, (f32(128, SLOTS), cells, cells), [VM] * 9, [part]
-    )(gathered_first, coefficient, coarse_inverse, basis, live, residual, inverse, smoothed, image)
+    )(gathered_first, coefficient, coarse, basis, live, residual, inverse, smoothed, image)
     second_image, payload = image_of(second_smoothed, residual, smoothed, image)
     gathered = gather(payload)
     pressure, residual, third_smoothed, direction, payload = call(
@@ -328,11 +434,10 @@
         [VM] * 12,
         [pltpu.VMEM((128, SLOTS), jnp.float32), part],
     )(
-        gathered, gathered_first, coefficient, coarse_inverse, basis, live, residual, inverse,
+        gathered, gathered_first, coefficient, coarse, basis, live, residual, inverse,
         smoothed, image, second_smoothed, second_image,
     )
-    totals = jnp.sum(gather(payload), axis=0)
-    direction = third_smoothed + totals[0] / totals[1] * direction
+    direction = call(finish_kernel, cells, [VM] * 3)(gather(payload), third_smoothed, direction)
     shape = (1, 2, 8, SLOTS)
     return pressure.reshape(shape), residual.reshape(shape), direction.reshape(shape)
 

time: 232 us -> 174 us (0.75)
  Pallas kernels: 77.9 us -> 30 us
  waiting for transfers between devices: 8.66 us -> 18.5 us
  other arithmetic: 7.72 us -> 0 us
  local copies, waits for them, and re-layouts: 7.65 us -> 0 us
    pallas_call x4 -> x15, Pallas kernels: 66.8 us -> 27.3 us  [the longest x1 17.1 us: per_device(): call(weights_kernel, (*(vmem(16, 16, 9, 8, SLOTS),) * 3, cells, cells, vm...]
    ppermute x10, waiting for transfers between devices: 5.06 us -> 13.4 us  [the longest x3 9.78 us: around(): above = lax.ppermute(lower, 'gy', down)]
    ppermute x10, starting transfers between devices: 20.7 us -> 17.2 us  [the longest x3 7.33 us: around(): below = lax.ppermute(upper, 'gy', up)]
    unnamed x29 -> x0, local copies, waits for them, and re-layouts: 3.14 us -> none
    pallas_call x1, Pallas kernels: 3.72 us -> 0.72 us  [per_device(): call(second_smooth_kernel, (f32(128, SLOTS), cells, cells), [VM] * 9, [pa...]
    pallas_call x1, Pallas kernels: 3.46 us -> 0.64 us  [per_device(): call(first_smooth_kernel, cells, [VM] * 6, [part])]
    pallas_call x1, Pallas kernels: 3.83 us -> 1.32 us  [per_device(): call(third_smooth_kernel, (cells, cells, cells, cells, f32(1, SLOTS)), [V...]
  transfers between devices with their start and end apart: 20 -> 20, of which waited for: 9 -> 13; matrix products, arithmetic and copies ran while one was open for 1% -> 0% of each run, Pallas kernels for 15% -> 0%
where the time goes in v2:
time: 174 us; the launch traced here: 173 us
  blocking collectives  65.9 us (38%)
  starting transfers between devices  58 us (33%)
  Pallas kernels  30 us (17%)
  waiting for transfers between devices  18.5 us (11%)
    all_to_all x3, blocking collectives, gather(): got = lax.all_to_all(spread, ('gx', 'gy'), 0, 0, tiled=True)  65.9 us
    pallas_call x1, Pallas kernels, per_device(): call(weights_kernel, (*(vmem(16, 16, 9, 8, SLOTS),) * 3, cells, cells, vm...  17.1 us
    all_to_all x1, starting transfers between devices, gather(): got = lax.all_to_all(spread, ('gx', 'gy'), 0, 0, tiled=True)  13.8 us
    ppermute x3, starting transfers between devices, around(): before = lax.ppermute(field, 'gx', up)  13.4 us
    ppermute x3, waiting for transfers between devices, around(): above = lax.ppermute(lower, 'gy', down)  9.78 us
    ppermute x3, starting transfers between devices, around(): across = lax.ppermute(face, 'gz', [(0, 1), (1, 0)])  9.73 us
    ppermute x3, starting transfers between devices, around(): below = lax.ppermute(upper, 'gy', up)  7.33 us
    pallas_call x2, Pallas kernels, image_of(): call(image_kernel, (cells, f32(2, SLOTS)), [SM, SM] + [VM] * (13 + len(ol...  7.2 us
  transfers between devices with their start and end apart: 20, of which 13 were waited for; matrix products, arithmetic and copies ran while one was open for 0% of the time, Pallas kernels for 0%

profile of v2, /device:TPU:1, one launch (start us, length us, event | category | flops | bytes accessed | tf_op | source)
XLA Modules:
  0.0 173.2 jit_solution(14775732004019957813)
XLA Ops:
  0.6 1.4 shard_map.94
  2.1 3.3 %collective-permute-start = (f32[1,128]{1,0:T(1,128)S(1)}, f32[1,128]{1,0:T(1,128)S(1)}, u32[]{:S(2)}, u32[]{:S(2)}) collective-permute-start(f32[1,128]{1,0:T(1,128)S(1)} %get-tuple-element.37.mine_ref), channel_id=1, source_target_pairs={{0,1},{1,0},{2,3},{3,2},{4,5},{5,4},{6,7},{7,6},{8,9},{9,8},{10,11... | collective-permute-start | bytes 1544 | tf_op jit(solution)/shard_map/ppermute | solution.py:360
  5.4 0.8 collective-permute-done.theirs_ref
  6.2 0.6 shard_map.95
  6.8 13.8 %all-to-all-start = ((f32[128,1,128]{2,1,0:T(1,128)}), f32[128,1,128]{2,1,0:T(1,128)S(1)}, u32[]{:S(2)}, u32[]{:S(2)}) async-start(f32[128,1,128]{2,1,0:T(1,128)} %shard_map.95), calls=%async_computation | async-start | bytes 131072 | tf_op jit(solution)/shard_map/all_to_all | solution.py:363
  20.7 1.3 collective-permute-start.2
  22.0 4.0 %collective-permute-start.1 = (f32[4,2,8,128]{3,2,1,0:T(8,128)S(1)}, f32[4,2,8,128]{3,2,1,0:T(8,128)S(1)}, u32[]{:S(2)}, u32[]{:S(2)}) collective-permute-start(f32[4,2,8,128]{3,2,1,0:T(8,128)S(1)} %get-tuple-element.39.field_ref.own_ref), channel_id=1, source_target_pairs={{0,8},{8,16},{16,24},{24,32},{32,40},{40,48},{48,56},{56,64},{64,7... | collective-permute-start | bytes 98312 | tf_op jit(solution)/shard_map/ppermute | solution.py:347
  26.0 0.0 collective-permute-done.2.after_ref
  26.0 1.0 collective-permute-done.1.before_ref
  27.0 2.5 %collective-permute-start.3 = (f32[4,3,8,128]{3,2,1,0:T(8,128)S(1)}, f32[4,3,8,128]{3,2,1,0:T(8,128)S(1)}, u32[]{:S(2)}, u32[]{:S(2)}) collective-permute-start(f32[4,3,8,128]{3,2,1,0:T(8,128)S(1)} %get-tuple-element.40), channel_id=1, source_target_pairs={{0,2},{2,4},{4,6},{1,3},{3,5},{5,7},{8,10},{10,12},{12,14},{9,11},... | collective-permute-start | bytes 147464 | tf_op jit(solution)/shard_map/ppermute | solution.py:352
  29.4 1.3 collective-permute-start.4
  30.7 0.0 collective-permute-done.3.below_ref
  30.8 3.5 %collective-permute-done.4.above_ref = f32[4,3,8,128]{3,2,1,0:T(8,128)S(1)} collective-permute-done((f32[4,3,8,128]{3,2,1,0:T(8,128)S(1)}, f32[4,3,8,128]{3,2,1,0:T(8,128)S(1)}, u32[]{:S(2)}, u32[]{:S(2)}) %collective-permute-start.4) | collective-permute-done | bytes 49184 | tf_op jit(solution)/shard_map/ppermute | solution.py:353
  34.3 3.6 %collective-permute-start.5 = (f32[4,12,128]{2,1,0:T(8,128)S(1)}, f32[4,12,128]{2,1,0:T(8,128)S(1)}, u32[]{:S(2)}, u32[]{:S(2)}) collective-permute-start(f32[4,12,128]{2,1,0:T(8,128)S(1)} %shard_map.97), channel_id=1, source_target_pairs={{0,1},{1,0},{2,3},{3,2},{4,5},{5,4},{6,7},{7,6},{8,9},{9,8},{10,11... | collective-permute-start | bytes 73736 | tf_op jit(solution)/shard_map/ppermute | solution.py:355
  37.9 0.0 all-to-all-done
  37.9 0.9 collective-permute-done.5.across_ref
  38.7 17.1 %shard_map.98 = (f32[16,16,9,8,128]{4,3,2,1,0:T(8,128)S(1)}, f32[16,16,9,8,128]{4,3,2,1,0:T(8,128)S(1)}, f32[16,16,9,8,128]{4,3,2,1,0:T(8,128)S(1)}, f32[2,8,128...) custom-call(s32[1]{0:T(128)} %bitcast.second_ref, s32[1,2,8]{2,1,0:T(2,128)S(1)} %get-tuple-element.36.counts_ref, ...), custom_call_target="tpu_custom_call" | custom-call | tf_op jit(solution)/shard_map/pallas_call | solution.py:398
  55.8 0.6 shard_map.99.own_ref.smoothed_ref.rest_0_.first_ref
  56.4 1.3 collective-permute-start.7
  57.7 5.4 %collective-permute-start.6 = (f32[1,2,8,128]{3,2,1,0:T(8,128)S(1)}, f32[1,2,8,128]{3,2,1,0:T(8,128)S(1)}, u32[]{:S(2)}, u32[]{:S(2)}) collective-permute-start(f32[1,2,8,128]{3,2,1,0:T(8,128)S(1)} %bitcast.31), channel_id=1, source_target_pairs={{0,8},{8,16},{16,24},{24,32},{32,40},{40,48},{48,56},{56,64},{64,7... | collective-permute-start | bytes 24584 | tf_op jit(solution)/shard_map/ppermute | solution.py:347
  63.2 0.0 collective-permute-done.7.after_ref
  63.2 0.8 collective-permute-done.6.before_ref
  63.9 2.7 %collective-permute-start.8 = (f32[1,3,8,128]{3,2,1,0:T(8,128)S(1)}, f32[1,3,8,128]{3,2,1,0:T(8,128)S(1)}, u32[]{:S(2)}, u32[]{:S(2)}) collective-permute-start(f32[1,3,8,128]{3,2,1,0:T(8,128)S(1)} %get-tuple-element.52), channel_id=1, source_target_pairs={{0,2},{2,4},{4,6},{1,3},{3,5},{5,7},{8,10},{10,12},{12,14},{9,11},... | collective-permute-start | bytes 36872 | tf_op jit(solution)/shard_map/ppermute | solution.py:352
  66.6 1.3 collective-permute-start.9
  67.9 0.0 collective-permute-done.8.below_ref
  67.9 3.1 %collective-permute-done.9.above_ref = f32[1,3,8,128]{3,2,1,0:T(8,128)S(1)} collective-permute-done((f32[1,3,8,128]{3,2,1,0:T(8,128)S(1)}, f32[1,3,8,128]{3,2,1,0:T(8,128)S(1)}, u32[]{:S(2)}, u32[]{:S(2)}) %collective-permute-start.9) | collective-permute-done | bytes 12320 | tf_op jit(solution)/shard_map/ppermute | solution.py:353
  71.1 1.8 %collective-permute-start.10 = (f32[1,12,128]{2,1,0:T(8,128)S(1)}, f32[1,12,128]{2,1,0:T(8,128)S(1)}, u32[]{:S(2)}, u32[]{:S(2)}) collective-permute-start(f32[1,12,128]{2,1,0:T(8,128)S(1)} %shard_map.101), channel_id=1, source_target_pairs={{0,1},{1,0},{2,3},{3,2},{4,5},{5,4},{6,7},{7,6},{8,9},{9,8},{10,11... | collective-permute-start | bytes 18440 | tf_op jit(solution)/shard_map/ppermute | solution.py:355
  72.9 0.8 collective-permute-done.10
  73.7 3.6 %shard_map.102 = (f32[2,8,128]{2,1,0:T(8,128)S(1)}, f32[2,128]{1,0:T(2,128)S(1)}) custom-call(s32[1]{0:T(128)} %bitcast.second_ref, s32[1,2,8]{2,1,0:T(2,128)S(1)} %get-tuple-element.36.counts_ref, f32[16,16,9,8,128]{4,3,2,1,0:T(8,128)S(1)} %get-tuple-element.44.weight_a, f32[16,16,9,8,128]{4,3,2,1,0:T(8,128)S(1)} %get-tuple-element.45.weight_b, ...), custom_call_target="tpu_custom_call" | custom-call | tf_op jit(solution)/shard_map/pallas_call | solution.py:411
  77.3 0.2 collective-permute-start.11
  77.6 1.0 collective-permute-done.11.theirs_ref
  78.6 28.3 %all_to_all.20 = f32[128,2,128]{2,1,0:T(2,128)S(1)} all-to-all(f32[128,2,128]{2,1,0:T(2,128)S(1)} %shard_map.103), channel_id=1, replica_groups=mesh['gx'=32,'gy'=4,'gz'=2] {'gx','gy'}, dimensions={0} | all-to-all | bytes 262144 | tf_op jit(solution)/shard_map/all_to_all | solution.py:363
  106.9 0.7 shard_map.104
  107.6 1.3 collective-permute-start.13
  108.9 4.0 %collective-permute-start.12 = (f32[1,2,8,128]{3,2,1,0:T(8,128)S(1)}, f32[1,2,8,128]{3,2,1,0:T(8,128)S(1)}, u32[]{:S(2)}, u32[]{:S(2)}) collective-permute-start(f32[1,2,8,128]{3,2,1,0:T(8,128)S(1)} %bitcast.36), channel_id=1, source_target_pairs={{0,8},{8,16},{16,24},{24,32},{32,40},{40,48},{48,56},{56,64},{64,7... | collective-permute-start | bytes 24584 | tf_op jit(solution)/shard_map/ppermute | solution.py:347
  112.9 0.0 collective-permute-done.13.after_ref
  112.9 0.8 collective-permute-done.12.before_ref
  113.7 2.2 %collective-permute-start.14 = (f32[1,3,8,128]{3,2,1,0:T(8,128)S(1)}, f32[1,3,8,128]{3,2,1,0:T(8,128)S(1)}, u32[]{:S(2)}, u32[]{:S(2)}) collective-permute-start(f32[1,3,8,128]{3,2,1,0:T(8,128)S(1)} %get-tuple-element.58), channel_id=1, source_target_pairs={{0,2},{2,4},{4,6},{1,3},{3,5},{5,7},{8,10},{10,12},{12,14},{9,11},... | collective-permute-start | bytes 36872 | tf_op jit(solution)/shard_map/ppermute | solution.py:352
  115.9 1.3 collective-permute-start.15
  117.2 0.0 collective-permute-done.14.below_ref
  117.2 3.1 %collective-permute-done.15.above_ref = f32[1,3,8,128]{3,2,1,0:T(8,128)S(1)} collective-permute-done((f32[1,3,8,128]{3,2,1,0:T(8,128)S(1)}, f32[1,3,8,128]{3,2,1,0:T(8,128)S(1)}, u32[]{:S(2)}, u32[]{:S(2)}) %collective-permute-start.15) | collective-permute-done | bytes 12320 | tf_op jit(solution)/shard_map/ppermute | solution.py:353
  120.4 4.4 %collective-permute-start.16 = (f32[1,12,128]{2,1,0:T(8,128)S(1)}, f32[1,12,128]{2,1,0:T(8,128)S(1)}, u32[]{:S(2)}, u32[]{:S(2)}) collective-permute-start(f32[1,12,128]{2,1,0:T(8,128)S(1)} %shard_map.106), channel_id=1, source_target_pairs={{0,1},{1,0},{2,3},{3,2},{4,5},{5,4},{6,7},{7,6},{8,9},{9,8},{10,11... | collective-permute-start | bytes 18440 | tf_op jit(solution)/shard_map/ppermute | solution.py:355
  124.7 0.8 collective-permute-done.16
  125.6 3.6 %shard_map.107 = (f32[2,8,128]{2,1,0:T(8,128)S(1)}, f32[2,128]{1,0:T(2,128)S(1)}) custom-call(s32[1]{0:T(128)} %bitcast.second_ref, s32[1,2,8]{2,1,0:T(2,128)S(1)} %get-tuple-element.36.counts_ref, f32[16,16,9,8,128]{4,3,2,1,0:T(8,128)S(1)} %get-tuple-element.44.weight_a, f32[16,16,9,8,128]{4,3,2,1,0:T(8,128)S(1)} %get-tuple-element.45.weight_b, ...), custom_call_target="tpu_custom_call" | custom-call | tf_op jit(solution)/shard_map/pallas_call | solution.py:411
  129.2 0.4 collective-permute-start.17
  129.6 1.0 collective-permute-done.17.theirs_ref
  130.6 21.5 %all_to_all.21 = f32[128,2,128]{2,1,0:T(2,128)S(1)} all-to-all(f32[128,2,128]{2,1,0:T(2,128)S(1)} %shard_map.108), channel_id=1, replica_groups=mesh['gx'=32,'gy'=4,'gz'=2] {'gx','gy'}, dimensions={0} | all-to-all | bytes 262144 | tf_op jit(solution)/shard_map/all_to_all | solution.py:363
  152.1 1.3 shard_map.109
  153.4 2.0 %collective-permute-start.18 = (f32[1,128]{1,0:T(1,128)S(1)}, f32[1,128]{1,0:T(1,128)S(1)}, u32[]{:S(2)}, u32[]{:S(2)}) collective-permute-start(f32[1,128]{1,0:T(1,128)S(1)} %get-tuple-element.66.mine_ref), channel_id=1, source_target_pairs={{0,1},{1,0},{2,3},{3,2},{4,5},{5,4},{6,7},{7,6},{8,9},{9,8},{10,11... | collective-permute-start | bytes 1544 | tf_op jit(solution)/shard_map/ppermute | solution.py:360
  155.5 0.8 collective-permute-done.18.theirs_ref
  156.3 16.1 %all_to_all.22 = f32[128,1,128]{2,1,0:T(1,128)S(1)} all-to-all(f32[128,1,128]{2,1,0:T(1,128)S(1)} %shard_map.110), channel_id=1, replica_groups=mesh['gx'=32,'gy'=4,'gz'=2] {'gx','gy'}, dimensions={0} | all-to-all | bytes 131072 | tf_op jit(solution)/shard_map/all_to_all | solution.py:363
  172.4 0.8 shard_map.111
  (9 shorter events, 0.2 us)
Async XLA Ops:
  2.1 4.1 %collective-permute-start = (f32[1,128]{1,0:T(1,128)S(1)}, f32[1,128]{1,0:T(1,128)S(1)}, u32[]{:S(2)}, u32[]{:S(2)}) collective-permute-start(f32[1,128]{1,0:T(1,128)S(1)} %get-tuple-element.37.mine_ref), channel_id=1, source_target_pairs={{0,1},{1,0},{2,3},{3,2},{4,5},{5,4},{6,7},{7,6},{8,9},{9,8},{10,11... | collective-permute-start | bytes 1544 | tf_op jit(solution)/shard_map/ppermute | solution.py:360
  6.8 31.0 %all-to-all-start = ((f32[128,1,128]{2,1,0:T(1,128)}), f32[128,1,128]{2,1,0:T(1,128)S(1)}, u32[]{:S(2)}, u32[]{:S(2)}) async-start(f32[128,1,128]{2,1,0:T(1,128)} %shard_map.95), calls=%async_computation | async-start | bytes 131072 | tf_op jit(solution)/shard_map/all_to_all | solution.py:363
  20.7 5.3 %collective-permute-start.2 = (f32[4,2,8,128]{3,2,1,0:T(8,128)S(1)}, f32[4,2,8,128]{3,2,1,0:T(8,128)S(1)}, u32[]{:S(2)}, u32[]{:S(2)}) collective-permute-start(f32[4,2,8,128]{3,2,1,0:T(8,128)S(1)} %get-tuple-element.39.field_ref.own_ref), channel_id=1, source_target_pairs={{8,0},{16,8},{24,16},{32,24},{40,32},{48,40},{56,48},{64,56},{72,6... | collective-permute-start | bytes 98312 | tf_op jit(solution)/shard_map/ppermute | solution.py:348
  22.0 5.0 %collective-permute-start.1 = (f32[4,2,8,128]{3,2,1,0:T(8,128)S(1)}, f32[4,2,8,128]{3,2,1,0:T(8,128)S(1)}, u32[]{:S(2)}, u32[]{:S(2)}) collective-permute-start(f32[4,2,8,128]{3,2,1,0:T(8,128)S(1)} %get-tuple-element.39.field_ref.own_ref), channel_id=1, source_target_pairs={{0,8},{8,16},{16,24},{24,32},{32,40},{40,48},{48,56},{56,64},{64,7... | collective-permute-start | bytes 98312 | tf_op jit(solution)/shard_map/ppermute | solution.py:347
  27.0 3.8 %collective-permute-start.3 = (f32[4,3,8,128]{3,2,1,0:T(8,128)S(1)}, f32[4,3,8,128]{3,2,1,0:T(8,128)S(1)}, u32[]{:S(2)}, u32[]{:S(2)}) collective-permute-start(f32[4,3,8,128]{3,2,1,0:T(8,128)S(1)} %get-tuple-element.40), channel_id=1, source_target_pairs={{0,2},{2,4},{4,6},{1,3},{3,5},{5,7},{8,10},{10,12},{12,14},{9,11},... | collective-permute-start | bytes 147464 | tf_op jit(solution)/shard_map/ppermute | solution.py:352
  29.4 4.8 %collective-permute-start.4 = (f32[4,3,8,128]{3,2,1,0:T(8,128)S(1)}, f32[4,3,8,128]{3,2,1,0:T(8,128)S(1)}, u32[]{:S(2)}, u32[]{:S(2)}) collective-permute-start(f32[4,3,8,128]{3,2,1,0:T(8,128)S(1)} %get-tuple-element.41), channel_id=1, source_target_pairs={{2,0},{4,2},{6,4},{3,1},{5,3},{7,5},{10,8},{12,10},{14,12},{11,9},... | collective-permute-start | bytes 147464 | tf_op jit(solution)/shard_map/ppermute | solution.py:353
  34.3 4.4 %collective-permute-start.5 = (f32[4,12,128]{2,1,0:T(8,128)S(1)}, f32[4,12,128]{2,1,0:T(8,128)S(1)}, u32[]{:S(2)}, u32[]{:S(2)}) collective-permute-start(f32[4,12,128]{2,1,0:T(8,128)S(1)} %shard_map.97), channel_id=1, source_target_pairs={{0,1},{1,0},{2,3},{3,2},{4,5},{5,4},{6,7},{7,6},{8,9},{9,8},{10,11... | collective-permute-start | bytes 73736 | tf_op jit(solution)/shard_map/ppermute | solution.py:355
  56.4 6.7 %collective-permute-start.7 = (f32[1,2,8,128]{3,2,1,0:T(8,128)S(1)}, f32[1,2,8,128]{3,2,1,0:T(8,128)S(1)}, u32[]{:S(2)}, u32[]{:S(2)}) collective-permute-start(f32[1,2,8,128]{3,2,1,0:T(8,128)S(1)} %bitcast.30), channel_id=1, source_target_pairs={{8,0},{16,8},{24,16},{32,24},{40,32},{48,40},{56,48},{64,56},{72,6... | collective-permute-start | bytes 24584 | tf_op jit(solution)/shard_map/ppermute | solution.py:348
  57.7 6.2 %collective-permute-start.6 = (f32[1,2,8,128]{3,2,1,0:T(8,128)S(1)}, f32[1,2,8,128]{3,2,1,0:T(8,128)S(1)}, u32[]{:S(2)}, u32[]{:S(2)}) collective-permute-start(f32[1,2,8,128]{3,2,1,0:T(8,128)S(1)} %bitcast.31), channel_id=1, source_target_pairs={{0,8},{8,16},{16,24},{24,32},{32,40},{40,48},{48,56},{56,64},{64,7... | collective-permute-start | bytes 24584 | tf_op jit(solution)/shard_map/ppermute | solution.py:347
  63.9 4.0 %collective-permute-start.8 = (f32[1,3,8,128]{3,2,1,0:T(8,128)S(1)}, f32[1,3,8,128]{3,2,1,0:T(8,128)S(1)}, u32[]{:S(2)}, u32[]{:S(2)}) collective-permute-start(f32[1,3,8,128]{3,2,1,0:T(8,128)S(1)} %get-tuple-element.52), channel_id=1, source_target_pairs={{0,2},{2,4},{4,6},{1,3},{3,5},{5,7},{8,10},{10,12},{12,14},{9,11},... | collective-permute-start | bytes 36872 | tf_op jit(solution)/shard_map/ppermute | solution.py:352
  66.6 4.4 %collective-permute-start.9 = (f32[1,3,8,128]{3,2,1,0:T(8,128)S(1)}, f32[1,3,8,128]{3,2,1,0:T(8,128)S(1)}, u32[]{:S(2)}, u32[]{:S(2)}) collective-permute-start(f32[1,3,8,128]{3,2,1,0:T(8,128)S(1)} %get-tuple-element.53), channel_id=1, source_target_pairs={{2,0},{4,2},{6,4},{3,1},{5,3},{7,5},{10,8},{12,10},{14,12},{11,9},... | collective-permute-start | bytes 36872 | tf_op jit(solution)/shard_map/ppermute | solution.py:353
  71.1 2.6 %collective-permute-start.10 = (f32[1,12,128]{2,1,0:T(8,128)S(1)}, f32[1,12,128]{2,1,0:T(8,128)S(1)}, u32[]{:S(2)}, u32[]{:S(2)}) collective-permute-start(f32[1,12,128]{2,1,0:T(8,128)S(1)} %shard_map.101), channel_id=1, source_target_pairs={{0,1},{1,0},{2,3},{3,2},{4,5},{5,4},{6,7},{7,6},{8,9},{9,8},{10,11... | collective-permute-start | bytes 18440 | tf_op jit(solution)/shard_map/ppermute | solution.py:355
  77.3 1.2 collective-permute-start.11
  107.6 5.3 %collective-permute-start.13 = (f32[1,2,8,128]{3,2,1,0:T(8,128)S(1)}, f32[1,2,8,128]{3,2,1,0:T(8,128)S(1)}, u32[]{:S(2)}, u32[]{:S(2)}) collective-permute-start(f32[1,2,8,128]{3,2,1,0:T(8,128)S(1)} %bitcast.35), channel_id=1, source_target_pairs={{8,0},{16,8},{24,16},{32,24},{40,32},{48,40},{56,48},{64,56},{72,6... | collective-permute-start | bytes 24584 | tf_op jit(solution)/shard_map/ppermute | solution.py:348
  108.9 4.8 %collective-permute-start.12 = (f32[1,2,8,128]{3,2,1,0:T(8,128)S(1)}, f32[1,2,8,128]{3,2,1,0:T(8,128)S(1)}, u32[]{:S(2)}, u32[]{:S(2)}) collective-permute-start(f32[1,2,8,128]{3,2,1,0:T(8,128)S(1)} %bitcast.36), channel_id=1, source_target_pairs={{0,8},{8,16},{16,24},{24,32},{32,40},{40,48},{48,56},{56,64},{64,7... | collective-permute-start | bytes 24584 | tf_op jit(solution)/shard_map/ppermute | solution.py:347
  113.7 3.5 %collective-permute-start.14 = (f32[1,3,8,128]{3,2,1,0:T(8,128)S(1)}, f32[1,3,8,128]{3,2,1,0:T(8,128)S(1)}, u32[]{:S(2)}, u32[]{:S(2)}) collective-permute-start(f32[1,3,8,128]{3,2,1,0:T(8,128)S(1)} %get-tuple-element.58), channel_id=1, source_target_pairs={{0,2},{2,4},{4,6},{1,3},{3,5},{5,7},{8,10},{10,12},{12,14},{9,11},... | collective-permute-start | bytes 36872 | tf_op jit(solution)/shard_map/ppermute | solution.py:352
  115.9 4.4 %collective-permute-start.15 = (f32[1,3,8,128]{3,2,1,0:T(8,128)S(1)}, f32[1,3,8,128]{3,2,1,0:T(8,128)S(1)}, u32[]{:S(2)}, u32[]{:S(2)}) collective-permute-start(f32[1,3,8,128]{3,2,1,0:T(8,128)S(1)} %get-tuple-element.59), channel_id=1, source_target_pairs={{2,0},{4,2},{6,4},{3,1},{5,3},{7,5},{10,8},{12,10},{14,12},{11,9},... | collective-permute-start | bytes 36872 | tf_op jit(solution)/shard_map/ppermute | solution.py:353
  120.4 5.2 %collective-permute-start.16 = (f32[1,12,128]{2,1,0:T(8,128)S(1)}, f32[1,12,128]{2,1,0:T(8,128)S(1)}, u32[]{:S(2)}, u32[]{:S(2)}) collective-permute-start(f32[1,12,128]{2,1,0:T(8,128)S(1)} %shard_map.106), channel_id=1, source_target_pairs={{0,1},{1,0},{2,3},{3,2},{4,5},{5,4},{6,7},{7,6},{8,9},{9,8},{10,11... | collective-permute-start | bytes 18440 | tf_op jit(solution)/shard_map/ppermute | solution.py:355
  129.2 1.4 collective-permute-start.17
  153.4 2.9 %collective-permute-start.18 = (f32[1,128]{1,0:T(1,128)S(1)}, f32[1,128]{1,0:T(1,128)S(1)}, u32[]{:S(2)}, u32[]{:S(2)}) collective-permute-start(f32[1,128]{1,0:T(1,128)S(1)} %get-tuple-element.66.mine_ref), channel_id=1, source_target_pairs={{0,1},{1,0},{2,3},{3,2},{4,5},{5,4},{6,7},{7,6},{8,9},{9,8},{10,11... | collective-permute-start | bytes 1544 | tf_op jit(solution)/shard_map/ppermute | solution.py:360

commit v3 on v2

--- a/solution.py
+++ b/solution.py
@@ -82,23 +82,30 @@
     payload_ref[...] = project(basis_ref, residual_ref[...], part_ref, second_ref[0])
 
 
-def side_faces_kernel(before_ref, field_ref, after_ref, up_ref, down_ref):
+def top_face_kernel(second_ref, field_ref, face_ref):
+    second = second_ref[0]
     for f in range(field_ref.shape[0]):
-        for x, ref in enumerate((before_ref, field_ref, after_ref)):
-            up_ref[f, x] = ref[f, 1]
-            down_ref[f, x] = ref[f, 0]
-
-
-def top_face_kernel(second_ref, before_ref, field_ref, after_ref, below_ref, above_ref, face_ref):
-    second = second_ref[0]
-
-    def pick(rows):
-        return jnp.where(second == 0, rows[7:8], rows[0:1])
-
+        for y in range(2):
+            rows = field_ref[f, y]
+            face_ref[f, y : y + 1, :] = jnp.where(second == 0, rows[7:8], rows[0:1])
+
+
+def side_faces_kernel(field_ref, across_ref, up_ref, down_ref):
     for f in range(field_ref.shape[0]):
-        for x, ref in enumerate((before_ref, field_ref, after_ref)):
-            for y, rows in enumerate((below_ref[f, x], ref[f, 0], ref[f, 1], above_ref[f, x])):
-                face_ref[f, x * 4 + y : x * 4 + y + 1, :] = pick(rows)
+        for y, ref in enumerate((down_ref, up_ref)):
+            ref[f, 0] = field_ref[f, y]
+            ref[f, 1] = jnp.broadcast_to(across_ref[f, y : y + 1, :], (8, SLOTS))
+
+
+def block_kernel(field_ref, across_ref, below_ref, above_ref, block_ref):
+    for f in range(field_ref.shape[0]):
+        block_ref[f, 0] = below_ref[f, 0]
+        block_ref[f, 1] = field_ref[f, 0]
+        block_ref[f, 2] = field_ref[f, 1]
+        block_ref[f, 3] = above_ref[f, 0]
+        rows = (below_ref[f, 1, 0:1], across_ref[f, 0:1], across_ref[f, 1:2], above_ref[f, 1, 0:1])
+        for y, row in enumerate(rows):
+            block_ref[f, 4, y : y + 1, :] = row
 
 
 def spread_kernel(mine_ref, theirs_ref, spread_ref):
@@ -114,20 +121,25 @@
     out_ref[...] = smoothed_ref[...] + inner / before * direction_ref[...]
 
 
-def assemble(own, before, after, below, above, across, second, put):
-    for x, block in enumerate((before, own, after)):
-        for y in range(4):
-            if y == 0:
-                rows = below(x)
-            elif y == 3:
-                rows = above(x)
-            else:
-                rows = block(y - 1)
-            for z in range(8):
-                put(x, y, z + 1, rows[z : z + 1])
-            row = across(x * 4 + y)
-            put(x, y, 0, jnp.where(second == 1, row, 0.0))
-            put(x, y, 9, jnp.where(second == 0, row, 0.0))
+def assemble(block, second, put):
+    for y in range(4):
+        rows = block(y)
+        for z in range(8):
+            put(y, z + 1, rows[z : z + 1])
+        row = block(4)[y : y + 1]
+        put(y, 0, jnp.where(second == 1, row, 0.0))
+        put(y, 9, jnp.where(second == 0, row, 0.0))
+
+
+def place_geometry(near_ref, slab, x, block_ref, second):
+    for f in range(4):
+        def put(y, z, row, f=f):
+            if f < 3:
+                row = row + float((x, y, z)[f])
+            near_ref[f, slab, y, z] = jnp.broadcast_to(row, (8, SLOTS))
+
+        assemble(lambda at: block_ref[f, at], second, put)
+    near_ref[0, slab] = jnp.where(near_ref[3, slab] == 0.0, FAR, near_ref[0, slab])
 
 
 def row_sums(sums_ref, out_ref):
@@ -135,30 +147,60 @@
         out_ref[cell // 8, cell % 8 : cell % 8 + 1, :] = jnp.sum(sums_ref[cell].T, axis=0, keepdims=True)
 
 
-def weights_kernel(
-    second_ref, counts_ref, own_ref, before_ref, after_ref, below_ref, above_ref, across_ref,
-    live_ref, dirichlet_ref, coarse_hbm,
-    weight_a, weight_b, weight_c, diagonal_ref, inverse_ref, coarse_ref, near_ref, mine_ref, sums_ref, sems,
-):
-    copies = fetch(((coarse_hbm, coarse_ref),), sems)
-    weight_refs = (weight_a, weight_b, weight_c)
-    second = second_ref[0]
-    tile = (8, SLOTS)
-    for f in range(4):
-        def put(x, y, z, row, f=f):
-            if f == 3:
-                near_ref[3, x, y, z] = jnp.broadcast_to(row, tile)
+def each_cell(one_cell):
+    for y in range(2):
+        def cell_of(z, _, y=y):
+            one_cell(y, z)
+            return 0
+
+        lax.fori_loop(0, 8, cell_of, 0)
+
+
+def weigh(counts_ref, near_ref, mine_ref, weight_refs, old_sums_ref, sums_ref):
+    def one_cell(y, z):
+        cell = y * 8 + z
+        groups = (counts_ref[0, y, z] + 7) >> 3
+
+        def some_groups(first, count):
+            spots = [pl.ds(pl.multiple_of((first + g) * 8, 8), 8) for g in range(count)]
+            mine = [[mine_ref[cell, f, spot, :] for f in range(4)] for spot in spots]
+            if old_sums_ref is None:
+                totals = [jnp.zeros((8, SLOTS), jnp.float32) for _ in spots]
             else:
-                near_ref[f, x, y, z] = jnp.broadcast_to(row + float((x, y, z)[f]), tile)
-
-        assemble(
-            lambda y: own_ref[f, y], lambda y: before_ref[f, y], lambda y: after_ref[f, y],
-            lambda x: below_ref[f, x], lambda x: above_ref[f, x],
-            lambda at: across_ref[f, at : at + 1], second, put,
-        )
-    dead = near_ref[3] == 0.0
-    near_ref[0] = jnp.where(dead, FAR, near_ref[0])
-
+                totals = [old_sums_ref[cell, spot, :] for spot in spots]
+            for slab, weight_ref in enumerate(weight_refs):
+                for at in range(9):
+                    near = [near_ref[f, slab, y + at // 3, z + at % 3] for f in range(4)]
+                    for g in range(count):
+                        dx, dy, dz = (near[f] - mine[g][f] for f in range(3))
+                        square = dx * dx + dy * dy + dz * dz
+                        radius = square * lax.rsqrt(jnp.maximum(square, 1e-30))
+                        fall = jnp.maximum(1.0 - radius, 0.0)
+                        weight = (square * fall) * (fall * fall) / (square + 0.01)
+                        weight = weight * (near[3] + mine[g][3])
+                        weight_ref[cell, first + g, at] = weight
+                        totals[g] = totals[g] + weight
+            for g in range(count):
+                sums_ref[cell, spots[g], :] = totals[g]
+
+        def four_groups(quad, _):
+            some_groups(quad * 4, 4)
+            return 0
+
+        lax.fori_loop(0, groups >> 2, four_groups, 0)
+
+        @pl.when((groups & 2) == 2)
+        def _():
+            some_groups((groups >> 2) * 4, 2)
+
+        @pl.when((groups & 1) == 1)
+        def _():
+            some_groups(groups - 1, 1)
+
+    each_cell(one_cell)
+
+
+def centre_kernel(own_ref, mine_ref):
     cell_row = lax.broadcasted_iota(jnp.int32, (16, SLOTS), 0)
     scale = own_ref[3].reshape(16, SLOTS)
     fields = (
@@ -172,46 +214,20 @@
         for cell in range(16):
             mine_ref[cell, f] = jnp.broadcast_to(columns[:, cell : cell + 1], (SLOTS, SLOTS))
 
-    def one_cell(y, z):
-        cell = y * 8 + z
-        groups = (counts_ref[0, y, z] + 7) >> 3
-
-        def some_groups(first, count):
-            spots = [pl.ds(pl.multiple_of((first + g) * 8, 8), 8) for g in range(count)]
-            mine = [[mine_ref[cell, f, spot, :] for f in range(4)] for spot in spots]
-            totals = [jnp.zeros(tile, jnp.float32) for _ in spots]
-            for at in range(27):
-                a, b, c = at // 9, at // 3 % 3, at % 3
-                near = [near_ref[f, a, y + b, z + c] for f in range(4)]
-                for g in range(count):
-                    dx, dy, dz = (near[f] - mine[g][f] for f in range(3))
-                    square = dx * dx + dy * dy + dz * dz
-                    radius = square * lax.rsqrt(jnp.maximum(square, 1e-30))
-                    fall = jnp.maximum(1.0 - radius, 0.0)
-                    weight = (square * fall) * (fall * fall) / (square + 0.01)
-                    weight = weight * (near[3] + mine[g][3])
-                    weight_refs[a][cell, first + g, at % 9] = weight
-                    totals[g] = totals[g] + weight
-            for g in range(count):
-                sums_ref[cell, spots[g], :] = totals[g]
-
-        def two_groups(pair, _):
-            some_groups(pair * 2, 2)
-            return 0
-
-        lax.fori_loop(0, groups >> 1, two_groups, 0)
-
-        @pl.when((groups & 1) == 1)
-        def _():
-            some_groups(groups - 1, 1)
-
-    for y in range(2):
-        def cell_of(z, _, y=y):
-            one_cell(y, z)
-            return 0
-
-        lax.fori_loop(0, 8, cell_of, 0)
-
+
+def middle_weights_kernel(second_ref, counts_ref, mine_ref, block_ref, weight_ref, sums_ref, near_ref):
+    place_geometry(near_ref, 0, 1, block_ref, second_ref[0])
+    weigh(counts_ref, near_ref, mine_ref, (weight_ref,), None, sums_ref)
+
+
+def outer_weights_kernel(
+    second_ref, counts_ref, before_ref, after_ref, old_sums_ref, mine_ref, live_ref, dirichlet_ref, coarse_hbm,
+    weight_a, weight_c, diagonal_ref, inverse_ref, coarse_ref, near_ref, sums_ref, sems,
+):
+    copies = fetch(((coarse_hbm, coarse_ref),), sems)
+    place_geometry(near_ref, 0, 0, before_ref, second_ref[0])
+    place_geometry(near_ref, 1, 2, after_ref, second_ref[0])
+    weigh(counts_ref, near_ref, mine_ref, (weight_a, weight_c), old_sums_ref, sums_ref)
     row_sums(sums_ref, diagonal_ref)
     live = live_ref[...]
     sums = jnp.where(live == 0.0, 0.0, diagonal_ref[...])
@@ -281,48 +297,51 @@
     payload_ref[...] = inner_row([(residual, smoothed), (residual_ref[...], smoothed_ref[...])])
 
 
+def place_field(near_ref, slab, block_ref, second):
+    def put(y, z, row):
+        near_ref[slab, y, z] = jnp.broadcast_to(row, (8, SLOTS))
+
+    assemble(lambda at: block_ref[at], second, put)
+
+
+def apply_weights(counts_ref, near_ref, weight_refs, old_sums_ref, sums_ref):
+    def one_cell(y, z):
+        cell = y * 8 + z
+
+        def two_groups(pair, _):
+            spots = [pl.ds(pl.multiple_of((pair * 2 + g) * 8, 8), 8) for g in range(2)]
+            parts = [[jnp.zeros((8, SLOTS), jnp.float32) for _ in range(3)] for _ in range(2)]
+            if old_sums_ref is not None:
+                for g in range(2):
+                    parts[g][0] = old_sums_ref[cell, spots[g], :]
+            for slab, weight_ref in enumerate(weight_refs):
+                for at in range(9):
+                    near = near_ref[slab, y + at // 3, z + at % 3]
+                    for g in range(2):
+                        parts[g][at % 3] = parts[g][at % 3] + weight_ref[cell, pair * 2 + g, at] * near
+            for g in range(2):
+                sums_ref[cell, spots[g], :] = parts[g][0] + parts[g][1] + parts[g][2]
+            return 0
+
+        lax.fori_loop(0, (counts_ref[0, y, z] + 15) >> 4, two_groups, 0)
+
+    each_cell(one_cell)
+
+
+def middle_image_kernel(second_ref, counts_ref, weight_ref, block_ref, sums_ref, near_ref):
+    place_field(near_ref, 0, block_ref, second_ref[0])
+    apply_weights(counts_ref, near_ref, (weight_ref,), None, sums_ref)
+
+
 def image_kernel(
-    second_ref, counts_ref, weight_a, weight_b, weight_c, own_ref, before_ref, after_ref, below_ref, above_ref,
-    across_ref, live_ref, diagonal_ref, residual_ref, basis_ref, *rest,
+    second_ref, counts_ref, weight_a, weight_c, own_ref, before_ref, after_ref, old_sums_ref,
+    live_ref, diagonal_ref, residual_ref, basis_ref, *rest,
 ):
-    weight_refs = (weight_a, weight_b, weight_c)
     olds, (image_ref, payload_ref, near_ref, sums_ref, part_ref) = rest[:-5], rest[-5:]
     second = second_ref[0]
-    tile = (8, SLOTS)
-
-    def put(x, y, z, row):
-        near_ref[x, y, z] = jnp.broadcast_to(row, tile)
-
-    assemble(
-        lambda y: own_ref[y], lambda y: before_ref[y], lambda y: after_ref[y],
-        lambda x: below_ref[x], lambda x: above_ref[x],
-        lambda at: across_ref[at : at + 1], second, put,
-    )
-
-    def one_cell(y, z):
-        cell = y * 8 + z
-
-        def two_groups(pair, _):
-            parts = [[jnp.zeros(tile, jnp.float32) for _ in range(3)] for _ in range(2)]
-            for at in range(27):
-                a, b, c = at // 9, at // 3 % 3, at % 3
-                near = near_ref[a, y + b, z + c]
-                for g in range(2):
-                    parts[g][at % 3] = parts[g][at % 3] + weight_refs[a][cell, pair * 2 + g, at % 9] * near
-            for g in range(2):
-                spot = pl.ds(pl.multiple_of((pair * 2 + g) * 8, 8), 8)
-                sums_ref[cell, spot, :] = parts[g][0] + parts[g][1] + parts[g][2]
-            return 0
-
-        lax.fori_loop(0, (counts_ref[0, y, z] + 15) >> 4, two_groups, 0)
-
-    for y in range(2):
-        def cell_of(z, _, y=y):
-            one_cell(y, z)
-            return 0
-
-        lax.fori_loop(0, 8, cell_of, 0)
-
+    place_field(near_ref, 0, before_ref, second)
+    place_field(near_ref, 1, after_ref, second)
+    apply_weights(counts_ref, near_ref, (weight_a, weight_c), old_sums_ref, sums_ref)
     row_sums(sums_ref, image_ref)
     own = own_ref[...]
     image = jnp.where(live_ref[...] == 0.0, 0.0, diagonal_ref[...] * own - image_ref[...])
@@ -341,19 +360,20 @@
     return up, [(j, i) for i, j in up]
 
 
-def around(field, second):
+def around(field, second, meanwhile=None):
     count = field.shape[0]
-    up, down = steps("gx")
-    before = lax.ppermute(field, "gx", up)
-    after = lax.ppermute(field, "gx", down)
-    side = f32(count, 3, 8, SLOTS)
-    upper, lower = call(side_faces_kernel, (side, side), [VM] * 3)(before, field, after)
+    face = call(top_face_kernel, f32(count, 2, SLOTS), [SM, VM])(second, field)
+    across = lax.ppermute(face, "gz", [(0, 1), (1, 0)])
+    side = f32(count, 2, 8, SLOTS)
+    upper, lower = call(side_faces_kernel, (side, side), [VM] * 2)(field, across)
     up, down = steps("gy")
     below = lax.ppermute(upper, "gy", up)
     above = lax.ppermute(lower, "gy", down)
-    face = call(top_face_kernel, f32(count, 12, SLOTS), [SM] + [VM] * 5)(second, before, field, after, below, above)
-    across = lax.ppermute(face, "gz", [(0, 1), (1, 0)])
-    return before, after, below, above, across
+    if meanwhile is not None:
+        below, above, meanwhile = lax.optimization_barrier((below, above, meanwhile))
+    block = call(block_kernel, f32(count, 5, 8, SLOTS), [VM] * 4)(field, across, below, above)
+    up, down = steps("gx")
+    return block, lax.ppermute(block, "gx", up), lax.ppermute(block, "gx", down), meanwhile
 
 
 def gather(payload):
@@ -391,30 +411,39 @@
         ],
     )(second, *map(outside, (counts, offsets, correction, right_side, dirichlet, basis)))
     counts, dirichlet, basis = onchip(counts), onchip(dirichlet), onchip(basis)
-    halo = around(geometry, second)
     coefficient = gather(payload)
-    coefficient, geometry = lax.optimization_barrier((coefficient, geometry))
-
-    *weights, diagonal, inverse, coarse = call(
-        weights_kernel,
-        (*(vmem(16, 16, 9, 8, SLOTS),) * 3, cells, cells, vmem(64, 128 * SLOTS)),
-        [SM, SM] + [VM] * 8 + [ANY],
-        [
-            vmem(4, 3, 4, 10, 8, SLOTS), vmem(16, 4, SLOTS, SLOTS), vmem(16, SLOTS, SLOTS),
-            pltpu.SemaphoreType.DMA((1,)),
-        ],
-        limit=8 * 2**20,
-    )(second, counts, geometry, *halo, live, dirichlet, outside(coarse_inverse))
-    weights, coarse = [onchip(x) for x in weights], onchip(coarse)
+    coefficient, centre = lax.optimization_barrier((coefficient, geometry))
+    mine = call(centre_kernel, f32(16, 4, SLOTS, SLOTS), [VM])(centre)
+    block, before, after, mine = around(geometry, second, mine)
+
+    sums_shape = f32(16, SLOTS, SLOTS)
+    weight_shape = vmem(16, 16, 9, 8, SLOTS)
+    weight_b, sums = call(
+        middle_weights_kernel,
+        (weight_shape, sums_shape),
+        [SM, SM] + [VM] * 2,
+        [vmem(4, 1, 4, 10, 8, SLOTS)],
+    )(second, counts, mine, block)
+    weight_a, weight_c, diagonal, inverse, coarse = call(
+        outer_weights_kernel,
+        (weight_shape, weight_shape, cells, cells, vmem(64, 128 * SLOTS)),
+        [SM, SM] + [VM] * 6 + [ANY],
+        [vmem(4, 2, 4, 10, 8, SLOTS), vmem(16, SLOTS, SLOTS), pltpu.SemaphoreType.DMA((1,))],
+    )(second, counts, before, after, sums, mine, live, dirichlet, outside(coarse_inverse))
+    weight_a, weight_b, weight_c, coarse = map(onchip, (weight_a, weight_b, weight_c, coarse))
 
     def image_of(field, residual, *olds):
+        block, before, after = (piece[0] for piece in around(field[None], second)[:3])
+        sums = call(middle_image_kernel, sums_shape, [SM, SM] + [VM] * 2, [vmem(1, 4, 10, 8, SLOTS)])(
+            second, counts, weight_b, block
+        )
         return call(
             image_kernel,
             (cells, f32(2, SLOTS)),
-            [SM, SM] + [VM] * (13 + len(olds)),
-            [vmem(3, 4, 10, 8, SLOTS), vmem(16, SLOTS, SLOTS), part],
+            [SM, SM] + [VM] * (10 + len(olds)),
+            [vmem(2, 4, 10, 8, SLOTS), vmem(16, SLOTS, SLOTS), part],
         )(
-            second, counts, *weights, field, *(piece[0] for piece in around(field[None], second)),
+            second, counts, weight_a, weight_c, field, before, after, sums,
             live, diagonal, residual, basis, *olds,
         )
 

time: 174 us -> 170 us (0.977)
  blocking collectives: 65.9 us -> 59.2 us
  Pallas kernels: 30 us -> 34.4 us
    all_to_all x3, blocking collectives: 65.9 us -> 59.2 us  [gather(): got = lax.all_to_all(spread, ('gx', 'gy'), 0, 0, tiled=True)]
    all_to_all x1, waiting for transfers between devices: 0.01 us -> 4.99 us  [gather(): got = lax.all_to_all(spread, ('gx', 'gy'), 0, 0, tiled=True)]
    pallas_call x9 -> x16, Pallas kernels: 24.3 us -> 28.8 us  [the longest x1 11.5 us: per_device(): call(outer_weights_kernel, (weight_shape, weight_shape, cells, cells, vme...]
    ppermute x4, starting transfers between devices: 6.01 us -> 10.5 us  [gather(): theirs = lax.ppermute(payload, 'gz', [(0, 1), (1, 0)])]
    ppermute x3, starting transfers between devices: 9.73 us -> 6.02 us  [around(): across = lax.ppermute(face, 'gz', [(0, 1), (1, 0)])]
    ppermute x3, waiting for transfers between devices: 9.78 us -> 6.17 us  [around(): above = lax.ppermute(lower, 'gy', down)]
    ppermute x6, waiting for transfers between devices: 2.53 us -> 0.02 us  [the longest x3 0.01 us: around(): lax.ppermute(block, 'gx', up)]
  transfers between devices with their start and end apart: 20 -> 20, of which waited for: 13 -> 10; matrix products, arithmetic and copies ran while one was open for 0% -> 0% of each run, Pallas kernels for 0% -> 7%
where the time goes in v3:
time: 170 us; the launch traced here: 169 us
  blocking collectives  59.2 us (35%)
  starting transfers between devices  57.3 us (34%)
  Pallas kernels  34.4 us (20%)
  waiting for transfers between devices  16.9 us (10%)
    all_to_all x3, blocking collectives, gather(): got = lax.all_to_all(spread, ('gx', 'gy'), 0, 0, tiled=True)  59.2 us
    all_to_all x1, starting transfers between devices, gather(): got = lax.all_to_all(spread, ('gx', 'gy'), 0, 0, tiled=True)  13.8 us
    ppermute x3, starting transfers between devices, around(): lax.ppermute(block, 'gx', up)  12 us
    pallas_call x1, Pallas kernels, per_device(): call(outer_weights_kernel, (weight_shape, weight_shape, cells, cells, vme...  11.5 us
    ppermute x4, starting transfers between devices, gather(): theirs = lax.ppermute(payload, 'gz', [(0, 1), (1, 0)])  10.5 us
    ppermute x3, starting transfers between devices, around(): below = lax.ppermute(upper, 'gy', up)  7.28 us
    pallas_call x1, Pallas kernels, per_device(): call(middle_weights_kernel, (weight_shape, sums_shape), [SM, SM] + [VM] *...  6.23 us
    pallas_call x2, Pallas kernels, image_of(): call(image_kernel, (cells, f32(2, SLOTS)), [SM, SM] + [VM] * (10 + len(ol...  6.17 us
  transfers between devices with their start and end apart: 20, of which 10 were waited for; matrix products, arithmetic and copies ran while one was open for 0% of the time, Pallas kernels for 7%

profile of v3, /device:TPU:1, one launch (start us, length us, event | category | flops | bytes accessed | tf_op | source)
XLA Modules:
  0.0 168.8 jit_solution(17463978318313833497)
XLA Ops:
  0.6 1.5 shard_map.94
  2.1 3.3 %collective-permute-start.3 = (f32[1,128]{1,0:T(1,128)S(1)}, f32[1,128]{1,0:T(1,128)S(1)}, u32[]{:S(2)}, u32[]{:S(2)}) collective-permute-start(f32[1,128]{1,0:T(1,128)S(1)} %get-tuple-element.44.mine_ref), channel_id=1, source_target_pairs={{0,1},{1,0},{2,3},{3,2},{4,5},{5,4},{6,7},{7,6},{8,9},{9,8},{10,11... | collective-permute-start | bytes 1544 | tf_op jit(solution)/shard_map/ppermute | solution.py:380
  5.4 0.8 collective-permute-done.3.theirs_ref
  6.2 0.7 shard_map.97
  6.9 13.8 %all-to-all-start = ((f32[128,1,128]{2,1,0:T(1,128)}), f32[128,1,128]{2,1,0:T(1,128)S(1)}, u32[]{:S(2)}, u32[]{:S(2)}) async-start(f32[128,1,128]{2,1,0:T(1,128)} %shard_map.97), calls=%async_computation | async-start | bytes 131072 | tf_op jit(solution)/shard_map/all_to_all | solution.py:383
  20.7 0.7 collective-permute-start
  21.4 0.8 collective-permute-done.across_ref
  22.2 2.7 %collective-permute-start.1 = (f32[4,2,8,128]{3,2,1,0:T(8,128)S(1)}, f32[4,2,8,128]{3,2,1,0:T(8,128)S(1)}, u32[]{:S(2)}, u32[]{:S(2)}) collective-permute-start(f32[4,2,8,128]{3,2,1,0:T(8,128)S(1)} %get-tuple-element.42), channel_id=1, source_target_pairs={{0,2},{2,4},{4,6},{1,3},{3,5},{5,7},{8,10},{10,12},{12,14},{9,11},... | collective-permute-start | bytes 98312 | tf_op jit(solution)/shard_map/ppermute | solution.py:370
  25.0 1.3 collective-permute-start.2
  26.3 5.0 %all-to-all-done = f32[128,1,128]{2,1,0:T(1,128)S(1)} async-done(((f32[128,1,128]{2,1,0:T(1,128)}), f32[128,1,128]{2,1,0:T(1,128)S(1)}, u32[]{:S(2)}, u32[]{:S(2)}) %all-to-all-start) | async-done | bytes 65568 | tf_op jit(solution)/shard_map/all_to_all | solution.py:383
  31.3 1.3 shard_map.98.mine_ref
  32.6 0.0 collective-permute-done.1.below_ref
  32.6 0.0 collective-permute-done.2.above_ref
  32.6 1.3 collective-permute-start.5
  33.9 4.0 %collective-permute-start.4 = (f32[4,5,8,128]{3,2,1,0:T(8,128)S(1)}, f32[4,5,8,128]{3,2,1,0:T(8,128)S(1)}, u32[]{:S(2)}, u32[]{:S(2)}) collective-permute-start(f32[4,5,8,128]{3,2,1,0:T(8,128)S(1)} %shard_map.99.block_ref), channel_id=1, source_target_pairs={{0,8},{8,16},{16,24},{24,32},{32,40},{40,48},{48,56},{56,64},{64,7... | collective-permute-start | bytes 245768 | tf_op jit(solution)/shard_map/ppermute | solution.py:376
  37.9 6.2 %shard_map.100 = (f32[16,16,9,8,128]{4,3,2,1,0:T(8,128)S(1)}, f32[16,128,128]{2,1,0:T(8,128)S(1)}) custom-call(s32[1]{0:T(128)} %bitcast.second_ref, s32[1,2,8]{2,1,0:T(2,128)S(1)} %get-tuple-element.40.counts_ref, f32[16,4,128,128]{3,2,1,0:T(8,128)S(1)} %shard_map.98.mine_ref, f32[4,5,8,128]{3,2,1,0:T(8,128)S(1)} %shard_map.99.block_ref), custom_call_target="tpu_custom_call" | custom-call | tf_op jit(solution)/shard_map/pallas_call | solution.py:421
  44.2 0.0 collective-permute-done.5.after_ref
  44.2 0.0 collective-permute-done.4.before_ref
  44.2 11.5 %shard_map.101 = (f32[16,16,9,8,128]{4,3,2,1,0:T(8,128)S(1)}, f32[16,16,9,8,128]{4,3,2,1,0:T(8,128)S(1)}, f32[2,8,128]{2,1,0:T(8,128)S(1)}, f32[2,8,128]{2,1,0:T(8,128)S(1)}, f32[64,16384]{1,0:T(8,128)S(1)}) custom-call(s32[1]{0:T(128)} %bitcast.second_ref, s32[1,2,8]{2,1,0:T(2,128)S(1)} %get-tuple-element.40.counts_ref, ...), custom_call_target="tpu_custom_call" | custom-call | tf_op jit(solution)/shard_map/pallas_call | solution.py:427
  55.7 0.6 shard_map.102.own_ref.smoothed_ref.rest_0_.first_ref
  56.3 3.0 %collective-permute-start.6 = (f32[1,2,128]{2,1,0:T(2,128)S(1)}, f32[1,2,128]{2,1,0:T(2,128)S(1)}, u32[]{:S(2)}, u32[]{:S(2)}) collective-permute-start(f32[1,2,128]{2,1,0:T(2,128)S(1)} %shard_map.103), channel_id=1, source_target_pairs={{0,1},{1,0},{2,3},{3,2},{4,5},{5,4},{6,7},{7,6},{8,9},{9,8},{10,11... | collective-permute-start | bytes 3080 | tf_op jit(solution)/shard_map/ppermute | solution.py:366
  59.2 0.8 collective-permute-done.6.across_ref
  60.1 2.6 %collective-permute-start.7 = (f32[1,2,8,128]{3,2,1,0:T(8,128)S(1)}, f32[1,2,8,128]{3,2,1,0:T(8,128)S(1)}, u32[]{:S(2)}, u32[]{:S(2)}) collective-permute-start(f32[1,2,8,128]{3,2,1,0:T(8,128)S(1)} %get-tuple-element.59), channel_id=1, source_target_pairs={{0,2},{2,4},{4,6},{1,3},{3,5},{5,7},{8,10},{10,12},{12,14},{9,11},... | collective-permute-start | bytes 24584 | tf_op jit(solution)/shard_map/ppermute | solution.py:370
  62.7 1.3 collective-permute-start.8
  64.0 0.0 collective-permute-done.7.below_ref
  64.0 3.1 %collective-permute-done.8.above_ref = f32[1,2,8,128]{3,2,1,0:T(8,128)S(1)} collective-permute-done((f32[1,2,8,128]{3,2,1,0:T(8,128)S(1)}, f32[1,2,8,128]{3,2,1,0:T(8,128)S(1)}, u32[]{:S(2)}, u32[]{:S(2)}) %collective-permute-start.8) | collective-permute-done | bytes 8224 | tf_op jit(solution)/shard_map/ppermute | solution.py:371
  67.1 1.3 collective-permute-start.10
  68.3 4.0 %collective-permute-start.9 = (f32[1,5,8,128]{3,2,1,0:T(8,128)S(1)}, f32[1,5,8,128]{3,2,1,0:T(8,128)S(1)}, u32[]{:S(2)}, u32[]{:S(2)}) collective-permute-start(f32[1,5,8,128]{3,2,1,0:T(8,128)S(1)} %shard_map.105), channel_id=1, source_target_pairs={{0,8},{8,16},{16,24},{24,32},{32,40},{40,48},{48,56},{56,64},{64,7... | collective-permute-start | bytes 61448 | tf_op jit(solution)/shard_map/ppermute | solution.py:376
  72.3 1.8 %shard_map.106.old_sums_ref = f32[16,128,128]{2,1,0:T(8,128)S(1)} custom-call(s32[1]{0:T(128)} %bitcast.second_ref, s32[1,2,8]{2,1,0:T(2,128)S(1)} %get-tuple-element.40.counts_ref, f32[16,16,9,8,128]{4,3,2,1,0:T(8,128)S(1)} %get-tuple-element.61.weight_ref, f32[5,8,128]{2,1,0:T(8,128)S(1)} %bitcast.33), custom_call_target="tpu_custom_call" | custom-call | tf_op jit(solution)/shard_map/pallas_call | solution.py:437
  74.1 0.0 collective-permute-done.10
  74.1 0.0 collective-permute-done.9
  74.2 3.1 %shard_map.107 = (f32[2,8,128]{2,1,0:T(8,128)S(1)}, f32[2,128]{1,0:T(2,128)S(1)}) custom-call(s32[1]{0:T(128)} %bitcast.second_ref, s32[1,2,8]{2,1,0:T(2,128)S(1)} %get-tuple-element.40.counts_ref, f32[16,16,9,8,128]{4,3,2,1,0:T(8,128)S(1)} %get-tuple-element.52.weight_a, f32[16,16,9,8,128]{4,3,2,1,0:T(8,128)S(1)} %get-tuple-element.53.weight_c, ...), custom_call_target="tpu_custom_call" | custom-call | tf_op jit(solution)/shard_map/pallas_call | solution.py:440
  77.2 2.6 %collective-permute-start.11 = (f32[2,128]{1,0:T(2,128)S(1)}, f32[2,128]{1,0:T(2,128)S(1)}, u32[]{:S(2)}, u32[]{:S(2)}) collective-permute-start(f32[2,128]{1,0:T(2,128)S(1)} %get-tuple-element.63.mine_ref), channel_id=1, source_target_pairs={{0,1},{1,0},{2,3},{3,2},{4,5},{5,4},{6,7},{7,6},{8,9},{9,8},{10,11... | collective-permute-start | bytes 3080 | tf_op jit(solution)/shard_map/ppermute | solution.py:380
  79.8 0.8 collective-permute-done.11.theirs_ref
  80.7 22.4 %all_to_all.20 = f32[128,2,128]{2,1,0:T(2,128)S(1)} all-to-all(f32[128,2,128]{2,1,0:T(2,128)S(1)} %shard_map.108), channel_id=1, replica_groups=mesh['gx'=32,'gy'=4,'gz'=2] {'gx','gy'}, dimensions={0} | all-to-all | bytes 262144 | tf_op jit(solution)/shard_map/all_to_all | solution.py:383
  103.1 0.7 shard_map.109
  103.8 2.3 %collective-permute-start.12 = (f32[1,2,128]{2,1,0:T(2,128)S(1)}, f32[1,2,128]{2,1,0:T(2,128)S(1)}, u32[]{:S(2)}, u32[]{:S(2)}) collective-permute-start(f32[1,2,128]{2,1,0:T(2,128)S(1)} %shard_map.110), channel_id=1, source_target_pairs={{0,1},{1,0},{2,3},{3,2},{4,5},{5,4},{6,7},{7,6},{8,9},{9,8},{10,11... | collective-permute-start | bytes 3080 | tf_op jit(solution)/shard_map/ppermute | solution.py:366
  106.2 0.8 collective-permute-done.12.across_ref
  107.0 2.0 %collective-permute-start.13 = (f32[1,2,8,128]{3,2,1,0:T(8,128)S(1)}, f32[1,2,8,128]{3,2,1,0:T(8,128)S(1)}, u32[]{:S(2)}, u32[]{:S(2)}) collective-permute-start(f32[1,2,8,128]{3,2,1,0:T(8,128)S(1)} %get-tuple-element.66), channel_id=1, source_target_pairs={{0,2},{2,4},{4,6},{1,3},{3,5},{5,7},{8,10},{10,12},{12,14},{9,11},... | collective-permute-start | bytes 24584 | tf_op jit(solution)/shard_map/ppermute | solution.py:370
  109.0 1.3 collective-permute-start.14
  110.3 0.0 collective-permute-done.13.below_ref
  110.3 3.1 %collective-permute-done.14.above_ref = f32[1,2,8,128]{3,2,1,0:T(8,128)S(1)} collective-permute-done((f32[1,2,8,128]{3,2,1,0:T(8,128)S(1)}, f32[1,2,8,128]{3,2,1,0:T(8,128)S(1)}, u32[]{:S(2)}, u32[]{:S(2)}) %collective-permute-start.14) | collective-permute-done | bytes 8224 | tf_op jit(solution)/shard_map/ppermute | solution.py:371
  113.4 1.3 collective-permute-start.16
  114.6 4.0 %collective-permute-start.15 = (f32[1,5,8,128]{3,2,1,0:T(8,128)S(1)}, f32[1,5,8,128]{3,2,1,0:T(8,128)S(1)}, u32[]{:S(2)}, u32[]{:S(2)}) collective-permute-start(f32[1,5,8,128]{3,2,1,0:T(8,128)S(1)} %shard_map.112), channel_id=1, source_target_pairs={{0,8},{8,16},{16,24},{24,32},{32,40},{40,48},{48,56},{56,64},{64,7... | collective-permute-start | bytes 61448 | tf_op jit(solution)/shard_map/ppermute | solution.py:376
  118.6 1.8 %shard_map.113.old_sums_ref = f32[16,128,128]{2,1,0:T(8,128)S(1)} custom-call(s32[1]{0:T(128)} %bitcast.second_ref, s32[1,2,8]{2,1,0:T(2,128)S(1)} %get-tuple-element.40.counts_ref, f32[16,16,9,8,128]{4,3,2,1,0:T(8,128)S(1)} %get-tuple-element.61.weight_ref, f32[5,8,128]{2,1,0:T(8,128)S(1)} %bitcast.34), custom_call_target="tpu_custom_call" | custom-call | tf_op jit(solution)/shard_map/pallas_call | solution.py:437
  120.4 0.0 collective-permute-done.16
  120.4 0.0 collective-permute-done.15
  120.5 3.1 %shard_map.114 = (f32[2,8,128]{2,1,0:T(8,128)S(1)}, f32[2,128]{1,0:T(2,128)S(1)}) custom-call(s32[1]{0:T(128)} %bitcast.second_ref, s32[1,2,8]{2,1,0:T(2,128)S(1)} %get-tuple-element.40.counts_ref, f32[16,16,9,8,128]{4,3,2,1,0:T(8,128)S(1)} %get-tuple-element.52.weight_a, f32[16,16,9,8,128]{4,3,2,1,0:T(8,128)S(1)} %get-tuple-element.53.weight_c, ...), custom_call_target="tpu_custom_call" | custom-call | tf_op jit(solution)/shard_map/pallas_call | solution.py:440
  123.5 2.6 %collective-permute-start.17 = (f32[2,128]{1,0:T(2,128)S(1)}, f32[2,128]{1,0:T(2,128)S(1)}, u32[]{:S(2)}, u32[]{:S(2)}) collective-permute-start(f32[2,128]{1,0:T(2,128)S(1)} %get-tuple-element.69.mine_ref), channel_id=1, source_target_pairs={{0,1},{1,0},{2,3},{3,2},{4,5},{5,4},{6,7},{7,6},{8,9},{9,8},{10,11... | collective-permute-start | bytes 3080 | tf_op jit(solution)/shard_map/ppermute | solution.py:380
  126.1 0.8 collective-permute-done.17.theirs_ref
  127.0 20.7 %all_to_all.21 = f32[128,2,128]{2,1,0:T(2,128)S(1)} all-to-all(f32[128,2,128]{2,1,0:T(2,128)S(1)} %shard_map.115), channel_id=1, replica_groups=mesh['gx'=32,'gy'=4,'gz'=2] {'gx','gy'}, dimensions={0} | all-to-all | bytes 262144 | tf_op jit(solution)/shard_map/all_to_all | solution.py:383
  147.7 1.3 shard_map.116
  149.0 2.0 %collective-permute-start.18 = (f32[1,128]{1,0:T(1,128)S(1)}, f32[1,128]{1,0:T(1,128)S(1)}, u32[]{:S(2)}, u32[]{:S(2)}) collective-permute-start(f32[1,128]{1,0:T(1,128)S(1)} %get-tuple-element.74.mine_ref), channel_id=1, source_target_pairs={{0,1},{1,0},{2,3},{3,2},{4,5},{5,4},{6,7},{7,6},{8,9},{9,8},{10,11... | collective-permute-start | bytes 1544 | tf_op jit(solution)/shard_map/ppermute | solution.py:380
  151.0 0.8 collective-permute-done.18.theirs_ref
  151.9 16.1 %all_to_all.22 = f32[128,1,128]{2,1,0:T(1,128)S(1)} all-to-all(f32[128,1,128]{2,1,0:T(1,128)S(1)} %shard_map.117), channel_id=1, replica_groups=mesh['gx'=32,'gy'=4,'gz'=2] {'gx','gy'}, dimensions={0} | all-to-all | bytes 131072 | tf_op jit(solution)/shard_map/all_to_all | solution.py:383
  168.0 0.8 shard_map.118
  (12 shorter events, 0.2 us)
Async XLA Ops:
  2.1 4.1 %collective-permute-start.3 = (f32[1,128]{1,0:T(1,128)S(1)}, f32[1,128]{1,0:T(1,128)S(1)}, u32[]{:S(2)}, u32[]{:S(2)}) collective-permute-start(f32[1,128]{1,0:T(1,128)S(1)} %get-tuple-element.44.mine_ref), channel_id=1, source_target_pairs={{0,1},{1,0},{2,3},{3,2},{4,5},{5,4},{6,7},{7,6},{8,9},{9,8},{10,11... | collective-permute-start | bytes 1544 | tf_op jit(solution)/shard_map/ppermute | solution.py:380
  6.9 24.4 %all-to-all-start = ((f32[128,1,128]{2,1,0:T(1,128)}), f32[128,1,128]{2,1,0:T(1,128)S(1)}, u32[]{:S(2)}, u32[]{:S(2)}) async-start(f32[128,1,128]{2,1,0:T(1,128)} %shard_map.97), calls=%async_computation | async-start | bytes 131072 | tf_op jit(solution)/shard_map/all_to_all | solution.py:383
  20.7 1.5 collective-permute-start
  22.2 10.4 %collective-permute-start.1 = (f32[4,2,8,128]{3,2,1,0:T(8,128)S(1)}, f32[4,2,8,128]{3,2,1,0:T(8,128)S(1)}, u32[]{:S(2)}, u32[]{:S(2)}) collective-permute-start(f32[4,2,8,128]{3,2,1,0:T(8,128)S(1)} %get-tuple-element.42), channel_id=1, source_target_pairs={{0,2},{2,4},{4,6},{1,3},{3,5},{5,7},{8,10},{10,12},{12,14},{9,11},... | collective-permute-start | bytes 98312 | tf_op jit(solution)/shard_map/ppermute | solution.py:370
  25.0 7.6 %collective-permute-start.2 = (f32[4,2,8,128]{3,2,1,0:T(8,128)S(1)}, f32[4,2,8,128]{3,2,1,0:T(8,128)S(1)}, u32[]{:S(2)}, u32[]{:S(2)}) collective-permute-start(f32[4,2,8,128]{3,2,1,0:T(8,128)S(1)} %get-tuple-element.43), channel_id=1, source_target_pairs={{2,0},{4,2},{6,4},{3,1},{5,3},{7,5},{10,8},{12,10},{14,12},{11,9},... | collective-permute-start | bytes 98312 | tf_op jit(solution)/shard_map/ppermute | solution.py:371
  32.6 11.5 %collective-permute-start.5 = (f32[4,5,8,128]{3,2,1,0:T(8,128)S(1)}, f32[4,5,8,128]{3,2,1,0:T(8,128)S(1)}, u32[]{:S(2)}, u32[]{:S(2)}) collective-permute-start(f32[4,5,8,128]{3,2,1,0:T(8,128)S(1)} %shard_map.99.block_ref), channel_id=1, source_target_pairs={{8,0},{16,8},{24,16},{32,24},{40,32},{48,40},{56,48},{64,56},{72,6... | collective-permute-start | bytes 245768 | tf_op jit(solution)/shard_map/ppermute | solution.py:376
  33.9 10.3 %collective-permute-start.4 = (f32[4,5,8,128]{3,2,1,0:T(8,128)S(1)}, f32[4,5,8,128]{3,2,1,0:T(8,128)S(1)}, u32[]{:S(2)}, u32[]{:S(2)}) collective-permute-start(f32[4,5,8,128]{3,2,1,0:T(8,128)S(1)} %shard_map.99.block_ref), channel_id=1, source_target_pairs={{0,8},{8,16},{16,24},{24,32},{32,40},{40,48},{48,56},{56,64},{64,7... | collective-permute-start | bytes 245768 | tf_op jit(solution)/shard_map/ppermute | solution.py:376
  56.3 3.8 %collective-permute-start.6 = (f32[1,2,128]{2,1,0:T(2,128)S(1)}, f32[1,2,128]{2,1,0:T(2,128)S(1)}, u32[]{:S(2)}, u32[]{:S(2)}) collective-permute-start(f32[1,2,128]{2,1,0:T(2,128)S(1)} %shard_map.103), channel_id=1, source_target_pairs={{0,1},{1,0},{2,3},{3,2},{4,5},{5,4},{6,7},{7,6},{8,9},{9,8},{10,11... | collective-permute-start | bytes 3080 | tf_op jit(solution)/shard_map/ppermute | solution.py:366
  60.1 3.9 %collective-permute-start.7 = (f32[1,2,8,128]{3,2,1,0:T(8,128)S(1)}, f32[1,2,8,128]{3,2,1,0:T(8,128)S(1)}, u32[]{:S(2)}, u32[]{:S(2)}) collective-permute-start(f32[1,2,8,128]{3,2,1,0:T(8,128)S(1)} %get-tuple-element.59), channel_id=1, source_target_pairs={{0,2},{2,4},{4,6},{1,3},{3,5},{5,7},{8,10},{10,12},{12,14},{9,11},... | collective-permute-start | bytes 24584 | tf_op jit(solution)/shard_map/ppermute | solution.py:370
  62.7 4.4 %collective-permute-start.8 = (f32[1,2,8,128]{3,2,1,0:T(8,128)S(1)}, f32[1,2,8,128]{3,2,1,0:T(8,128)S(1)}, u32[]{:S(2)}, u32[]{:S(2)}) collective-permute-start(f32[1,2,8,128]{3,2,1,0:T(8,128)S(1)} %get-tuple-element.60), channel_id=1, source_target_pairs={{2,0},{4,2},{6,4},{3,1},{5,3},{7,5},{10,8},{12,10},{14,12},{11,9},... | collective-permute-start | bytes 24584 | tf_op jit(solution)/shard_map/ppermute | solution.py:371
  67.1 7.1 %collective-permute-start.10 = (f32[1,5,8,128]{3,2,1,0:T(8,128)S(1)}, f32[1,5,8,128]{3,2,1,0:T(8,128)S(1)}, u32[]{:S(2)}, u32[]{:S(2)}) collective-permute-start(f32[1,5,8,128]{3,2,1,0:T(8,128)S(1)} %shard_map.105), channel_id=1, source_target_pairs={{8,0},{16,8},{24,16},{32,24},{40,32},{48,40},{56,48},{64,56},{72,6... | collective-permute-start | bytes 61448 | tf_op jit(solution)/shard_map/ppermute | solution.py:376
  68.3 5.8 %collective-permute-start.9 = (f32[1,5,8,128]{3,2,1,0:T(8,128)S(1)}, f32[1,5,8,128]{3,2,1,0:T(8,128)S(1)}, u32[]{:S(2)}, u32[]{:S(2)}) collective-permute-start(f32[1,5,8,128]{3,2,1,0:T(8,128)S(1)} %shard_map.105), channel_id=1, source_target_pairs={{0,8},{8,16},{16,24},{24,32},{32,40},{40,48},{48,56},{56,64},{64,7... | collective-permute-start | bytes 61448 | tf_op jit(solution)/shard_map/ppermute | solution.py:376
  77.2 3.4 %collective-permute-start.11 = (f32[2,128]{1,0:T(2,128)S(1)}, f32[2,128]{1,0:T(2,128)S(1)}, u32[]{:S(2)}, u32[]{:S(2)}) collective-permute-start(f32[2,128]{1,0:T(2,128)S(1)} %get-tuple-element.63.mine_ref), channel_id=1, source_target_pairs={{0,1},{1,0},{2,3},{3,2},{4,5},{5,4},{6,7},{7,6},{8,9},{9,8},{10,11... | collective-permute-start | bytes 3080 | tf_op jit(solution)/shard_map/ppermute | solution.py:380
  103.8 3.1 %collective-permute-start.12 = (f32[1,2,128]{2,1,0:T(2,128)S(1)}, f32[1,2,128]{2,1,0:T(2,128)S(1)}, u32[]{:S(2)}, u32[]{:S(2)}) collective-permute-start(f32[1,2,128]{2,1,0:T(2,128)S(1)} %shard_map.110), channel_id=1, source_target_pairs={{0,1},{1,0},{2,3},{3,2},{4,5},{5,4},{6,7},{7,6},{8,9},{9,8},{10,11... | collective-permute-start | bytes 3080 | tf_op jit(solution)/shard_map/ppermute | solution.py:366
  107.0 3.3 %collective-permute-start.13 = (f32[1,2,8,128]{3,2,1,0:T(8,128)S(1)}, f32[1,2,8,128]{3,2,1,0:T(8,128)S(1)}, u32[]{:S(2)}, u32[]{:S(2)}) collective-permute-start(f32[1,2,8,128]{3,2,1,0:T(8,128)S(1)} %get-tuple-element.66), channel_id=1, source_target_pairs={{0,2},{2,4},{4,6},{1,3},{3,5},{5,7},{8,10},{10,12},{12,14},{9,11},... | collective-permute-start | bytes 24584 | tf_op jit(solution)/shard_map/ppermute | solution.py:370
  109.0 4.4 %collective-permute-start.14 = (f32[1,2,8,128]{3,2,1,0:T(8,128)S(1)}, f32[1,2,8,128]{3,2,1,0:T(8,128)S(1)}, u32[]{:S(2)}, u32[]{:S(2)}) collective-permute-start(f32[1,2,8,128]{3,2,1,0:T(8,128)S(1)} %get-tuple-element.67), channel_id=1, source_target_pairs={{2,0},{4,2},{6,4},{3,1},{5,3},{7,5},{10,8},{12,10},{14,12},{11,9},... | collective-permute-start | bytes 24584 | tf_op jit(solution)/shard_map/ppermute | solution.py:371
  113.4 7.1 %collective-permute-start.16 = (f32[1,5,8,128]{3,2,1,0:T(8,128)S(1)}, f32[1,5,8,128]{3,2,1,0:T(8,128)S(1)}, u32[]{:S(2)}, u32[]{:S(2)}) collective-permute-start(f32[1,5,8,128]{3,2,1,0:T(8,128)S(1)} %shard_map.112), channel_id=1, source_target_pairs={{8,0},{16,8},{24,16},{32,24},{40,32},{48,40},{56,48},{64,56},{72,6... | collective-permute-start | bytes 61448 | tf_op jit(solution)/shard_map/ppermute | solution.py:376
  114.6 5.8 %collective-permute-start.15 = (f32[1,5,8,128]{3,2,1,0:T(8,128)S(1)}, f32[1,5,8,128]{3,2,1,0:T(8,128)S(1)}, u32[]{:S(2)}, u32[]{:S(2)}) collective-permute-start(f32[1,5,8,128]{3,2,1,0:T(8,128)S(1)} %shard_map.112), channel_id=1, source_target_pairs={{0,8},{8,16},{16,24},{24,32},{32,40},{40,48},{48,56},{56,64},{64,7... | collective-permute-start | bytes 61448 | tf_op jit(solution)/shard_map/ppermute | solution.py:376
  123.5 3.4 %collective-permute-start.17 = (f32[2,128]{1,0:T(2,128)S(1)}, f32[2,128]{1,0:T(2,128)S(1)}, u32[]{:S(2)}, u32[]{:S(2)}) collective-permute-start(f32[2,128]{1,0:T(2,128)S(1)} %get-tuple-element.69.mine_ref), channel_id=1, source_target_pairs={{0,1},{1,0},{2,3},{3,2},{4,5},{5,4},{6,7},{7,6},{8,9},{9,8},{10,11... | collective-permute-start | bytes 3080 | tf_op jit(solution)/shard_map/ppermute | solution.py:380
  149.0 2.9 %collective-permute-start.18 = (f32[1,128]{1,0:T(1,128)S(1)}, f32[1,128]{1,0:T(1,128)S(1)}, u32[]{:S(2)}, u32[]{:S(2)}) collective-permute-start(f32[1,128]{1,0:T(1,128)S(1)} %get-tuple-element.74.mine_ref), channel_id=1, source_target_pairs={{0,1},{1,0},{2,3},{3,2},{4,5},{5,4},{6,7},{7,6},{8,9},{9,8},{10,11... | collective-permute-start | bytes 1544 | tf_op jit(solution)/shard_map/ppermute | solution.py:380

commit v4 on v3

--- a/solution.py
+++ b/solution.py
@@ -7,6 +7,7 @@
 
 SLOTS = 128
 FAR = 1000.0
+GX, GY = 32, 4
 LIMIT = 4 * 2**20
 
 VM = pl.BlockSpec(memory_space=pltpu.VMEM)
@@ -97,14 +98,18 @@
             ref[f, 1] = jnp.broadcast_to(across_ref[f, y : y + 1, :], (8, SLOTS))
 
 
-def block_kernel(field_ref, across_ref, below_ref, above_ref, block_ref):
-    for f in range(field_ref.shape[0]):
-        block_ref[f, 0] = below_ref[f, 0]
+def block_kernel(spot_ref, field_ref, across_ref, below_ref, above_ref, block_ref):
+    count = field_ref.shape[0]
+    for f in range(count):
+        sides = [below_ref[f, 0], above_ref[f, 0], below_ref[f, 1, 0:1], above_ref[f, 1, 0:1]]
+        if f == 3:
+            inside = (spot_ref[0] > 0, spot_ref[0] < GY - 1)
+            sides = [jnp.where(inside[at % 2], rows, 0.0) for at, rows in enumerate(sides)]
+        block_ref[f, 0] = sides[0]
         block_ref[f, 1] = field_ref[f, 0]
         block_ref[f, 2] = field_ref[f, 1]
-        block_ref[f, 3] = above_ref[f, 0]
-        rows = (below_ref[f, 1, 0:1], across_ref[f, 0:1], across_ref[f, 1:2], above_ref[f, 1, 0:1])
-        for y, row in enumerate(rows):
+        block_ref[f, 3] = sides[1]
+        for y, row in enumerate((sides[2], across_ref[f, 0:1], across_ref[f, 1:2], sides[3])):
             block_ref[f, 4, y : y + 1, :] = row
 
 
@@ -113,12 +118,16 @@
     spread_ref[...] = jnp.broadcast_to(rows[None], spread_ref.shape)
 
 
-def finish_kernel(gathered_ref, smoothed_ref, direction_ref, out_ref):
+def finish_kernel(
+    gathered_ref, smoothed_ref, direction_ref, pressure_ref, residual_ref, pressure_out, residual_out, out_ref
+):
     rows = gathered_ref[...]
     lane = lax.broadcasted_iota(jnp.int32, rows.shape, 1)
     inner = jnp.sum(jnp.where(lane == 0, rows, 0.0))
     before = jnp.sum(jnp.where(lane == 1, rows, 0.0))
     out_ref[...] = smoothed_ref[...] + inner / before * direction_ref[...]
+    pressure_out[...] = pressure_ref[...]
+    residual_out[...] = residual_ref[...]
 
 
 def assemble(block, second, put):
@@ -131,11 +140,13 @@
         put(y, 9, jnp.where(second == 0, row, 0.0))
 
 
-def place_geometry(near_ref, slab, x, block_ref, second):
+def place_geometry(near_ref, slab, x, block_ref, second, inside=None):
     for f in range(4):
         def put(y, z, row, f=f):
             if f < 3:
                 row = row + float((x, y, z)[f])
+            elif inside is not None:
+                row = jnp.where(inside, row, 0.0)
             near_ref[f, slab, y, z] = jnp.broadcast_to(row, (8, SLOTS))
 
         assemble(lambda at: block_ref[f, at], second, put)
@@ -221,12 +232,12 @@
 
 
 def outer_weights_kernel(
-    second_ref, counts_ref, before_ref, after_ref, old_sums_ref, mine_ref, live_ref, dirichlet_ref, coarse_hbm,
+    second_ref, spot_ref, counts_ref, before_ref, after_ref, old_sums_ref, mine_ref, live_ref, dirichlet_ref, coarse_hbm,
     weight_a, weight_c, diagonal_ref, inverse_ref, coarse_ref, near_ref, sums_ref, sems,
 ):
     copies = fetch(((coarse_hbm, coarse_ref),), sems)
-    place_geometry(near_ref, 0, 0, before_ref, second_ref[0])
-    place_geometry(near_ref, 1, 2, after_ref, second_ref[0])
+    place_geometry(near_ref, 0, 0, before_ref, second_ref[0], spot_ref[0] > 0)
+    place_geometry(near_ref, 1, 2, after_ref, second_ref[0], spot_ref[0] < GX - 1)
     weigh(counts_ref, near_ref, mine_ref, (weight_a, weight_c), old_sums_ref, sums_ref)
     row_sums(sums_ref, diagonal_ref)
     live = live_ref[...]
@@ -307,23 +318,32 @@
 def apply_weights(counts_ref, near_ref, weight_refs, old_sums_ref, sums_ref):
     def one_cell(y, z):
         cell = y * 8 + z
-
-        def two_groups(pair, _):
-            spots = [pl.ds(pl.multiple_of((pair * 2 + g) * 8, 8), 8) for g in range(2)]
-            parts = [[jnp.zeros((8, SLOTS), jnp.float32) for _ in range(3)] for _ in range(2)]
+        groups = (counts_ref[0, y, z] + 7) >> 3
+
+        def some_groups(first, count):
+            spots = [pl.ds(pl.multiple_of((first + g) * 8, 8), 8) for g in range(count)]
+            parts = [[jnp.zeros((8, SLOTS), jnp.float32) for _ in range(3)] for _ in range(count)]
             if old_sums_ref is not None:
-                for g in range(2):
+                for g in range(count):
                     parts[g][0] = old_sums_ref[cell, spots[g], :]
             for slab, weight_ref in enumerate(weight_refs):
                 for at in range(9):
                     near = near_ref[slab, y + at // 3, z + at % 3]
-                    for g in range(2):
-                        parts[g][at % 3] = parts[g][at % 3] + weight_ref[cell, pair * 2 + g, at] * near
-            for g in range(2):
+                    for g in range(count):
+                        parts[g][at % 3] = parts[g][at % 3] + weight_ref[cell, first + g, at] * near
+            for g in range(count):
                 sums_ref[cell, spots[g], :] = parts[g][0] + parts[g][1] + parts[g][2]
+
+        def four_groups(quad, _):
+            some_groups(quad * 4, 4)
             return 0
 
-        lax.fori_loop(0, (counts_ref[0, y, z] + 15) >> 4, two_groups, 0)
+        def two_groups(pair, _):
+            some_groups((groups >> 2) * 4 + pair * 2, 2)
+            return 0
+
+        lax.fori_loop(0, groups >> 2, four_groups, 0)
+        lax.fori_loop(0, ((groups & 3) + 1) >> 1, two_groups, 0)
 
     each_cell(one_cell)
 
@@ -354,26 +374,24 @@
     payload_ref[1:2, :] = inner_row(pairs)
 
 
-def steps(axis):
+def turns(axis):
     size = lax.axis_size(axis)
-    up = [(i, i + 1) for i in range(size - 1)]
+    up = [(i, (i + 1) % size) for i in range(size)]
     return up, [(j, i) for i, j in up]
 
 
-def around(field, second, meanwhile=None):
+def around(field, second, gy_spot):
     count = field.shape[0]
     face = call(top_face_kernel, f32(count, 2, SLOTS), [SM, VM])(second, field)
     across = lax.ppermute(face, "gz", [(0, 1), (1, 0)])
     side = f32(count, 2, 8, SLOTS)
     upper, lower = call(side_faces_kernel, (side, side), [VM] * 2)(field, across)
-    up, down = steps("gy")
+    up, down = turns("gy")
     below = lax.ppermute(upper, "gy", up)
     above = lax.ppermute(lower, "gy", down)
-    if meanwhile is not None:
-        below, above, meanwhile = lax.optimization_barrier((below, above, meanwhile))
-    block = call(block_kernel, f32(count, 5, 8, SLOTS), [VM] * 4)(field, across, below, above)
-    up, down = steps("gx")
-    return block, lax.ppermute(block, "gx", up), lax.ppermute(block, "gx", down), meanwhile
+    block = call(block_kernel, f32(count, 5, 8, SLOTS), [SM] + [VM] * 4)(gy_spot, field, across, below, above)
+    up, down = turns("gx")
+    return block, lax.ppermute(block, "gx", up), lax.ppermute(block, "gx", down)
 
 
 def gather(payload):
@@ -387,6 +405,7 @@
 def per_device(offsets, counts, correction, dirichlet, right_side, deflation, coarse_inverse):
     second = lax.axis_index("gz").astype(jnp.int32)
     second = second.reshape(1)
+    gx_spot, gy_spot = (lax.axis_index(axis).astype(jnp.int32).reshape(1) for axis in ("gx", "gy"))
     block = lambda x: x.reshape(2, 8, SLOTS)
     offsets = offsets.reshape(3, 2, 8, SLOTS)
     dirichlet, right_side, correction = block(dirichlet), block(right_side), block(correction)
@@ -412,9 +431,9 @@
     )(second, *map(outside, (counts, offsets, correction, right_side, dirichlet, basis)))
     counts, dirichlet, basis = onchip(counts), onchip(dirichlet), onchip(basis)
     coefficient = gather(payload)
-    coefficient, centre = lax.optimization_barrier((coefficient, geometry))
+    block, before, after = around(geometry, second, gy_spot)
+    coefficient, block, centre = lax.optimization_barrier((coefficient, block, geometry))
     mine = call(centre_kernel, f32(16, 4, SLOTS, SLOTS), [VM])(centre)
-    block, before, after, mine = around(geometry, second, mine)
 
     sums_shape = f32(16, SLOTS, SLOTS)
     weight_shape = vmem(16, 16, 9, 8, SLOTS)
@@ -427,13 +446,13 @@
     weight_a, weight_c, diagonal, inverse, coarse = call(
         outer_weights_kernel,
         (weight_shape, weight_shape, cells, cells, vmem(64, 128 * SLOTS)),
-        [SM, SM] + [VM] * 6 + [ANY],
+        [SM, SM, SM] + [VM] * 6 + [ANY],
         [vmem(4, 2, 4, 10, 8, SLOTS), vmem(16, SLOTS, SLOTS), pltpu.SemaphoreType.DMA((1,))],
-    )(second, counts, before, after, sums, mine, live, dirichlet, outside(coarse_inverse))
+    )(second, gx_spot, counts, before, after, sums, mine, live, dirichlet, outside(coarse_inverse))
     weight_a, weight_b, weight_c, coarse = map(onchip, (weight_a, weight_b, weight_c, coarse))
 
     def image_of(field, residual, *olds):
-        block, before, after = (piece[0] for piece in around(field[None], second)[:3])
+        block, before, after = (piece[0] for piece in around(field[None], second, gy_spot))
         sums = call(middle_image_kernel, sums_shape, [SM, SM] + [VM] * 2, [vmem(1, 4, 10, 8, SLOTS)])(
             second, counts, weight_b, block
         )
@@ -459,14 +478,16 @@
     gathered = gather(payload)
     pressure, residual, third_smoothed, direction, payload = call(
         third_smooth_kernel,
-        (cells, cells, cells, cells, f32(1, SLOTS)),
+        (vmem(2, 8, SLOTS), vmem(2, 8, SLOTS), cells, cells, f32(1, SLOTS)),
         [VM] * 12,
         [pltpu.VMEM((128, SLOTS), jnp.float32), part],
     )(
         gathered, gathered_first, coefficient, coarse, basis, live, residual, inverse,
         smoothed, image, second_smoothed, second_image,
     )
-    direction = call(finish_kernel, cells, [VM] * 3)(gather(payload), third_smoothed, direction)
+    pressure, residual, direction = call(finish_kernel, (cells, cells, cells), [VM] * 5)(
+        gather(payload), third_smoothed, direction, onchip(pressure), onchip(residual)
+    )
     shape = (1, 2, 8, SLOTS)
     return pressure.reshape(shape), residual.reshape(shape), direction.reshape(shape)
 

time: 170 us -> 152 us (0.89)
  starting transfers between devices: 57.3 us -> 49 us
  blocking collectives: 59.2 us -> 51.4 us
    ppermute x3, starting transfers between devices: 12 us -> 0.76 us  [around(): lax.ppermute(block, 'gx', up)]
    all_to_all x3, blocking collectives: 59.2 us -> 51.4 us  [gather(): got = lax.all_to_all(spread, ('gx', 'gy'), 0, 0, tiled=True)]
    ppermute x3, waiting for transfers between devices: 0.01 us -> 7.78 us  [around(): lax.ppermute(block, 'gx', up)]
    ppermute x3, starting transfers between devices: 3.85 us -> 10.5 us  [around(): lax.ppermute(block, 'gx', down)]
    ppermute x3, waiting for transfers between devices: 6.17 us -> 0.01 us  [around(): above = lax.ppermute(lower, 'gy', down)]
    ppermute x3, starting transfers between devices: 7.28 us -> 2.07 us  [around(): below = lax.ppermute(upper, 'gy', up)]
    all_to_all x1, waiting for transfers between devices: 4.99 us -> 0.01 us  [gather(): got = lax.all_to_all(spread, ('gx', 'gy'), 0, 0, tiled=True)]
    ppermute x3, waiting for transfers between devices: 0.01 us -> 3.68 us  [around(): below = lax.ppermute(upper, 'gy', up)]
  transfers between devices with their start and end apart: 20 -> 20, of which waited for: 10 -> 12; matrix products, arithmetic and copies ran while one was open for 0% -> 0% of each run, Pallas kernels for 7% -> 7%
where the time goes in v4:
time: 152 us
  blocking collectives  51.4 us (34%)
  starting transfers between devices  49 us (32%)
  Pallas kernels  33.3 us (22%)
  waiting for transfers between devices  17.2 us (11%)
    all_to_all x3, blocking collectives, gather(): got = lax.all_to_all(spread, ('gx', 'gy'), 0, 0, tiled=True)  51.4 us
    all_to_all x1, starting transfers between devices, gather(): got = lax.all_to_all(spread, ('gx', 'gy'), 0, 0, tiled=True)  13.8 us
    pallas_call x1, Pallas kernels, per_device(): call(outer_weights_kernel, (weight_shape, weight_shape, cells, cells, vme...  11.3 us
    ppermute x4, starting transfers between devices, gather(): theirs = lax.ppermute(payload, 'gz', [(0, 1), (1, 0)])  11.1 us
    ppermute x3, starting transfers between devices, around(): lax.ppermute(block, 'gx', down)  10.5 us
    ppermute x3, waiting for transfers between devices, around(): lax.ppermute(block, 'gx', up)  7.78 us
    ppermute x3, starting transfers between devices, around(): above = lax.ppermute(lower, 'gy', down)  7.01 us
    pallas_call x1, Pallas kernels, per_device(): call(middle_weights_kernel, (weight_shape, sums_shape), [SM, SM] + [VM] *...  6.17 us
  transfers between devices with their start and end apart: 20, of which 12 were waited for; matrix products, arithmetic and copies ran while one was open for 0% of the time, Pallas kernels for 7%

profile of v4, /device:TPU:1, one launch (start us, length us, event | category | flops | bytes accessed | tf_op | source)
XLA Modules:
  0.0 151.8 jit_solution(15509393305188471846)
XLA Ops:
  0.6 1.4 shard_map.94
  2.1 3.3 %collective-permute-start.5 = (f32[1,128]{1,0:T(1,128)S(1)}, f32[1,128]{1,0:T(1,128)S(1)}, u32[]{:S(2)}, u32[]{:S(2)}) collective-permute-start(f32[1,128]{1,0:T(1,128)S(1)} %get-tuple-element.45.mine_ref), channel_id=1, source_target_pairs={{0,1},{1,0},{2,3},{3,2},{4,5},{5,4},{6,7},{7,6},{8,9},{9,8},{10,11... | collective-permute-start | bytes 1544 | tf_op jit(solution)/shard_map/ppermute | solution.py:398
  5.4 0.8 collective-permute-done.5.theirs_ref
  6.2 0.7 shard_map.98
  6.9 13.8 %all-to-all-start = ((f32[128,1,128]{2,1,0:T(1,128)}), f32[128,1,128]{2,1,0:T(1,128)S(1)}, u32[]{:S(2)}, u32[]{:S(2)}) async-start(f32[128,1,128]{2,1,0:T(1,128)} %shard_map.98), calls=%async_computation | async-start | bytes 131072 | tf_op jit(solution)/shard_map/all_to_all | solution.py:401
  20.7 0.7 collective-permute-start
  21.4 0.8 collective-permute-done.across_ref
  22.2 0.9 collective-permute-start.1
  23.1 1.8 %collective-permute-start.2 = (f32[4,2,8,128]{3,2,1,0:T(8,128)S(1)}, f32[4,2,8,128]{3,2,1,0:T(8,128)S(1)}, u32[]{:S(2)}, u32[]{:S(2)}) collective-permute-start(f32[4,2,8,128]{3,2,1,0:T(8,128)S(1)} %get-tuple-element.44), channel_id=1, source_target_pairs={{2,0},{4,2},{6,4},{0,6},{3,1},{5,3},{7,5},{1,7},{10,8},{12,10},{14... | collective-permute-start | bytes 98312 | tf_op jit(solution)/shard_map/ppermute | solution.py:391
  24.9 1.6 %collective-permute-done.1.below_ref = f32[4,2,8,128]{3,2,1,0:T(8,128)S(1)} collective-permute-done((f32[4,2,8,128]{3,2,1,0:T(8,128)S(1)}, f32[4,2,8,128]{3,2,1,0:T(8,128)S(1)}, u32[]{:S(2)}, u32[]{:S(2)}) %collective-permute-start.1) | collective-permute-done | bytes 32800 | tf_op jit(solution)/shard_map/ppermute | solution.py:390
  26.5 0.0 collective-permute-done.2.above_ref
  26.5 5.0 %collective-permute-start.4 = (f32[4,5,8,128]{3,2,1,0:T(8,128)S(1)}, f32[4,5,8,128]{3,2,1,0:T(8,128)S(1)}, u32[]{:S(2)}, u32[]{:S(2)}) collective-permute-start(f32[4,5,8,128]{3,2,1,0:T(8,128)S(1)} %shard_map.97.block_ref), channel_id=1, source_target_pairs={{8,0},{16,8},{24,16},{32,24},{40,32},{48,40},{56,48},{64,56},{72,6... | collective-permute-start | bytes 245768 | tf_op jit(solution)/shard_map/ppermute | solution.py:394
  31.6 0.0 collective-permute-start.3
  31.6 0.0 all-to-all-done
  31.6 1.3 shard_map.99.mine_ref
  32.9 6.2 %shard_map.100 = (f32[16,16,9,8,128]{4,3,2,1,0:T(8,128)S(1)}, f32[16,128,128]{2,1,0:T(8,128)S(1)}) custom-call(s32[1]{0:T(128)} %bitcast.second_ref, s32[1,2,8]{2,1,0:T(2,128)S(1)} %get-tuple-element.41.counts_ref, f32[16,4,128,128]{3,2,1,0:T(8,128)S(1)} %shard_map.99.mine_ref, f32[4,5,8,128]{3,2,1,0:T(8,128)S(1)} %shard_map.97.block_ref), custom_call_target="tpu_custom_call" | custom-call | tf_op jit(solution)/shard_map/pallas_call | solution.py:440
  39.1 0.0 collective-permute-done.4.after_ref
  39.1 0.0 collective-permute-done.3.before_ref
  39.1 11.3 %shard_map.101 = (f32[16,16,9,8,128]{4,3,2,1,0:T(8,128)S(1)}, f32[16,16,9,8,128]{4,3,2,1,0:T(8,128)S(1)}, f32[2,8,128]{2,1,0:T(8,128)S(1)}, f32[2,8,128]{2,1,0:T(8,128)S(1)}, f32[64,16384]{1,0:T(8,128)S(1)}) custom-call(s32[1]{0:T(128)} %bitcast.second_ref, s32[1]{0:T(128)} %bitcast.6.spot_ref, s32[1,2,8]{2,1,0:T(2,128)S(1)} %get-tuple-element.41.counts_ref, ...), custom_call_target="tpu_custom_call" | custom-call | tf_op jit(solution)/shard_map/pallas_call | solution.py:446
  50.4 0.6 shard_map.102.own_ref.smoothed_ref.rest_0_.first_ref
  51.1 0.9 collective-permute-start.6
  52.0 0.8 collective-permute-done.6.across_ref
  52.8 1.1 collective-permute-start.7
  53.9 2.6 %collective-permute-start.8 = (f32[1,2,8,128]{3,2,1,0:T(8,128)S(1)}, f32[1,2,8,128]{3,2,1,0:T(8,128)S(1)}, u32[]{:S(2)}, u32[]{:S(2)}) collective-permute-start(f32[1,2,8,128]{3,2,1,0:T(8,128)S(1)} %get-tuple-element.59), channel_id=1, source_target_pairs={{2,0},{4,2},{6,4},{0,6},{3,1},{5,3},{7,5},{1,7},{10,8},{12,10},{14... | collective-permute-start | bytes 24584 | tf_op jit(solution)/shard_map/ppermute | solution.py:391
  56.5 1.0 collective-permute-done.7.below_ref
  57.5 0.0 collective-permute-done.8.above_ref
  57.6 4.8 %collective-permute-start.10 = (f32[1,5,8,128]{3,2,1,0:T(8,128)S(1)}, f32[1,5,8,128]{3,2,1,0:T(8,128)S(1)}, u32[]{:S(2)}, u32[]{:S(2)}) collective-permute-start(f32[1,5,8,128]{3,2,1,0:T(8,128)S(1)} %shard_map.105), channel_id=1, source_target_pairs={{8,0},{16,8},{24,16},{32,24},{40,32},{48,40},{56,48},{64,56},{72,6... | collective-permute-start | bytes 61448 | tf_op jit(solution)/shard_map/ppermute | solution.py:394
  62.4 0.0 collective-permute-start.9
  62.4 1.7 %shard_map.106.old_sums_ref = f32[16,128,128]{2,1,0:T(8,128)S(1)} custom-call(s32[1]{0:T(128)} %bitcast.second_ref, s32[1,2,8]{2,1,0:T(2,128)S(1)} %get-tuple-element.41.counts_ref, f32[16,16,9,8,128]{4,3,2,1,0:T(8,128)S(1)} %get-tuple-element.60.weight_ref, f32[5,8,128]{2,1,0:T(8,128)S(1)} %bitcast.36), custom_call_target="tpu_custom_call" | custom-call | tf_op jit(solution)/shard_map/pallas_call | solution.py:456
  64.0 0.0 collective-permute-done.10
  64.0 4.3 %collective-permute-done.9 = f32[1,5,8,128]{3,2,1,0:T(8,128)S(1)} collective-permute-done((f32[1,5,8,128]{3,2,1,0:T(8,128)S(1)}, f32[1,5,8,128]{3,2,1,0:T(8,128)S(1)}, u32[]{:S(2)}, u32[]{:S(2)}) %collective-permute-start.9) | collective-permute-done | bytes 20512 | tf_op jit(solution)/shard_map/ppermute | solution.py:394
  68.3 2.9 %shard_map.107 = (f32[2,8,128]{2,1,0:T(8,128)S(1)}, f32[2,128]{1,0:T(2,128)S(1)}) custom-call(s32[1]{0:T(128)} %bitcast.second_ref, s32[1,2,8]{2,1,0:T(2,128)S(1)} %get-tuple-element.41.counts_ref, f32[16,16,9,8,128]{4,3,2,1,0:T(8,128)S(1)} %get-tuple-element.51.weight_a, f32[16,16,9,8,128]{4,3,2,1,0:T(8,128)S(1)} %get-tuple-element.52.weight_c, ...), custom_call_target="tpu_custom_call" | custom-call | tf_op jit(solution)/shard_map/pallas_call | solution.py:459
  71.2 2.8 %collective-permute-start.11 = (f32[2,128]{1,0:T(2,128)S(1)}, f32[2,128]{1,0:T(2,128)S(1)}, u32[]{:S(2)}, u32[]{:S(2)}) collective-permute-start(f32[2,128]{1,0:T(2,128)S(1)} %get-tuple-element.62.mine_ref), channel_id=1, source_target_pairs={{0,1},{1,0},{2,3},{3,2},{4,5},{5,4},{6,7},{7,6},{8,9},{9,8},{10,11... | collective-permute-start | bytes 3080 | tf_op jit(solution)/shard_map/ppermute | solution.py:398
  74.0 0.8 collective-permute-done.11.theirs_ref
  74.9 17.3 %all_to_all.20 = f32[128,2,128]{2,1,0:T(2,128)S(1)} all-to-all(f32[128,2,128]{2,1,0:T(2,128)S(1)} %shard_map.108), channel_id=1, replica_groups=mesh['gx'=32,'gy'=4,'gz'=2] {'gx','gy'}, dimensions={0} | all-to-all | bytes 262144 | tf_op jit(solution)/shard_map/all_to_all | solution.py:401
  92.2 0.8 shard_map.109
  93.0 2.1 %collective-permute-start.12 = (f32[1,2,128]{2,1,0:T(2,128)S(1)}, f32[1,2,128]{2,1,0:T(2,128)S(1)}, u32[]{:S(2)}, u32[]{:S(2)}) collective-permute-start(f32[1,2,128]{2,1,0:T(2,128)S(1)} %shard_map.110), channel_id=1, source_target_pairs={{0,1},{1,0},{2,3},{3,2},{4,5},{5,4},{6,7},{7,6},{8,9},{9,8},{10,11... | collective-permute-start | bytes 3080 | tf_op jit(solution)/shard_map/ppermute | solution.py:386
  95.1 0.8 collective-permute-done.12.across_ref
  95.9 0.1 collective-permute-start.13
  96.0 2.6 %collective-permute-start.14 = (f32[1,2,8,128]{3,2,1,0:T(8,128)S(1)}, f32[1,2,8,128]{3,2,1,0:T(8,128)S(1)}, u32[]{:S(2)}, u32[]{:S(2)}) collective-permute-start(f32[1,2,8,128]{3,2,1,0:T(8,128)S(1)} %get-tuple-element.66), channel_id=1, source_target_pairs={{2,0},{4,2},{6,4},{0,6},{3,1},{5,3},{7,5},{1,7},{10,8},{12,10},{14... | collective-permute-start | bytes 24584 | tf_op jit(solution)/shard_map/ppermute | solution.py:391
  98.6 1.0 collective-permute-done.13.below_ref
  99.6 0.0 collective-permute-done.14.above_ref
  99.6 0.7 collective-permute-start.16
  100.4 0.8 collective-permute-start.15
  101.1 1.7 %shard_map.113.old_sums_ref = f32[16,128,128]{2,1,0:T(8,128)S(1)} custom-call(s32[1]{0:T(128)} %bitcast.second_ref, s32[1,2,8]{2,1,0:T(2,128)S(1)} %get-tuple-element.41.counts_ref, f32[16,16,9,8,128]{4,3,2,1,0:T(8,128)S(1)} %get-tuple-element.60.weight_ref, f32[5,8,128]{2,1,0:T(8,128)S(1)} %bitcast.35), custom_call_target="tpu_custom_call" | custom-call | tf_op jit(solution)/shard_map/pallas_call | solution.py:456
  102.8 0.0 collective-permute-done.16
  102.8 3.5 %collective-permute-done.15 = f32[1,5,8,128]{3,2,1,0:T(8,128)S(1)} collective-permute-done((f32[1,5,8,128]{3,2,1,0:T(8,128)S(1)}, f32[1,5,8,128]{3,2,1,0:T(8,128)S(1)}, u32[]{:S(2)}, u32[]{:S(2)}) %collective-permute-start.15) | collective-permute-done | bytes 20512 | tf_op jit(solution)/shard_map/ppermute | solution.py:394
  106.3 2.9 %shard_map.114 = (f32[2,8,128]{2,1,0:T(8,128)S(1)}, f32[2,128]{1,0:T(2,128)S(1)}) custom-call(s32[1]{0:T(128)} %bitcast.second_ref, s32[1,2,8]{2,1,0:T(2,128)S(1)} %get-tuple-element.41.counts_ref, f32[16,16,9,8,128]{4,3,2,1,0:T(8,128)S(1)} %get-tuple-element.51.weight_a, f32[16,16,9,8,128]{4,3,2,1,0:T(8,128)S(1)} %get-tuple-element.52.weight_c, ...), custom_call_target="tpu_custom_call" | custom-call | tf_op jit(solution)/shard_map/pallas_call | solution.py:459
  109.2 2.9 %collective-permute-start.17 = (f32[2,128]{1,0:T(2,128)S(1)}, f32[2,128]{1,0:T(2,128)S(1)}, u32[]{:S(2)}, u32[]{:S(2)}) collective-permute-start(f32[2,128]{1,0:T(2,128)S(1)} %get-tuple-element.68.mine_ref), channel_id=1, source_target_pairs={{0,1},{1,0},{2,3},{3,2},{4,5},{5,4},{6,7},{7,6},{8,9},{9,8},{10,11... | collective-permute-start | bytes 3080 | tf_op jit(solution)/shard_map/ppermute | solution.py:398
  112.1 0.8 collective-permute-done.17.theirs_ref
  113.0 18.0 %all_to_all.21 = f32[128,2,128]{2,1,0:T(2,128)S(1)} all-to-all(f32[128,2,128]{2,1,0:T(2,128)S(1)} %shard_map.115), channel_id=1, replica_groups=mesh['gx'=32,'gy'=4,'gz'=2] {'gx','gy'}, dimensions={0} | all-to-all | bytes 262144 | tf_op jit(solution)/shard_map/all_to_all | solution.py:401
  131.0 0.9 shard_map.116
  132.0 2.1 %collective-permute-start.18 = (f32[1,128]{1,0:T(1,128)S(1)}, f32[1,128]{1,0:T(1,128)S(1)}, u32[]{:S(2)}, u32[]{:S(2)}) collective-permute-start(f32[1,128]{1,0:T(1,128)S(1)} %get-tuple-element.71.mine_ref), channel_id=1, source_target_pairs={{0,1},{1,0},{2,3},{3,2},{4,5},{5,4},{6,7},{7,6},{8,9},{9,8},{10,11... | collective-permute-start | bytes 1544 | tf_op jit(solution)/shard_map/ppermute | solution.py:398
  134.1 0.8 collective-permute-done.18.theirs_ref
  134.9 16.1 %all_to_all.22 = f32[128,1,128]{2,1,0:T(1,128)S(1)} all-to-all(f32[128,1,128]{2,1,0:T(1,128)S(1)} %shard_map.117), channel_id=1, replica_groups=mesh['gx'=32,'gy'=4,'gz'=2] {'gx','gy'}, dimensions={0} | all-to-all | bytes 131072 | tf_op jit(solution)/shard_map/all_to_all | solution.py:401
  151.1 0.8 shard_map.118
  (12 shorter events, 0.2 us)
Async XLA Ops:
  2.1 4.1 %collective-permute-start.5 = (f32[1,128]{1,0:T(1,128)S(1)}, f32[1,128]{1,0:T(1,128)S(1)}, u32[]{:S(2)}, u32[]{:S(2)}) collective-permute-start(f32[1,128]{1,0:T(1,128)S(1)} %get-tuple-element.45.mine_ref), channel_id=1, source_target_pairs={{0,1},{1,0},{2,3},{3,2},{4,5},{5,4},{6,7},{7,6},{8,9},{9,8},{10,11... | collective-permute-start | bytes 1544 | tf_op jit(solution)/shard_map/ppermute | solution.py:398
  6.9 24.7 %all-to-all-start = ((f32[128,1,128]{2,1,0:T(1,128)}), f32[128,1,128]{2,1,0:T(1,128)S(1)}, u32[]{:S(2)}, u32[]{:S(2)}) async-start(f32[128,1,128]{2,1,0:T(1,128)} %shard_map.98), calls=%async_computation | async-start | bytes 131072 | tf_op jit(solution)/shard_map/all_to_all | solution.py:401
  20.7 1.5 %collective-permute-start = (f32[4,2,128]{2,1,0:T(2,128)S(1)}, f32[4,2,128]{2,1,0:T(2,128)S(1)}, u32[]{:S(2)}, u32[]{:S(2)}) collective-permute-start(f32[4,2,128]{2,1,0:T(2,128)S(1)} %shard_map.95), channel_id=1, source_target_pairs={{0,1},{1,0},{2,3},{3,2},{4,5},{5,4},{6,7},{7,6},{8,9},{9,8},{10,11... | collective-permute-start | bytes 12296 | tf_op jit(solution)/shard_map/ppermute | solution.py:386
  22.2 4.3 %collective-permute-start.1 = (f32[4,2,8,128]{3,2,1,0:T(8,128)S(1)}, f32[4,2,8,128]{3,2,1,0:T(8,128)S(1)}, u32[]{:S(2)}, u32[]{:S(2)}) collective-permute-start(f32[4,2,8,128]{3,2,1,0:T(8,128)S(1)} %get-tuple-element.43), channel_id=1, source_target_pairs={{0,2},{2,4},{4,6},{6,0},{1,3},{3,5},{5,7},{7,1},{8,10},{10,12},{12... | collective-permute-start | bytes 98312 | tf_op jit(solution)/shard_map/ppermute | solution.py:390
  23.1 3.4 %collective-permute-start.2 = (f32[4,2,8,128]{3,2,1,0:T(8,128)S(1)}, f32[4,2,8,128]{3,2,1,0:T(8,128)S(1)}, u32[]{:S(2)}, u32[]{:S(2)}) collective-permute-start(f32[4,2,8,128]{3,2,1,0:T(8,128)S(1)} %get-tuple-element.44), channel_id=1, source_target_pairs={{2,0},{4,2},{6,4},{0,6},{3,1},{5,3},{7,5},{1,7},{10,8},{12,10},{14... | collective-permute-start | bytes 98312 | tf_op jit(solution)/shard_map/ppermute | solution.py:391
  26.5 12.5 %collective-permute-start.4 = (f32[4,5,8,128]{3,2,1,0:T(8,128)S(1)}, f32[4,5,8,128]{3,2,1,0:T(8,128)S(1)}, u32[]{:S(2)}, u32[]{:S(2)}) collective-permute-start(f32[4,5,8,128]{3,2,1,0:T(8,128)S(1)} %shard_map.97.block_ref), channel_id=1, source_target_pairs={{8,0},{16,8},{24,16},{32,24},{40,32},{48,40},{56,48},{64,56},{72,6... | collective-permute-start | bytes 245768 | tf_op jit(solution)/shard_map/ppermute | solution.py:394
  31.6 7.5 %collective-permute-start.3 = (f32[4,5,8,128]{3,2,1,0:T(8,128)S(1)}, f32[4,5,8,128]{3,2,1,0:T(8,128)S(1)}, u32[]{:S(2)}, u32[]{:S(2)}) collective-permute-start(f32[4,5,8,128]{3,2,1,0:T(8,128)S(1)} %shard_map.97.block_ref), channel_id=1, source_target_pairs={{0,8},{8,16},{16,24},{24,32},{32,40},{40,48},{48,56},{56,64},{64,7... | collective-permute-start | bytes 245768 | tf_op jit(solution)/shard_map/ppermute | solution.py:394
  51.1 1.7 %collective-permute-start.6 = (f32[1,2,128]{2,1,0:T(2,128)S(1)}, f32[1,2,128]{2,1,0:T(2,128)S(1)}, u32[]{:S(2)}, u32[]{:S(2)}) collective-permute-start(f32[1,2,128]{2,1,0:T(2,128)S(1)} %shard_map.103), channel_id=1, source_target_pairs={{0,1},{1,0},{2,3},{3,2},{4,5},{5,4},{6,7},{7,6},{8,9},{9,8},{10,11... | collective-permute-start | bytes 3080 | tf_op jit(solution)/shard_map/ppermute | solution.py:386
  52.8 4.8 %collective-permute-start.7 = (f32[1,2,8,128]{3,2,1,0:T(8,128)S(1)}, f32[1,2,8,128]{3,2,1,0:T(8,128)S(1)}, u32[]{:S(2)}, u32[]{:S(2)}) collective-permute-start(f32[1,2,8,128]{3,2,1,0:T(8,128)S(1)} %get-tuple-element.58), channel_id=1, source_target_pairs={{0,2},{2,4},{4,6},{6,0},{1,3},{3,5},{5,7},{7,1},{8,10},{10,12},{12... | collective-permute-start | bytes 24584 | tf_op jit(solution)/shard_map/ppermute | solution.py:390
  53.9 3.6 %collective-permute-start.8 = (f32[1,2,8,128]{3,2,1,0:T(8,128)S(1)}, f32[1,2,8,128]{3,2,1,0:T(8,128)S(1)}, u32[]{:S(2)}, u32[]{:S(2)}) collective-permute-start(f32[1,2,8,128]{3,2,1,0:T(8,128)S(1)} %get-tuple-element.59), channel_id=1, source_target_pairs={{2,0},{4,2},{6,4},{0,6},{3,1},{5,3},{7,5},{1,7},{10,8},{12,10},{14... | collective-permute-start | bytes 24584 | tf_op jit(solution)/shard_map/ppermute | solution.py:391
  57.6 6.5 %collective-permute-start.10 = (f32[1,5,8,128]{3,2,1,0:T(8,128)S(1)}, f32[1,5,8,128]{3,2,1,0:T(8,128)S(1)}, u32[]{:S(2)}, u32[]{:S(2)}) collective-permute-start(f32[1,5,8,128]{3,2,1,0:T(8,128)S(1)} %shard_map.105), channel_id=1, source_target_pairs={{8,0},{16,8},{24,16},{32,24},{40,32},{48,40},{56,48},{64,56},{72,6... | collective-permute-start | bytes 61448 | tf_op jit(solution)/shard_map/ppermute | solution.py:394
  62.4 6.0 %collective-permute-start.9 = (f32[1,5,8,128]{3,2,1,0:T(8,128)S(1)}, f32[1,5,8,128]{3,2,1,0:T(8,128)S(1)}, u32[]{:S(2)}, u32[]{:S(2)}) collective-permute-start(f32[1,5,8,128]{3,2,1,0:T(8,128)S(1)} %shard_map.105), channel_id=1, source_target_pairs={{0,8},{8,16},{16,24},{24,32},{32,40},{40,48},{48,56},{56,64},{64,7... | collective-permute-start | bytes 61448 | tf_op jit(solution)/shard_map/ppermute | solution.py:394
  71.2 3.6 %collective-permute-start.11 = (f32[2,128]{1,0:T(2,128)S(1)}, f32[2,128]{1,0:T(2,128)S(1)}, u32[]{:S(2)}, u32[]{:S(2)}) collective-permute-start(f32[2,128]{1,0:T(2,128)S(1)} %get-tuple-element.62.mine_ref), channel_id=1, source_target_pairs={{0,1},{1,0},{2,3},{3,2},{4,5},{5,4},{6,7},{7,6},{8,9},{9,8},{10,11... | collective-permute-start | bytes 3080 | tf_op jit(solution)/shard_map/ppermute | solution.py:398
  93.0 2.9 %collective-permute-start.12 = (f32[1,2,128]{2,1,0:T(2,128)S(1)}, f32[1,2,128]{2,1,0:T(2,128)S(1)}, u32[]{:S(2)}, u32[]{:S(2)}) collective-permute-start(f32[1,2,128]{2,1,0:T(2,128)S(1)} %shard_map.110), channel_id=1, source_target_pairs={{0,1},{1,0},{2,3},{3,2},{4,5},{5,4},{6,7},{7,6},{8,9},{9,8},{10,11... | collective-permute-start | bytes 3080 | tf_op jit(solution)/shard_map/ppermute | solution.py:386
  95.9 3.7 %collective-permute-start.13 = (f32[1,2,8,128]{3,2,1,0:T(8,128)S(1)}, f32[1,2,8,128]{3,2,1,0:T(8,128)S(1)}, u32[]{:S(2)}, u32[]{:S(2)}) collective-permute-start(f32[1,2,8,128]{3,2,1,0:T(8,128)S(1)} %get-tuple-element.65), channel_id=1, source_target_pairs={{0,2},{2,4},{4,6},{6,0},{1,3},{3,5},{5,7},{7,1},{8,10},{10,12},{12... | collective-permute-start | bytes 24584 | tf_op jit(solution)/shard_map/ppermute | solution.py:390
  96.0 3.6 %collective-permute-start.14 = (f32[1,2,8,128]{3,2,1,0:T(8,128)S(1)}, f32[1,2,8,128]{3,2,1,0:T(8,128)S(1)}, u32[]{:S(2)}, u32[]{:S(2)}) collective-permute-start(f32[1,2,8,128]{3,2,1,0:T(8,128)S(1)} %get-tuple-element.66), channel_id=1, source_target_pairs={{2,0},{4,2},{6,4},{0,6},{3,1},{5,3},{7,5},{1,7},{10,8},{12,10},{14... | collective-permute-start | bytes 24584 | tf_op jit(solution)/shard_map/ppermute | solution.py:391
  99.6 3.1 %collective-permute-start.16 = (f32[1,5,8,128]{3,2,1,0:T(8,128)S(1)}, f32[1,5,8,128]{3,2,1,0:T(8,128)S(1)}, u32[]{:S(2)}, u32[]{:S(2)}) collective-permute-start(f32[1,5,8,128]{3,2,1,0:T(8,128)S(1)} %shard_map.112), channel_id=1, source_target_pairs={{8,0},{16,8},{24,16},{32,24},{40,32},{48,40},{56,48},{64,56},{72,6... | collective-permute-start | bytes 61448 | tf_op jit(solution)/shard_map/ppermute | solution.py:394
  100.4 6.0 %collective-permute-start.15 = (f32[1,5,8,128]{3,2,1,0:T(8,128)S(1)}, f32[1,5,8,128]{3,2,1,0:T(8,128)S(1)}, u32[]{:S(2)}, u32[]{:S(2)}) collective-permute-start(f32[1,5,8,128]{3,2,1,0:T(8,128)S(1)} %shard_map.112), channel_id=1, source_target_pairs={{0,8},{8,16},{16,24},{24,32},{32,40},{40,48},{48,56},{56,64},{64,7... | collective-permute-start | bytes 61448 | tf_op jit(solution)/shard_map/ppermute | solution.py:394
  109.2 3.7 %collective-permute-start.17 = (f32[2,128]{1,0:T(2,128)S(1)}, f32[2,128]{1,0:T(2,128)S(1)}, u32[]{:S(2)}, u32[]{:S(2)}) collective-permute-start(f32[2,128]{1,0:T(2,128)S(1)} %get-tuple-element.68.mine_ref), channel_id=1, source_target_pairs={{0,1},{1,0},{2,3},{3,2},{4,5},{5,4},{6,7},{7,6},{8,9},{9,8},{10,11... | collective-permute-start | bytes 3080 | tf_op jit(solution)/shard_map/ppermute | solution.py:398
  132.0 3.0 %collective-permute-start.18 = (f32[1,128]{1,0:T(1,128)S(1)}, f32[1,128]{1,0:T(1,128)S(1)}, u32[]{:S(2)}, u32[]{:S(2)}) collective-permute-start(f32[1,128]{1,0:T(1,128)S(1)} %get-tuple-element.71.mine_ref), channel_id=1, source_target_pairs={{0,1},{1,0},{2,3},{3,2},{4,5},{5,4},{6,7},{7,6},{8,9},{9,8},{10,11... | collective-permute-start | bytes 1544 | tf_op jit(solution)/shard_map/ppermute | solution.py:398

commit v5 on v4

--- a/solution.py
+++ b/solution.py
@@ -158,17 +158,21 @@
         out_ref[cell // 8, cell % 8 : cell % 8 + 1, :] = jnp.sum(sums_ref[cell].T, axis=0, keepdims=True)
 
 
-def each_cell(one_cell):
-    for y in range(2):
-        def cell_of(z, _, y=y):
-            one_cell(y, z)
+def each_cell(second, one_cell):
+    def plane(y, _):
+        def inner(z, _):
+            one_cell(y, z + 1 - second, 0, 3)
             return 0
 
-        lax.fori_loop(0, 8, cell_of, 0)
-
-
-def weigh(counts_ref, near_ref, mine_ref, weight_refs, old_sums_ref, sums_ref):
-    def one_cell(y, z):
+        lax.fori_loop(0, 7, inner, 0)
+        one_cell(y, second * 7, 1 - second, 2)
+        return 0
+
+    lax.fori_loop(0, 2, plane, 0)
+
+
+def weigh(second, counts_ref, near_ref, mine_ref, weight_refs, old_sums_ref, sums_ref):
+    def one_cell(y, z, layer, layers):
         cell = y * 8 + z
         groups = (counts_ref[0, y, z] + 7) >> 3
 
@@ -180,8 +184,8 @@
             else:
                 totals = [old_sums_ref[cell, spot, :] for spot in spots]
             for slab, weight_ref in enumerate(weight_refs):
-                for at in range(9):
-                    near = [near_ref[f, slab, y + at // 3, z + at % 3] for f in range(4)]
+                for b, c in [(b, layer + c) for b in range(3) for c in range(layers)]:
+                    near = [near_ref[f, slab, y + b, z + c] for f in range(4)]
                     for g in range(count):
                         dx, dy, dz = (near[f] - mine[g][f] for f in range(3))
                         square = dx * dx + dy * dy + dz * dz
@@ -189,7 +193,7 @@
                         fall = jnp.maximum(1.0 - radius, 0.0)
                         weight = (square * fall) * (fall * fall) / (square + 0.01)
                         weight = weight * (near[3] + mine[g][3])
-                        weight_ref[cell, first + g, at] = weight
+                        weight_ref[cell, first + g, b * 3 + c] = weight
                         totals[g] = totals[g] + weight
             for g in range(count):
                 sums_ref[cell, spots[g], :] = totals[g]
@@ -208,7 +212,7 @@
         def _():
             some_groups(groups - 1, 1)
 
-    each_cell(one_cell)
+    each_cell(second, one_cell)
 
 
 def centre_kernel(own_ref, mine_ref):
@@ -228,7 +232,7 @@
 
 def middle_weights_kernel(second_ref, counts_ref, mine_ref, block_ref, weight_ref, sums_ref, near_ref):
     place_geometry(near_ref, 0, 1, block_ref, second_ref[0])
-    weigh(counts_ref, near_ref, mine_ref, (weight_ref,), None, sums_ref)
+    weigh(second_ref[0], counts_ref, near_ref, mine_ref, (weight_ref,), None, sums_ref)
 
 
 def outer_weights_kernel(
@@ -238,7 +242,7 @@
     copies = fetch(((coarse_hbm, coarse_ref),), sems)
     place_geometry(near_ref, 0, 0, before_ref, second_ref[0], spot_ref[0] > 0)
     place_geometry(near_ref, 1, 2, after_ref, second_ref[0], spot_ref[0] < GX - 1)
-    weigh(counts_ref, near_ref, mine_ref, (weight_a, weight_c), old_sums_ref, sums_ref)
+    weigh(second_ref[0], counts_ref, near_ref, mine_ref, (weight_a, weight_c), old_sums_ref, sums_ref)
     row_sums(sums_ref, diagonal_ref)
     live = live_ref[...]
     sums = jnp.where(live == 0.0, 0.0, diagonal_ref[...])
@@ -315,8 +319,8 @@
     assemble(lambda at: block_ref[at], second, put)
 
 
-def apply_weights(counts_ref, near_ref, weight_refs, old_sums_ref, sums_ref):
-    def one_cell(y, z):
+def apply_weights(second, counts_ref, near_ref, weight_refs, old_sums_ref, sums_ref):
+    def one_cell(y, z, layer, layers):
         cell = y * 8 + z
         groups = (counts_ref[0, y, z] + 7) >> 3
 
@@ -327,10 +331,10 @@
                 for g in range(count):
                     parts[g][0] = old_sums_ref[cell, spots[g], :]
             for slab, weight_ref in enumerate(weight_refs):
-                for at in range(9):
-                    near = near_ref[slab, y + at // 3, z + at % 3]
+                for b, c in [(b, layer + c) for b in range(3) for c in range(layers)]:
+                    near = near_ref[slab, y + b, z + c]
                     for g in range(count):
-                        parts[g][at % 3] = parts[g][at % 3] + weight_ref[cell, first + g, at] * near
+                        parts[g][b] = parts[g][b] + weight_ref[cell, first + g, b * 3 + c] * near
             for g in range(count):
                 sums_ref[cell, spots[g], :] = parts[g][0] + parts[g][1] + parts[g][2]
 
@@ -345,12 +349,12 @@
         lax.fori_loop(0, groups >> 2, four_groups, 0)
         lax.fori_loop(0, ((groups & 3) + 1) >> 1, two_groups, 0)
 
-    each_cell(one_cell)
+    each_cell(second, one_cell)
 
 
 def middle_image_kernel(second_ref, counts_ref, weight_ref, block_ref, sums_ref, near_ref):
     place_field(near_ref, 0, block_ref, second_ref[0])
-    apply_weights(counts_ref, near_ref, (weight_ref,), None, sums_ref)
+    apply_weights(second_ref[0], counts_ref, near_ref, (weight_ref,), None, sums_ref)
 
 
 def image_kernel(
@@ -361,7 +365,7 @@
     second = second_ref[0]
     place_field(near_ref, 0, before_ref, second)
     place_field(near_ref, 1, after_ref, second)
-    apply_weights(counts_ref, near_ref, (weight_a, weight_c), old_sums_ref, sums_ref)
+    apply_weights(second_ref[0], counts_ref, near_ref, (weight_a, weight_c), old_sums_ref, sums_ref)
     row_sums(sums_ref, image_ref)
     own = own_ref[...]
     image = jnp.where(live_ref[...] == 0.0, 0.0, diagonal_ref[...] * own - image_ref[...])

time: 152 us -> 152 us (level)
  Pallas kernels: 33.3 us -> 30.7 us
  starting transfers between devices: 49 us -> 51.3 us
    ppermute x3, starting transfers between devices: 3.73 us -> 7.24 us  [around(): across = lax.ppermute(face, 'gz', [(0, 1), (1, 0)])]
    ppermute x3, starting transfers between devices: 10.5 us -> 8.18 us  [around(): lax.ppermute(block, 'gx', down)]
    pallas_call x1, Pallas kernels: 11.3 us -> 9.74 us  [per_device(): call(outer_weights_kernel, (weight_shape, weight_shape, cells, cells, vme...]
where the time goes in v5:
time: 152 us; the launch traced here: 151 us
  blocking collectives  51.4 us (34%)
  starting transfers between devices  51.3 us (34%)
  Pallas kernels  30.7 us (20%)
  waiting for transfers between devices  17.2 us (11%)
    all_to_all x3, blocking collectives, gather(): got = lax.all_to_all(spread, ('gx', 'gy'), 0, 0, tiled=True)  51.4 us
    all_to_all x1, starting transfers between devices, gather(): got = lax.all_to_all(spread, ('gx', 'gy'), 0, 0, tiled=True)  13.8 us
    ppermute x4, starting transfers between devices, gather(): theirs = lax.ppermute(payload, 'gz', [(0, 1), (1, 0)])  11.8 us
    pallas_call x1, Pallas kernels, per_device(): call(outer_weights_kernel, (weight_shape, weight_shape, cells, cells, vme...  9.74 us
    ppermute x3, starting transfers between devices, around(): above = lax.ppermute(lower, 'gy', down)  8.26 us
    ppermute x3, starting transfers between devices, around(): lax.ppermute(block, 'gx', down)  8.18 us
    ppermute x3, waiting for transfers between devices, around(): lax.ppermute(block, 'gx', up)  7.8 us
    ppermute x3, starting transfers between devices, around(): across = lax.ppermute(face, 'gz', [(0, 1), (1, 0)])  7.24 us
  transfers between devices with their start and end apart: 20, of which 12 were waited for; matrix products, arithmetic and copies ran while one was open for 0% of the time, Pallas kernels for 7%

profile of v5, /device:TPU:1, one launch (start us, length us, event | category | flops | bytes accessed | tf_op | source)
XLA Modules:
  0.0 151.5 jit_solution(16742035412844232634)
XLA Ops:
  0.6 1.4 shard_map.94
  2.1 3.3 %collective-permute-start.5 = (f32[1,128]{1,0:T(1,128)S(1)}, f32[1,128]{1,0:T(1,128)S(1)}, u32[]{:S(2)}, u32[]{:S(2)}) collective-permute-start(f32[1,128]{1,0:T(1,128)S(1)} %get-tuple-element.45.mine_ref), channel_id=1, source_target_pairs={{0,1},{1,0},{2,3},{3,2},{4,5},{5,4},{6,7},{7,6},{8,9},{9,8},{10,11... | collective-permute-start | bytes 1544 | tf_op jit(solution)/shard_map/ppermute | solution.py:402
  5.4 0.8 collective-permute-done.5.theirs_ref
  6.2 0.7 shard_map.98
  6.9 13.8 %all-to-all-start = ((f32[128,1,128]{2,1,0:T(1,128)}), f32[128,1,128]{2,1,0:T(1,128)S(1)}, u32[]{:S(2)}, u32[]{:S(2)}) async-start(f32[128,1,128]{2,1,0:T(1,128)} %shard_map.98), calls=%async_computation | async-start | bytes 131072 | tf_op jit(solution)/shard_map/all_to_all | solution.py:405
  20.7 0.7 collective-permute-start
  21.4 0.8 collective-permute-done.across_ref
  22.2 0.9 collective-permute-start.1
  23.1 1.8 %collective-permute-start.2 = (f32[4,2,8,128]{3,2,1,0:T(8,128)S(1)}, f32[4,2,8,128]{3,2,1,0:T(8,128)S(1)}, u32[]{:S(2)}, u32[]{:S(2)}) collective-permute-start(f32[4,2,8,128]{3,2,1,0:T(8,128)S(1)} %get-tuple-element.44), channel_id=1, source_target_pairs={{2,0},{4,2},{6,4},{0,6},{3,1},{5,3},{7,5},{1,7},{10,8},{12,10},{14... | collective-permute-start | bytes 98312 | tf_op jit(solution)/shard_map/ppermute | solution.py:395
  24.9 1.6 %collective-permute-done.1.below_ref = f32[4,2,8,128]{3,2,1,0:T(8,128)S(1)} collective-permute-done((f32[4,2,8,128]{3,2,1,0:T(8,128)S(1)}, f32[4,2,8,128]{3,2,1,0:T(8,128)S(1)}, u32[]{:S(2)}, u32[]{:S(2)}) %collective-permute-start.1) | collective-permute-done | bytes 32800 | tf_op jit(solution)/shard_map/ppermute | solution.py:394
  26.5 0.0 collective-permute-done.2.above_ref
  26.5 5.0 %collective-permute-start.4 = (f32[4,5,8,128]{3,2,1,0:T(8,128)S(1)}, f32[4,5,8,128]{3,2,1,0:T(8,128)S(1)}, u32[]{:S(2)}, u32[]{:S(2)}) collective-permute-start(f32[4,5,8,128]{3,2,1,0:T(8,128)S(1)} %shard_map.97.block_ref), channel_id=1, source_target_pairs={{8,0},{16,8},{24,16},{32,24},{40,32},{48,40},{56,48},{64,56},{72,6... | collective-permute-start | bytes 245768 | tf_op jit(solution)/shard_map/ppermute | solution.py:398
  31.6 0.0 collective-permute-start.3
  31.6 0.0 all-to-all-done
  31.6 1.3 shard_map.99.mine_ref
  32.9 5.4 %shard_map.100 = (f32[16,16,9,8,128]{4,3,2,1,0:T(8,128)S(1)}, f32[16,128,128]{2,1,0:T(8,128)S(1)}) custom-call(s32[1]{0:T(128)} %bitcast.second_ref, s32[1,2,8]{2,1,0:T(2,128)S(1)} %get-tuple-element.41.counts_ref, f32[16,4,128,128]{3,2,1,0:T(8,128)S(1)} %shard_map.99.mine_ref, f32[4,5,8,128]{3,2,1,0:T(8,128)S(1)} %shard_map.97.block_ref), custom_call_target="tpu_custom_call" | custom-call | tf_op jit(solution)/shard_map/pallas_call | solution.py:444
  38.3 0.0 collective-permute-done.4.after_ref
  38.3 0.0 collective-permute-done.3.before_ref
  38.3 9.7 %shard_map.101 = (f32[16,16,9,8,128]{4,3,2,1,0:T(8,128)S(1)}, f32[16,16,9,8,128]{4,3,2,1,0:T(8,128)S(1)}, f32[2,8,128]{2,1,0:T(8,128)S(1)}, f32[2,8,128]{2,1,0:T(8,128)S(1)}, f32[64,16384]{1,0:T(8,128)S(1)}) custom-call(s32[1]{0:T(128)} %bitcast.second_ref, s32[1]{0:T(128)} %bitcast.6.spot_ref, s32[1,2,8]{2,1,0:T(2,128)S(1)} %get-tuple-element.41.counts_ref, ...), custom_call_target="tpu_custom_call" | custom-call | tf_op jit(solution)/shard_map/pallas_call | solution.py:450
  48.1 0.6 shard_map.102.own_ref.smoothed_ref.rest_0_.first_ref
  48.7 4.4 %collective-permute-start.6 = (f32[1,2,128]{2,1,0:T(2,128)S(1)}, f32[1,2,128]{2,1,0:T(2,128)S(1)}, u32[]{:S(2)}, u32[]{:S(2)}) collective-permute-start(f32[1,2,128]{2,1,0:T(2,128)S(1)} %shard_map.103), channel_id=1, source_target_pairs={{0,1},{1,0},{2,3},{3,2},{4,5},{5,4},{6,7},{7,6},{8,9},{9,8},{10,11... | collective-permute-start | bytes 3080 | tf_op jit(solution)/shard_map/ppermute | solution.py:390
  53.1 0.8 collective-permute-done.6.across_ref
  54.0 0.4 collective-permute-start.7
  54.4 3.8 %collective-permute-start.8 = (f32[1,2,8,128]{3,2,1,0:T(8,128)S(1)}, f32[1,2,8,128]{3,2,1,0:T(8,128)S(1)}, u32[]{:S(2)}, u32[]{:S(2)}) collective-permute-start(f32[1,2,8,128]{3,2,1,0:T(8,128)S(1)} %get-tuple-element.59), channel_id=1, source_target_pairs={{2,0},{4,2},{6,4},{0,6},{3,1},{5,3},{7,5},{1,7},{10,8},{12,10},{14... | collective-permute-start | bytes 24584 | tf_op jit(solution)/shard_map/ppermute | solution.py:395
  58.2 1.0 collective-permute-done.7.below_ref
  59.2 0.0 collective-permute-done.8.above_ref
  59.2 2.4 %collective-permute-start.10 = (f32[1,5,8,128]{3,2,1,0:T(8,128)S(1)}, f32[1,5,8,128]{3,2,1,0:T(8,128)S(1)}, u32[]{:S(2)}, u32[]{:S(2)}) collective-permute-start(f32[1,5,8,128]{3,2,1,0:T(8,128)S(1)} %shard_map.105), channel_id=1, source_target_pairs={{8,0},{16,8},{24,16},{32,24},{40,32},{48,40},{56,48},{64,56},{72,6... | collective-permute-start | bytes 61448 | tf_op jit(solution)/shard_map/ppermute | solution.py:398
  61.7 0.0 collective-permute-start.9
  61.7 1.7 %shard_map.106.old_sums_ref = f32[16,128,128]{2,1,0:T(8,128)S(1)} custom-call(s32[1]{0:T(128)} %bitcast.second_ref, s32[1,2,8]{2,1,0:T(2,128)S(1)} %get-tuple-element.41.counts_ref, f32[16,16,9,8,128]{4,3,2,1,0:T(8,128)S(1)} %get-tuple-element.60.weight_ref, f32[5,8,128]{2,1,0:T(8,128)S(1)} %bitcast.36), custom_call_target="tpu_custom_call" | custom-call | tf_op jit(solution)/shard_map/pallas_call | solution.py:460
  63.3 0.0 collective-permute-done.10
  63.4 4.3 %collective-permute-done.9 = f32[1,5,8,128]{3,2,1,0:T(8,128)S(1)} collective-permute-done((f32[1,5,8,128]{3,2,1,0:T(8,128)S(1)}, f32[1,5,8,128]{3,2,1,0:T(8,128)S(1)}, u32[]{:S(2)}, u32[]{:S(2)}) %collective-permute-start.9) | collective-permute-done | bytes 20512 | tf_op jit(solution)/shard_map/ppermute | solution.py:398
  67.6 2.8 %shard_map.107 = (f32[2,8,128]{2,1,0:T(8,128)S(1)}, f32[2,128]{1,0:T(2,128)S(1)}) custom-call(s32[1]{0:T(128)} %bitcast.second_ref, s32[1,2,8]{2,1,0:T(2,128)S(1)} %get-tuple-element.41.counts_ref, f32[16,16,9,8,128]{4,3,2,1,0:T(8,128)S(1)} %get-tuple-element.51.weight_a, f32[16,16,9,8,128]{4,3,2,1,0:T(8,128)S(1)} %get-tuple-element.52.weight_c, ...), custom_call_target="tpu_custom_call" | custom-call | tf_op jit(solution)/shard_map/pallas_call | solution.py:463
  70.4 3.2 %collective-permute-start.11 = (f32[2,128]{1,0:T(2,128)S(1)}, f32[2,128]{1,0:T(2,128)S(1)}, u32[]{:S(2)}, u32[]{:S(2)}) collective-permute-start(f32[2,128]{1,0:T(2,128)S(1)} %get-tuple-element.62.mine_ref), channel_id=1, source_target_pairs={{0,1},{1,0},{2,3},{3,2},{4,5},{5,4},{6,7},{7,6},{8,9},{9,8},{10,11... | collective-permute-start | bytes 3080 | tf_op jit(solution)/shard_map/ppermute | solution.py:402
  73.6 0.8 collective-permute-done.11.theirs_ref
  74.4 17.4 %all_to_all.20 = f32[128,2,128]{2,1,0:T(2,128)S(1)} all-to-all(f32[128,2,128]{2,1,0:T(2,128)S(1)} %shard_map.108), channel_id=1, replica_groups=mesh['gx'=32,'gy'=4,'gz'=2] {'gx','gy'}, dimensions={0} | all-to-all | bytes 262144 | tf_op jit(solution)/shard_map/all_to_all | solution.py:405
  91.8 0.8 shard_map.109
  92.6 2.1 %collective-permute-start.12 = (f32[1,2,128]{2,1,0:T(2,128)S(1)}, f32[1,2,128]{2,1,0:T(2,128)S(1)}, u32[]{:S(2)}, u32[]{:S(2)}) collective-permute-start(f32[1,2,128]{2,1,0:T(2,128)S(1)} %shard_map.110), channel_id=1, source_target_pairs={{0,1},{1,0},{2,3},{3,2},{4,5},{5,4},{6,7},{7,6},{8,9},{9,8},{10,11... | collective-permute-start | bytes 3080 | tf_op jit(solution)/shard_map/ppermute | solution.py:390
  94.8 0.8 collective-permute-done.12.across_ref
  95.6 0.1 collective-permute-start.13
  95.6 2.6 %collective-permute-start.14 = (f32[1,2,8,128]{3,2,1,0:T(8,128)S(1)}, f32[1,2,8,128]{3,2,1,0:T(8,128)S(1)}, u32[]{:S(2)}, u32[]{:S(2)}) collective-permute-start(f32[1,2,8,128]{3,2,1,0:T(8,128)S(1)} %get-tuple-element.66), channel_id=1, source_target_pairs={{2,0},{4,2},{6,4},{0,6},{3,1},{5,3},{7,5},{1,7},{10,8},{12,10},{14... | collective-permute-start | bytes 24584 | tf_op jit(solution)/shard_map/ppermute | solution.py:395
  98.3 1.0 collective-permute-done.13.below_ref
  99.3 0.0 collective-permute-done.14.above_ref
  99.3 0.7 collective-permute-start.16
  100.0 0.8 collective-permute-start.15
  100.8 1.7 %shard_map.113.old_sums_ref = f32[16,128,128]{2,1,0:T(8,128)S(1)} custom-call(s32[1]{0:T(128)} %bitcast.second_ref, s32[1,2,8]{2,1,0:T(2,128)S(1)} %get-tuple-element.41.counts_ref, f32[16,16,9,8,128]{4,3,2,1,0:T(8,128)S(1)} %get-tuple-element.60.weight_ref, f32[5,8,128]{2,1,0:T(8,128)S(1)} %bitcast.35), custom_call_target="tpu_custom_call" | custom-call | tf_op jit(solution)/shard_map/pallas_call | solution.py:460
  102.4 0.0 collective-permute-done.16
  102.4 3.5 %collective-permute-done.15 = f32[1,5,8,128]{3,2,1,0:T(8,128)S(1)} collective-permute-done((f32[1,5,8,128]{3,2,1,0:T(8,128)S(1)}, f32[1,5,8,128]{3,2,1,0:T(8,128)S(1)}, u32[]{:S(2)}, u32[]{:S(2)}) %collective-permute-start.15) | collective-permute-done | bytes 20512 | tf_op jit(solution)/shard_map/ppermute | solution.py:398
  106.0 2.8 %shard_map.114 = (f32[2,8,128]{2,1,0:T(8,128)S(1)}, f32[2,128]{1,0:T(2,128)S(1)}) custom-call(s32[1]{0:T(128)} %bitcast.second_ref, s32[1,2,8]{2,1,0:T(2,128)S(1)} %get-tuple-element.41.counts_ref, f32[16,16,9,8,128]{4,3,2,1,0:T(8,128)S(1)} %get-tuple-element.51.weight_a, f32[16,16,9,8,128]{4,3,2,1,0:T(8,128)S(1)} %get-tuple-element.52.weight_c, ...), custom_call_target="tpu_custom_call" | custom-call | tf_op jit(solution)/shard_map/pallas_call | solution.py:463
  108.7 3.2 %collective-permute-start.17 = (f32[2,128]{1,0:T(2,128)S(1)}, f32[2,128]{1,0:T(2,128)S(1)}, u32[]{:S(2)}, u32[]{:S(2)}) collective-permute-start(f32[2,128]{1,0:T(2,128)S(1)} %get-tuple-element.68.mine_ref), channel_id=1, source_target_pairs={{0,1},{1,0},{2,3},{3,2},{4,5},{5,4},{6,7},{7,6},{8,9},{9,8},{10,11... | collective-permute-start | bytes 3080 | tf_op jit(solution)/shard_map/ppermute | solution.py:402
  111.9 0.8 collective-permute-done.17.theirs_ref
  112.8 17.9 %all_to_all.21 = f32[128,2,128]{2,1,0:T(2,128)S(1)} all-to-all(f32[128,2,128]{2,1,0:T(2,128)S(1)} %shard_map.115), channel_id=1, replica_groups=mesh['gx'=32,'gy'=4,'gz'=2] {'gx','gy'}, dimensions={0} | all-to-all | bytes 262144 | tf_op jit(solution)/shard_map/all_to_all | solution.py:405
  130.7 0.9 shard_map.116
  131.6 2.1 %collective-permute-start.18 = (f32[1,128]{1,0:T(1,128)S(1)}, f32[1,128]{1,0:T(1,128)S(1)}, u32[]{:S(2)}, u32[]{:S(2)}) collective-permute-start(f32[1,128]{1,0:T(1,128)S(1)} %get-tuple-element.71.mine_ref), channel_id=1, source_target_pairs={{0,1},{1,0},{2,3},{3,2},{4,5},{5,4},{6,7},{7,6},{8,9},{9,8},{10,11... | collective-permute-start | bytes 1544 | tf_op jit(solution)/shard_map/ppermute | solution.py:402
  133.7 0.8 collective-permute-done.18.theirs_ref
  134.6 16.1 %all_to_all.22 = f32[128,1,128]{2,1,0:T(1,128)S(1)} all-to-all(f32[128,1,128]{2,1,0:T(1,128)S(1)} %shard_map.117), channel_id=1, replica_groups=mesh['gx'=32,'gy'=4,'gz'=2] {'gx','gy'}, dimensions={0} | all-to-all | bytes 131072 | tf_op jit(solution)/shard_map/all_to_all | solution.py:405
  150.7 0.8 shard_map.118
  (12 shorter events, 0.2 us)
Async XLA Ops:
  2.1 4.1 %collective-permute-start.5 = (f32[1,128]{1,0:T(1,128)S(1)}, f32[1,128]{1,0:T(1,128)S(1)}, u32[]{:S(2)}, u32[]{:S(2)}) collective-permute-start(f32[1,128]{1,0:T(1,128)S(1)} %get-tuple-element.45.mine_ref), channel_id=1, source_target_pairs={{0,1},{1,0},{2,3},{3,2},{4,5},{5,4},{6,7},{7,6},{8,9},{9,8},{10,11... | collective-permute-start | bytes 1544 | tf_op jit(solution)/shard_map/ppermute | solution.py:402
  6.9 24.7 %all-to-all-start = ((f32[128,1,128]{2,1,0:T(1,128)}), f32[128,1,128]{2,1,0:T(1,128)S(1)}, u32[]{:S(2)}, u32[]{:S(2)}) async-start(f32[128,1,128]{2,1,0:T(1,128)} %shard_map.98), calls=%async_computation | async-start | bytes 131072 | tf_op jit(solution)/shard_map/all_to_all | solution.py:405
  20.7 1.5 %collective-permute-start = (f32[4,2,128]{2,1,0:T(2,128)S(1)}, f32[4,2,128]{2,1,0:T(2,128)S(1)}, u32[]{:S(2)}, u32[]{:S(2)}) collective-permute-start(f32[4,2,128]{2,1,0:T(2,128)S(1)} %shard_map.95), channel_id=1, source_target_pairs={{0,1},{1,0},{2,3},{3,2},{4,5},{5,4},{6,7},{7,6},{8,9},{9,8},{10,11... | collective-permute-start | bytes 12296 | tf_op jit(solution)/shard_map/ppermute | solution.py:390
  22.2 4.3 %collective-permute-start.1 = (f32[4,2,8,128]{3,2,1,0:T(8,128)S(1)}, f32[4,2,8,128]{3,2,1,0:T(8,128)S(1)}, u32[]{:S(2)}, u32[]{:S(2)}) collective-permute-start(f32[4,2,8,128]{3,2,1,0:T(8,128)S(1)} %get-tuple-element.43), channel_id=1, source_target_pairs={{0,2},{2,4},{4,6},{6,0},{1,3},{3,5},{5,7},{7,1},{8,10},{10,12},{12... | collective-permute-start | bytes 98312 | tf_op jit(solution)/shard_map/ppermute | solution.py:394
  23.1 3.4 %collective-permute-start.2 = (f32[4,2,8,128]{3,2,1,0:T(8,128)S(1)}, f32[4,2,8,128]{3,2,1,0:T(8,128)S(1)}, u32[]{:S(2)}, u32[]{:S(2)}) collective-permute-start(f32[4,2,8,128]{3,2,1,0:T(8,128)S(1)} %get-tuple-element.44), channel_id=1, source_target_pairs={{2,0},{4,2},{6,4},{0,6},{3,1},{5,3},{7,5},{1,7},{10,8},{12,10},{14... | collective-permute-start | bytes 98312 | tf_op jit(solution)/shard_map/ppermute | solution.py:395
  26.5 11.8 %collective-permute-start.4 = (f32[4,5,8,128]{3,2,1,0:T(8,128)S(1)}, f32[4,5,8,128]{3,2,1,0:T(8,128)S(1)}, u32[]{:S(2)}, u32[]{:S(2)}) collective-permute-start(f32[4,5,8,128]{3,2,1,0:T(8,128)S(1)} %shard_map.97.block_ref), channel_id=1, source_target_pairs={{8,0},{16,8},{24,16},{32,24},{40,32},{48,40},{56,48},{64,56},{72,6... | collective-permute-start | bytes 245768 | tf_op jit(solution)/shard_map/ppermute | solution.py:398
  31.6 6.8 %collective-permute-start.3 = (f32[4,5,8,128]{3,2,1,0:T(8,128)S(1)}, f32[4,5,8,128]{3,2,1,0:T(8,128)S(1)}, u32[]{:S(2)}, u32[]{:S(2)}) collective-permute-start(f32[4,5,8,128]{3,2,1,0:T(8,128)S(1)} %shard_map.97.block_ref), channel_id=1, source_target_pairs={{0,8},{8,16},{16,24},{24,32},{32,40},{40,48},{48,56},{56,64},{64,7... | collective-permute-start | bytes 245768 | tf_op jit(solution)/shard_map/ppermute | solution.py:398
  48.7 5.2 %collective-permute-start.6 = (f32[1,2,128]{2,1,0:T(2,128)S(1)}, f32[1,2,128]{2,1,0:T(2,128)S(1)}, u32[]{:S(2)}, u32[]{:S(2)}) collective-permute-start(f32[1,2,128]{2,1,0:T(2,128)S(1)} %shard_map.103), channel_id=1, source_target_pairs={{0,1},{1,0},{2,3},{3,2},{4,5},{5,4},{6,7},{7,6},{8,9},{9,8},{10,11... | collective-permute-start | bytes 3080 | tf_op jit(solution)/shard_map/ppermute | solution.py:390
  54.0 5.3 %collective-permute-start.7 = (f32[1,2,8,128]{3,2,1,0:T(8,128)S(1)}, f32[1,2,8,128]{3,2,1,0:T(8,128)S(1)}, u32[]{:S(2)}, u32[]{:S(2)}) collective-permute-start(f32[1,2,8,128]{3,2,1,0:T(8,128)S(1)} %get-tuple-element.58), channel_id=1, source_target_pairs={{0,2},{2,4},{4,6},{6,0},{1,3},{3,5},{5,7},{7,1},{8,10},{10,12},{12... | collective-permute-start | bytes 24584 | tf_op jit(solution)/shard_map/ppermute | solution.py:394
  54.4 4.9 %collective-permute-start.8 = (f32[1,2,8,128]{3,2,1,0:T(8,128)S(1)}, f32[1,2,8,128]{3,2,1,0:T(8,128)S(1)}, u32[]{:S(2)}, u32[]{:S(2)}) collective-permute-start(f32[1,2,8,128]{3,2,1,0:T(8,128)S(1)} %get-tuple-element.59), channel_id=1, source_target_pairs={{2,0},{4,2},{6,4},{0,6},{3,1},{5,3},{7,5},{1,7},{10,8},{12,10},{14... | collective-permute-start | bytes 24584 | tf_op jit(solution)/shard_map/ppermute | solution.py:395
  59.2 4.1 %collective-permute-start.10 = (f32[1,5,8,128]{3,2,1,0:T(8,128)S(1)}, f32[1,5,8,128]{3,2,1,0:T(8,128)S(1)}, u32[]{:S(2)}, u32[]{:S(2)}) collective-permute-start(f32[1,5,8,128]{3,2,1,0:T(8,128)S(1)} %shard_map.105), channel_id=1, source_target_pairs={{8,0},{16,8},{24,16},{32,24},{40,32},{48,40},{56,48},{64,56},{72,6... | collective-permute-start | bytes 61448 | tf_op jit(solution)/shard_map/ppermute | solution.py:398
  61.7 6.0 %collective-permute-start.9 = (f32[1,5,8,128]{3,2,1,0:T(8,128)S(1)}, f32[1,5,8,128]{3,2,1,0:T(8,128)S(1)}, u32[]{:S(2)}, u32[]{:S(2)}) collective-permute-start(f32[1,5,8,128]{3,2,1,0:T(8,128)S(1)} %shard_map.105), channel_id=1, source_target_pairs={{0,8},{8,16},{16,24},{24,32},{32,40},{40,48},{48,56},{56,64},{64,7... | collective-permute-start | bytes 61448 | tf_op jit(solution)/shard_map/ppermute | solution.py:398
  70.4 4.0 %collective-permute-start.11 = (f32[2,128]{1,0:T(2,128)S(1)}, f32[2,128]{1,0:T(2,128)S(1)}, u32[]{:S(2)}, u32[]{:S(2)}) collective-permute-start(f32[2,128]{1,0:T(2,128)S(1)} %get-tuple-element.62.mine_ref), channel_id=1, source_target_pairs={{0,1},{1,0},{2,3},{3,2},{4,5},{5,4},{6,7},{7,6},{8,9},{9,8},{10,11... | collective-permute-start | bytes 3080 | tf_op jit(solution)/shard_map/ppermute | solution.py:402
  92.6 2.9 %collective-permute-start.12 = (f32[1,2,128]{2,1,0:T(2,128)S(1)}, f32[1,2,128]{2,1,0:T(2,128)S(1)}, u32[]{:S(2)}, u32[]{:S(2)}) collective-permute-start(f32[1,2,128]{2,1,0:T(2,128)S(1)} %shard_map.110), channel_id=1, source_target_pairs={{0,1},{1,0},{2,3},{3,2},{4,5},{5,4},{6,7},{7,6},{8,9},{9,8},{10,11... | collective-permute-start | bytes 3080 | tf_op jit(solution)/shard_map/ppermute | solution.py:390
  95.6 3.7 %collective-permute-start.13 = (f32[1,2,8,128]{3,2,1,0:T(8,128)S(1)}, f32[1,2,8,128]{3,2,1,0:T(8,128)S(1)}, u32[]{:S(2)}, u32[]{:S(2)}) collective-permute-start(f32[1,2,8,128]{3,2,1,0:T(8,128)S(1)} %get-tuple-element.65), channel_id=1, source_target_pairs={{0,2},{2,4},{4,6},{6,0},{1,3},{3,5},{5,7},{7,1},{8,10},{10,12},{12... | collective-permute-start | bytes 24584 | tf_op jit(solution)/shard_map/ppermute | solution.py:394
  95.6 3.6 %collective-permute-start.14 = (f32[1,2,8,128]{3,2,1,0:T(8,128)S(1)}, f32[1,2,8,128]{3,2,1,0:T(8,128)S(1)}, u32[]{:S(2)}, u32[]{:S(2)}) collective-permute-start(f32[1,2,8,128]{3,2,1,0:T(8,128)S(1)} %get-tuple-element.66), channel_id=1, source_target_pairs={{2,0},{4,2},{6,4},{0,6},{3,1},{5,3},{7,5},{1,7},{10,8},{12,10},{14... | collective-permute-start | bytes 24584 | tf_op jit(solution)/shard_map/ppermute | solution.py:395
  99.3 3.1 %collective-permute-start.16 = (f32[1,5,8,128]{3,2,1,0:T(8,128)S(1)}, f32[1,5,8,128]{3,2,1,0:T(8,128)S(1)}, u32[]{:S(2)}, u32[]{:S(2)}) collective-permute-start(f32[1,5,8,128]{3,2,1,0:T(8,128)S(1)} %shard_map.112), channel_id=1, source_target_pairs={{8,0},{16,8},{24,16},{32,24},{40,32},{48,40},{56,48},{64,56},{72,6... | collective-permute-start | bytes 61448 | tf_op jit(solution)/shard_map/ppermute | solution.py:398
  100.0 6.0 %collective-permute-start.15 = (f32[1,5,8,128]{3,2,1,0:T(8,128)S(1)}, f32[1,5,8,128]{3,2,1,0:T(8,128)S(1)}, u32[]{:S(2)}, u32[]{:S(2)}) collective-permute-start(f32[1,5,8,128]{3,2,1,0:T(8,128)S(1)} %shard_map.112), channel_id=1, source_target_pairs={{0,8},{8,16},{16,24},{24,32},{32,40},{40,48},{48,56},{56,64},{64,7... | collective-permute-start | bytes 61448 | tf_op jit(solution)/shard_map/ppermute | solution.py:398
  108.7 4.0 %collective-permute-start.17 = (f32[2,128]{1,0:T(2,128)S(1)}, f32[2,128]{1,0:T(2,128)S(1)}, u32[]{:S(2)}, u32[]{:S(2)}) collective-permute-start(f32[2,128]{1,0:T(2,128)S(1)} %get-tuple-element.68.mine_ref), channel_id=1, source_target_pairs={{0,1},{1,0},{2,3},{3,2},{4,5},{5,4},{6,7},{7,6},{8,9},{9,8},{10,11... | collective-permute-start | bytes 3080 | tf_op jit(solution)/shard_map/ppermute | solution.py:402
  131.6 3.0 %collective-permute-start.18 = (f32[1,128]{1,0:T(1,128)S(1)}, f32[1,128]{1,0:T(1,128)S(1)}, u32[]{:S(2)}, u32[]{:S(2)}) collective-permute-start(f32[1,128]{1,0:T(1,128)S(1)} %get-tuple-element.71.mine_ref), channel_id=1, source_target_pairs={{0,1},{1,0},{2,3},{3,2},{4,5},{5,4},{6,7},{7,6},{8,9},{9,8},{10,11... | collective-permute-start | bytes 1544 | tf_op jit(solution)/shard_map/ppermute | solution.py:402

commit v6 on v5

--- a/solution.py
+++ b/solution.py
@@ -56,9 +56,17 @@
     return copies
 
 
+def facing(rows, second):
+    return jnp.where(second == 0, rows[7:8], rows[0:1])
+
+
+def from_across(across_ref, f, y):
+    return across_ref[8 + f * 2 + y : 9 + f * 2 + y, :] if across_ref.ndim == 2 else across_ref[f, y : y + 1]
+
+
 def prepare_kernel(
     second_ref, counts_hbm, offsets_hbm, correction_hbm, right_hbm, dirichlet_hbm, basis_hbm,
-    geometry_ref, live_ref, residual_ref, payload_ref, counts_ref, dirichlet_ref, basis_ref,
+    geometry_ref, live_ref, residual_ref, packed_ref, counts_ref, dirichlet_ref, basis_ref,
     counts_smem, offsets_ref, correction_ref, right_ref, part_ref, sems,
 ):
     copies = fetch(
@@ -79,23 +87,25 @@
     geometry_ref[0:3] = offsets_ref[...]
     geometry_ref[3] = correction_ref[...] * live * (10.0 / SLOTS)
     residual_ref[...] = right_ref[...] * live
+    for f in range(4):
+        for y in range(2):
+            packed_ref[8 + f * 2 + y : 9 + f * 2 + y, :] = facing(geometry_ref[f, y], second_ref[0])
     copies[-1].wait()
-    payload_ref[...] = project(basis_ref, residual_ref[...], part_ref, second_ref[0])
+    packed_ref[0:8, :] = jnp.broadcast_to(project(basis_ref, residual_ref[...], part_ref, second_ref[0]), (8, SLOTS))
 
 
 def top_face_kernel(second_ref, field_ref, face_ref):
     second = second_ref[0]
     for f in range(field_ref.shape[0]):
         for y in range(2):
-            rows = field_ref[f, y]
-            face_ref[f, y : y + 1, :] = jnp.where(second == 0, rows[7:8], rows[0:1])
+            face_ref[f, y : y + 1, :] = facing(field_ref[f, y], second)
 
 
 def side_faces_kernel(field_ref, across_ref, up_ref, down_ref):
     for f in range(field_ref.shape[0]):
         for y, ref in enumerate((down_ref, up_ref)):
             ref[f, 0] = field_ref[f, y]
-            ref[f, 1] = jnp.broadcast_to(across_ref[f, y : y + 1, :], (8, SLOTS))
+            ref[f, 1] = jnp.broadcast_to(from_across(across_ref, f, y), (8, SLOTS))
 
 
 def block_kernel(spot_ref, field_ref, across_ref, below_ref, above_ref, block_ref):
@@ -109,12 +119,13 @@
         block_ref[f, 1] = field_ref[f, 0]
         block_ref[f, 2] = field_ref[f, 1]
         block_ref[f, 3] = sides[1]
-        for y, row in enumerate((sides[2], across_ref[f, 0:1], across_ref[f, 1:2], sides[3])):
+        for y, row in enumerate((sides[2], from_across(across_ref, f, 0), from_across(across_ref, f, 1), sides[3])):
             block_ref[f, 4, y : y + 1, :] = row
 
 
 def spread_kernel(mine_ref, theirs_ref, spread_ref):
-    rows = mine_ref[...] + theirs_ref[...]
+    count = spread_ref.shape[1]
+    rows = mine_ref[0:count, :] + theirs_ref[0:count, :]
     spread_ref[...] = jnp.broadcast_to(rows[None], spread_ref.shape)
 
 
@@ -378,16 +389,20 @@
     payload_ref[1:2, :] = inner_row(pairs)
 
 
+def swap(x):
+    return lax.ppermute(x, "gz", [(0, 1), (1, 0)])
+
+
 def turns(axis):
     size = lax.axis_size(axis)
     up = [(i, (i + 1) % size) for i in range(size)]
     return up, [(j, i) for i, j in up]
 
 
-def around(field, second, gy_spot):
+def around(field, second, gy_spot, across=None):
     count = field.shape[0]
-    face = call(top_face_kernel, f32(count, 2, SLOTS), [SM, VM])(second, field)
-    across = lax.ppermute(face, "gz", [(0, 1), (1, 0)])
+    if across is None:
+        across = swap(call(top_face_kernel, f32(count, 2, SLOTS), [SM, VM])(second, field))
     side = f32(count, 2, 8, SLOTS)
     upper, lower = call(side_faces_kernel, (side, side), [VM] * 2)(field, across)
     up, down = turns("gy")
@@ -398,9 +413,9 @@
     return block, lax.ppermute(block, "gx", up), lax.ppermute(block, "gx", down)
 
 
-def gather(payload):
-    theirs = lax.ppermute(payload, "gz", [(0, 1), (1, 0)])
-    rows = payload.shape[0]
+def gather(payload, theirs=None, rows=None):
+    theirs = swap(payload) if theirs is None else theirs
+    rows = payload.shape[0] if rows is None else rows
     spread = call(spread_kernel, f32(128, rows, SLOTS), [VM] * 2)(payload, theirs)
     got = lax.all_to_all(spread, ("gx", "gy"), 0, 0, tiled=True)
     return got.reshape(128 * rows, SLOTS)
@@ -421,10 +436,10 @@
     vmem = lambda *shape: pltpu.VMEM(shape, jnp.float32)
     part = vmem(64, SLOTS)
 
-    geometry, live, residual, payload, counts, dirichlet, basis = call(
+    geometry, live, residual, packed, counts, dirichlet, basis = call(
         prepare_kernel,
         (
-            f32(4, 2, 8, SLOTS), cells, cells, f32(1, SLOTS),
+            f32(4, 2, 8, SLOTS), cells, cells, f32(16, SLOTS),
             pltpu.VMEM((1, 2, 8), jnp.int32), vmem(2, 8, SLOTS), vmem(64, 2, 8, SLOTS),
         ),
         [SM] + [ANY] * 6,
@@ -434,8 +449,9 @@
         ],
     )(second, *map(outside, (counts, offsets, correction, right_side, dirichlet, basis)))
     counts, dirichlet, basis = onchip(counts), onchip(dirichlet), onchip(basis)
-    coefficient = gather(payload)
-    block, before, after = around(geometry, second, gy_spot)
+    theirs = swap(packed)
+    coefficient = gather(packed, theirs, 1)
+    block, before, after = around(geometry, second, gy_spot, theirs)
     coefficient, block, centre = lax.optimization_barrier((coefficient, block, geometry))
     mine = call(centre_kernel, f32(16, 4, SLOTS, SLOTS), [VM])(centre)
 

time: 152 us -> 150 us (0.987)
  starting transfers between devices: 51.3 us -> 46.4 us
  Pallas kernels: 30.7 us -> 33.5 us
    ppermute x7 -> x6, starting transfers between devices: 19 us -> 13.6 us  [swap(): return lax.ppermute(x, 'gz', [(0, 1), (1, 0)])]
    ppermute x3, starting transfers between devices: 8.26 us -> 5.85 us  [around(): above = lax.ppermute(lower, 'gy', down)]
    ppermute x3, starting transfers between devices: 8.18 us -> 10.2 us  [around(): lax.ppermute(block, 'gx', down)]
    ppermute x7 -> x6, waiting for transfers between devices: 5.74 us -> 4.93 us  [swap(): return lax.ppermute(x, 'gz', [(0, 1), (1, 0)])]
  transfers between devices with their start and end apart: 20 -> 19, of which waited for: 12 -> 13; matrix products, arithmetic and copies ran while one was open for 0% -> 0% of each run, Pallas kernels for 7% -> 7%
where the time goes in v6:
time: 150 us
  blocking collectives  51.2 us (34%)
  starting transfers between devices  46.4 us (31%)
  Pallas kernels  33.5 us (22%)
  waiting for transfers between devices  18.3 us (12%)
    all_to_all x3, blocking collectives, gather(): got = lax.all_to_all(spread, ('gx', 'gy'), 0, 0, tiled=True)  51.2 us
    all_to_all x1, starting transfers between devices, gather(): got = lax.all_to_all(spread, ('gx', 'gy'), 0, 0, tiled=True)  13.8 us
    ppermute x6, starting transfers between devices, swap(): return lax.ppermute(x, 'gz', [(0, 1), (1, 0)])  13.6 us
    pallas_call x1, Pallas kernels, per_device(): call(outer_weights_kernel, (weight_shape, weight_shape, cells, cells, vme...  11.2 us
    ppermute x3, starting transfers between devices, around(): lax.ppermute(block, 'gx', down)  10.2 us
    ppermute x3, waiting for transfers between devices, around(): lax.ppermute(block, 'gx', up)  7.61 us
    pallas_call x1, Pallas kernels, per_device(): call(middle_weights_kernel, (weight_shape, sums_shape), [SM, SM] + [VM] *...  6.19 us
    pallas_call x2, Pallas kernels, image_of(): call(image_kernel, (cells, f32(2, SLOTS)), [SM, SM] + [VM] * (10 + len(ol...  5.87 us
  transfers between devices with their start and end apart: 19, of which 13 were waited for; matrix products, arithmetic and copies ran while one was open for 0% of the time, Pallas kernels for 7%

profile of v6, /device:TPU:1, one launch (start us, length us, event | category | flops | bytes accessed | tf_op | source)
XLA Modules:
  0.0 150.1 jit_solution(4860979560020645269)
XLA Ops:
  0.6 1.4 shard_map.94
  2.1 3.3 %collective-permute-start = (f32[16,128]{1,0:T(8,128)S(1)}, f32[16,128]{1,0:T(8,128)S(1)}, u32[]{:S(2)}, u32[]{:S(2)}) collective-permute-start(f32[16,128]{1,0:T(8,128)S(1)} %get-tuple-element.43.mine_ref), channel_id=1, source_target_pairs={{0,1},{1,0},{2,3},{3,2},{4,5},{5,4},{6,7},{7,6},{8,9},{9,8},{10,11... | collective-permute-start | bytes 24584 | tf_op jit(solution)/shard_map/ppermute | solution.py:393
  5.4 0.8 collective-permute-done.across_ref.theirs_ref
  6.2 0.7 shard_map.97
  6.9 13.8 %all-to-all-start = ((f32[128,1,128]{2,1,0:T(1,128)}), f32[128,1,128]{2,1,0:T(1,128)S(1)}, u32[]{:S(2)}, u32[]{:S(2)}) async-start(f32[128,1,128]{2,1,0:T(1,128)} %shard_map.97), calls=%async_computation | async-start | bytes 131072 | tf_op jit(solution)/shard_map/all_to_all | solution.py:420
  20.7 0.7 collective-permute-start.1
  21.3 2.1 %collective-permute-start.2 = (f32[4,2,8,128]{3,2,1,0:T(8,128)S(1)}, f32[4,2,8,128]{3,2,1,0:T(8,128)S(1)}, u32[]{:S(2)}, u32[]{:S(2)}) collective-permute-start(f32[4,2,8,128]{3,2,1,0:T(8,128)S(1)} %get-tuple-element.45), channel_id=1, source_target_pairs={{2,0},{4,2},{6,4},{0,6},{3,1},{5,3},{7,5},{1,7},{10,8},{12,10},{14... | collective-permute-start | bytes 98312 | tf_op jit(solution)/shard_map/ppermute | solution.py:410
  23.4 1.6 %collective-permute-done.1.below_ref = f32[4,2,8,128]{3,2,1,0:T(8,128)S(1)} collective-permute-done((f32[4,2,8,128]{3,2,1,0:T(8,128)S(1)}, f32[4,2,8,128]{3,2,1,0:T(8,128)S(1)}, u32[]{:S(2)}, u32[]{:S(2)}) %collective-permute-start.1) | collective-permute-done | bytes 32800 | tf_op jit(solution)/shard_map/ppermute | solution.py:409
  25.1 0.0 collective-permute-done.2.above_ref
  25.1 4.7 %collective-permute-start.4 = (f32[4,5,8,128]{3,2,1,0:T(8,128)S(1)}, f32[4,5,8,128]{3,2,1,0:T(8,128)S(1)}, u32[]{:S(2)}, u32[]{:S(2)}) collective-permute-start(f32[4,5,8,128]{3,2,1,0:T(8,128)S(1)} %shard_map.96.block_ref), channel_id=1, source_target_pairs={{8,0},{16,8},{24,16},{32,24},{40,32},{48,40},{56,48},{64,56},{72,6... | collective-permute-start | bytes 245768 | tf_op jit(solution)/shard_map/ppermute | solution.py:413
  29.8 0.0 collective-permute-start.3
  29.8 1.5 all-to-all-done
  31.3 1.3 shard_map.98.mine_ref
  32.6 6.2 %shard_map.99 = (f32[16,16,9,8,128]{4,3,2,1,0:T(8,128)S(1)}, f32[16,128,128]{2,1,0:T(8,128)S(1)}) custom-call(s32[1]{0:T(128)} %bitcast.second_ref, s32[1,2,8]{2,1,0:T(2,128)S(1)} %get-tuple-element.41.counts_ref, f32[16,4,128,128]{3,2,1,0:T(8,128)S(1)} %shard_map.98.mine_ref, f32[4,5,8,128]{3,2,1,0:T(8,128)S(1)} %shard_map.96.block_ref), custom_call_target="tpu_custom_call" | custom-call | tf_op jit(solution)/shard_map/pallas_call | solution.py:460
  38.8 0.0 collective-permute-done.4.after_ref
  38.8 0.0 collective-permute-done.3.before_ref
  38.8 11.2 %shard_map.100 = (f32[16,16,9,8,128]{4,3,2,1,0:T(8,128)S(1)}, f32[16,16,9,8,128]{4,3,2,1,0:T(8,128)S(1)}, f32[2,8,128]{2,1,0:T(8,128)S(1)}, f32[2,8,128]{2,1,0:T(8,128)S(1)}, f32[64,16384]{1,0:T(8,128)S(1)}) custom-call(s32[1]{0:T(128)} %bitcast.second_ref, s32[1]{0:T(128)} %bitcast.6.spot_ref, s32[1,2,8]{2,1,0:T(2,128)S(1)} %get-tuple-element.41.counts_ref, ...), custom_call_target="tpu_custom_call" | custom-call | tf_op jit(solution)/shard_map/pallas_call | solution.py:466
  50.0 0.6 shard_map.101.own_ref.smoothed_ref.rest_0_.first_ref
  50.7 0.4 collective-permute-start.5
  51.1 0.8 collective-permute-done.5.across_ref
  51.9 1.5 %collective-permute-start.6 = (f32[1,2,8,128]{3,2,1,0:T(8,128)S(1)}, f32[1,2,8,128]{3,2,1,0:T(8,128)S(1)}, u32[]{:S(2)}, u32[]{:S(2)}) collective-permute-start(f32[1,2,8,128]{3,2,1,0:T(8,128)S(1)} %get-tuple-element.58), channel_id=1, source_target_pairs={{0,2},{2,4},{4,6},{6,0},{1,3},{3,5},{5,7},{7,1},{8,10},{10,12},{12... | collective-permute-start | bytes 24584 | tf_op jit(solution)/shard_map/ppermute | solution.py:409
  53.5 1.1 collective-permute-start.7
  54.6 1.0 collective-permute-done.6.below_ref
  55.7 0.6 collective-permute-done.7.above_ref
  56.3 4.7 %collective-permute-start.9 = (f32[1,5,8,128]{3,2,1,0:T(8,128)S(1)}, f32[1,5,8,128]{3,2,1,0:T(8,128)S(1)}, u32[]{:S(2)}, u32[]{:S(2)}) collective-permute-start(f32[1,5,8,128]{3,2,1,0:T(8,128)S(1)} %shard_map.104), channel_id=1, source_target_pairs={{8,0},{16,8},{24,16},{32,24},{40,32},{48,40},{56,48},{64,56},{72,6... | collective-permute-start | bytes 61448 | tf_op jit(solution)/shard_map/ppermute | solution.py:413
  61.0 0.0 collective-permute-start.8
  61.0 1.8 %shard_map.105.old_sums_ref = f32[16,128,128]{2,1,0:T(8,128)S(1)} custom-call(s32[1]{0:T(128)} %bitcast.second_ref, s32[1,2,8]{2,1,0:T(2,128)S(1)} %get-tuple-element.41.counts_ref, f32[16,16,9,8,128]{4,3,2,1,0:T(8,128)S(1)} %get-tuple-element.60.weight_ref, f32[5,8,128]{2,1,0:T(8,128)S(1)} %bitcast.36), custom_call_target="tpu_custom_call" | custom-call | tf_op jit(solution)/shard_map/pallas_call | solution.py:476
  62.7 0.0 collective-permute-done.9
  62.8 4.2 %collective-permute-done.8 = f32[1,5,8,128]{3,2,1,0:T(8,128)S(1)} collective-permute-done((f32[1,5,8,128]{3,2,1,0:T(8,128)S(1)}, f32[1,5,8,128]{3,2,1,0:T(8,128)S(1)}, u32[]{:S(2)}, u32[]{:S(2)}) %collective-permute-start.8) | collective-permute-done | bytes 20512 | tf_op jit(solution)/shard_map/ppermute | solution.py:413
  66.9 2.9 %shard_map.106 = (f32[2,8,128]{2,1,0:T(8,128)S(1)}, f32[2,128]{1,0:T(2,128)S(1)}) custom-call(s32[1]{0:T(128)} %bitcast.second_ref, s32[1,2,8]{2,1,0:T(2,128)S(1)} %get-tuple-element.41.counts_ref, f32[16,16,9,8,128]{4,3,2,1,0:T(8,128)S(1)} %get-tuple-element.51.weight_a, f32[16,16,9,8,128]{4,3,2,1,0:T(8,128)S(1)} %get-tuple-element.52.weight_c, ...), custom_call_target="tpu_custom_call" | custom-call | tf_op jit(solution)/shard_map/pallas_call | solution.py:479
  69.9 2.7 %collective-permute-start.10 = (f32[2,128]{1,0:T(2,128)S(1)}, f32[2,128]{1,0:T(2,128)S(1)}, u32[]{:S(2)}, u32[]{:S(2)}) collective-permute-start(f32[2,128]{1,0:T(2,128)S(1)} %get-tuple-element.62.mine_ref), channel_id=1, source_target_pairs={{0,1},{1,0},{2,3},{3,2},{4,5},{5,4},{6,7},{7,6},{8,9},{9,8},{10,11... | collective-permute-start | bytes 3080 | tf_op jit(solution)/shard_map/ppermute | solution.py:393
  72.6 0.8 collective-permute-done.10.theirs_ref
  73.4 17.3 %all_to_all.20 = f32[128,2,128]{2,1,0:T(2,128)S(1)} all-to-all(f32[128,2,128]{2,1,0:T(2,128)S(1)} %shard_map.107), channel_id=1, replica_groups=mesh['gx'=32,'gy'=4,'gz'=2] {'gx','gy'}, dimensions={0} | all-to-all | bytes 262144 | tf_op jit(solution)/shard_map/all_to_all | solution.py:420
  90.7 0.8 shard_map.108
  91.5 2.1 %collective-permute-start.11 = (f32[1,2,128]{2,1,0:T(2,128)S(1)}, f32[1,2,128]{2,1,0:T(2,128)S(1)}, u32[]{:S(2)}, u32[]{:S(2)}) collective-permute-start(f32[1,2,128]{2,1,0:T(2,128)S(1)} %shard_map.109), channel_id=1, source_target_pairs={{0,1},{1,0},{2,3},{3,2},{4,5},{5,4},{6,7},{7,6},{8,9},{9,8},{10,11... | collective-permute-start | bytes 3080 | tf_op jit(solution)/shard_map/ppermute | solution.py:393
  93.6 0.8 collective-permute-done.11.across_ref
  94.5 0.1 collective-permute-start.12
  94.5 2.6 %collective-permute-start.13 = (f32[1,2,8,128]{3,2,1,0:T(8,128)S(1)}, f32[1,2,8,128]{3,2,1,0:T(8,128)S(1)}, u32[]{:S(2)}, u32[]{:S(2)}) collective-permute-start(f32[1,2,8,128]{3,2,1,0:T(8,128)S(1)} %get-tuple-element.66), channel_id=1, source_target_pairs={{2,0},{4,2},{6,4},{0,6},{3,1},{5,3},{7,5},{1,7},{10,8},{12,10},{14... | collective-permute-start | bytes 24584 | tf_op jit(solution)/shard_map/ppermute | solution.py:410
  97.1 1.0 collective-permute-done.12.below_ref
  98.2 0.0 collective-permute-done.13.above_ref
  98.2 0.7 collective-permute-start.15
  98.9 0.8 collective-permute-start.14
  99.7 1.8 %shard_map.112.old_sums_ref = f32[16,128,128]{2,1,0:T(8,128)S(1)} custom-call(s32[1]{0:T(128)} %bitcast.second_ref, s32[1,2,8]{2,1,0:T(2,128)S(1)} %get-tuple-element.41.counts_ref, f32[16,16,9,8,128]{4,3,2,1,0:T(8,128)S(1)} %get-tuple-element.60.weight_ref, f32[5,8,128]{2,1,0:T(8,128)S(1)} %bitcast.35), custom_call_target="tpu_custom_call" | custom-call | tf_op jit(solution)/shard_map/pallas_call | solution.py:476
  101.4 0.0 collective-permute-done.15
  101.4 3.4 %collective-permute-done.14 = f32[1,5,8,128]{3,2,1,0:T(8,128)S(1)} collective-permute-done((f32[1,5,8,128]{3,2,1,0:T(8,128)S(1)}, f32[1,5,8,128]{3,2,1,0:T(8,128)S(1)}, u32[]{:S(2)}, u32[]{:S(2)}) %collective-permute-start.14) | collective-permute-done | bytes 20512 | tf_op jit(solution)/shard_map/ppermute | solution.py:413
  104.9 2.9 %shard_map.113 = (f32[2,8,128]{2,1,0:T(8,128)S(1)}, f32[2,128]{1,0:T(2,128)S(1)}) custom-call(s32[1]{0:T(128)} %bitcast.second_ref, s32[1,2,8]{2,1,0:T(2,128)S(1)} %get-tuple-element.41.counts_ref, f32[16,16,9,8,128]{4,3,2,1,0:T(8,128)S(1)} %get-tuple-element.51.weight_a, f32[16,16,9,8,128]{4,3,2,1,0:T(8,128)S(1)} %get-tuple-element.52.weight_c, ...), custom_call_target="tpu_custom_call" | custom-call | tf_op jit(solution)/shard_map/pallas_call | solution.py:479
  107.8 2.9 %collective-permute-start.16 = (f32[2,128]{1,0:T(2,128)S(1)}, f32[2,128]{1,0:T(2,128)S(1)}, u32[]{:S(2)}, u32[]{:S(2)}) collective-permute-start(f32[2,128]{1,0:T(2,128)S(1)} %get-tuple-element.68.mine_ref), channel_id=1, source_target_pairs={{0,1},{1,0},{2,3},{3,2},{4,5},{5,4},{6,7},{7,6},{8,9},{9,8},{10,11... | collective-permute-start | bytes 3080 | tf_op jit(solution)/shard_map/ppermute | solution.py:393
  110.7 0.8 collective-permute-done.16.theirs_ref
  111.5 17.8 %all_to_all.21 = f32[128,2,128]{2,1,0:T(2,128)S(1)} all-to-all(f32[128,2,128]{2,1,0:T(2,128)S(1)} %shard_map.114), channel_id=1, replica_groups=mesh['gx'=32,'gy'=4,'gz'=2] {'gx','gy'}, dimensions={0} | all-to-all | bytes 262144 | tf_op jit(solution)/shard_map/all_to_all | solution.py:420
  129.3 0.9 shard_map.115
  130.3 2.1 %collective-permute-start.17 = (f32[1,128]{1,0:T(1,128)S(1)}, f32[1,128]{1,0:T(1,128)S(1)}, u32[]{:S(2)}, u32[]{:S(2)}) collective-permute-start(f32[1,128]{1,0:T(1,128)S(1)} %get-tuple-element.71.mine_ref), channel_id=1, source_target_pairs={{0,1},{1,0},{2,3},{3,2},{4,5},{5,4},{6,7},{7,6},{8,9},{9,8},{10,11... | collective-permute-start | bytes 1544 | tf_op jit(solution)/shard_map/ppermute | solution.py:393
  132.4 0.8 collective-permute-done.17.theirs_ref
  133.2 16.1 %all_to_all.22 = f32[128,1,128]{2,1,0:T(1,128)S(1)} all-to-all(f32[128,1,128]{2,1,0:T(1,128)S(1)} %shard_map.116), channel_id=1, replica_groups=mesh['gx'=32,'gy'=4,'gz'=2] {'gx','gy'}, dimensions={0} | all-to-all | bytes 131072 | tf_op jit(solution)/shard_map/all_to_all | solution.py:420
  149.4 0.8 shard_map.117
  (11 shorter events, 0.2 us)
Async XLA Ops:
  2.1 4.1 %collective-permute-start = (f32[16,128]{1,0:T(8,128)S(1)}, f32[16,128]{1,0:T(8,128)S(1)}, u32[]{:S(2)}, u32[]{:S(2)}) collective-permute-start(f32[16,128]{1,0:T(8,128)S(1)} %get-tuple-element.43.mine_ref), channel_id=1, source_target_pairs={{0,1},{1,0},{2,3},{3,2},{4,5},{5,4},{6,7},{7,6},{8,9},{9,8},{10,11... | collective-permute-start | bytes 24584 | tf_op jit(solution)/shard_map/ppermute | solution.py:393
  6.9 24.4 %all-to-all-start = ((f32[128,1,128]{2,1,0:T(1,128)}), f32[128,1,128]{2,1,0:T(1,128)S(1)}, u32[]{:S(2)}, u32[]{:S(2)}) async-start(f32[128,1,128]{2,1,0:T(1,128)} %shard_map.97), calls=%async_computation | async-start | bytes 131072 | tf_op jit(solution)/shard_map/all_to_all | solution.py:420
  20.7 4.4 %collective-permute-start.1 = (f32[4,2,8,128]{3,2,1,0:T(8,128)S(1)}, f32[4,2,8,128]{3,2,1,0:T(8,128)S(1)}, u32[]{:S(2)}, u32[]{:S(2)}) collective-permute-start(f32[4,2,8,128]{3,2,1,0:T(8,128)S(1)} %get-tuple-element.44), channel_id=1, source_target_pairs={{0,2},{2,4},{4,6},{6,0},{1,3},{3,5},{5,7},{7,1},{8,10},{10,12},{12... | collective-permute-start | bytes 98312 | tf_op jit(solution)/shard_map/ppermute | solution.py:409
  21.3 3.7 %collective-permute-start.2 = (f32[4,2,8,128]{3,2,1,0:T(8,128)S(1)}, f32[4,2,8,128]{3,2,1,0:T(8,128)S(1)}, u32[]{:S(2)}, u32[]{:S(2)}) collective-permute-start(f32[4,2,8,128]{3,2,1,0:T(8,128)S(1)} %get-tuple-element.45), channel_id=1, source_target_pairs={{2,0},{4,2},{6,4},{0,6},{3,1},{5,3},{7,5},{1,7},{10,8},{12,10},{14... | collective-permute-start | bytes 98312 | tf_op jit(solution)/shard_map/ppermute | solution.py:410
  25.1 13.7 %collective-permute-start.4 = (f32[4,5,8,128]{3,2,1,0:T(8,128)S(1)}, f32[4,5,8,128]{3,2,1,0:T(8,128)S(1)}, u32[]{:S(2)}, u32[]{:S(2)}) collective-permute-start(f32[4,5,8,128]{3,2,1,0:T(8,128)S(1)} %shard_map.96.block_ref), channel_id=1, source_target_pairs={{8,0},{16,8},{24,16},{32,24},{40,32},{48,40},{56,48},{64,56},{72,6... | collective-permute-start | bytes 245768 | tf_op jit(solution)/shard_map/ppermute | solution.py:413
  29.8 9.0 %collective-permute-start.3 = (f32[4,5,8,128]{3,2,1,0:T(8,128)S(1)}, f32[4,5,8,128]{3,2,1,0:T(8,128)S(1)}, u32[]{:S(2)}, u32[]{:S(2)}) collective-permute-start(f32[4,5,8,128]{3,2,1,0:T(8,128)S(1)} %shard_map.96.block_ref), channel_id=1, source_target_pairs={{0,8},{8,16},{16,24},{24,32},{32,40},{40,48},{48,56},{56,64},{64,7... | collective-permute-start | bytes 245768 | tf_op jit(solution)/shard_map/ppermute | solution.py:413
  50.7 1.2 collective-permute-start.5
  51.9 3.7 %collective-permute-start.6 = (f32[1,2,8,128]{3,2,1,0:T(8,128)S(1)}, f32[1,2,8,128]{3,2,1,0:T(8,128)S(1)}, u32[]{:S(2)}, u32[]{:S(2)}) collective-permute-start(f32[1,2,8,128]{3,2,1,0:T(8,128)S(1)} %get-tuple-element.58), channel_id=1, source_target_pairs={{0,2},{2,4},{4,6},{6,0},{1,3},{3,5},{5,7},{7,1},{8,10},{10,12},{12... | collective-permute-start | bytes 24584 | tf_op jit(solution)/shard_map/ppermute | solution.py:409
  53.5 2.8 %collective-permute-start.7 = (f32[1,2,8,128]{3,2,1,0:T(8,128)S(1)}, f32[1,2,8,128]{3,2,1,0:T(8,128)S(1)}, u32[]{:S(2)}, u32[]{:S(2)}) collective-permute-start(f32[1,2,8,128]{3,2,1,0:T(8,128)S(1)} %get-tuple-element.59), channel_id=1, source_target_pairs={{2,0},{4,2},{6,4},{0,6},{3,1},{5,3},{7,5},{1,7},{10,8},{12,10},{14... | collective-permute-start | bytes 24584 | tf_op jit(solution)/shard_map/ppermute | solution.py:410
  56.3 6.5 %collective-permute-start.9 = (f32[1,5,8,128]{3,2,1,0:T(8,128)S(1)}, f32[1,5,8,128]{3,2,1,0:T(8,128)S(1)}, u32[]{:S(2)}, u32[]{:S(2)}) collective-permute-start(f32[1,5,8,128]{3,2,1,0:T(8,128)S(1)} %shard_map.104), channel_id=1, source_target_pairs={{8,0},{16,8},{24,16},{32,24},{40,32},{48,40},{56,48},{64,56},{72,6... | collective-permute-start | bytes 61448 | tf_op jit(solution)/shard_map/ppermute | solution.py:413
  61.0 6.0 %collective-permute-start.8 = (f32[1,5,8,128]{3,2,1,0:T(8,128)S(1)}, f32[1,5,8,128]{3,2,1,0:T(8,128)S(1)}, u32[]{:S(2)}, u32[]{:S(2)}) collective-permute-start(f32[1,5,8,128]{3,2,1,0:T(8,128)S(1)} %shard_map.104), channel_id=1, source_target_pairs={{0,8},{8,16},{16,24},{24,32},{32,40},{40,48},{48,56},{56,64},{64,7... | collective-permute-start | bytes 61448 | tf_op jit(solution)/shard_map/ppermute | solution.py:413
  69.9 3.5 %collective-permute-start.10 = (f32[2,128]{1,0:T(2,128)S(1)}, f32[2,128]{1,0:T(2,128)S(1)}, u32[]{:S(2)}, u32[]{:S(2)}) collective-permute-start(f32[2,128]{1,0:T(2,128)S(1)} %get-tuple-element.62.mine_ref), channel_id=1, source_target_pairs={{0,1},{1,0},{2,3},{3,2},{4,5},{5,4},{6,7},{7,6},{8,9},{9,8},{10,11... | collective-permute-start | bytes 3080 | tf_op jit(solution)/shard_map/ppermute | solution.py:393
  91.5 2.9 %collective-permute-start.11 = (f32[1,2,128]{2,1,0:T(2,128)S(1)}, f32[1,2,128]{2,1,0:T(2,128)S(1)}, u32[]{:S(2)}, u32[]{:S(2)}) collective-permute-start(f32[1,2,128]{2,1,0:T(2,128)S(1)} %shard_map.109), channel_id=1, source_target_pairs={{0,1},{1,0},{2,3},{3,2},{4,5},{5,4},{6,7},{7,6},{8,9},{9,8},{10,11... | collective-permute-start | bytes 3080 | tf_op jit(solution)/shard_map/ppermute | solution.py:393
  94.5 3.7 %collective-permute-start.12 = (f32[1,2,8,128]{3,2,1,0:T(8,128)S(1)}, f32[1,2,8,128]{3,2,1,0:T(8,128)S(1)}, u32[]{:S(2)}, u32[]{:S(2)}) collective-permute-start(f32[1,2,8,128]{3,2,1,0:T(8,128)S(1)} %get-tuple-element.65), channel_id=1, source_target_pairs={{0,2},{2,4},{4,6},{6,0},{1,3},{3,5},{5,7},{7,1},{8,10},{10,12},{12... | collective-permute-start | bytes 24584 | tf_op jit(solution)/shard_map/ppermute | solution.py:409
  94.5 3.6 %collective-permute-start.13 = (f32[1,2,8,128]{3,2,1,0:T(8,128)S(1)}, f32[1,2,8,128]{3,2,1,0:T(8,128)S(1)}, u32[]{:S(2)}, u32[]{:S(2)}) collective-permute-start(f32[1,2,8,128]{3,2,1,0:T(8,128)S(1)} %get-tuple-element.66), channel_id=1, source_target_pairs={{2,0},{4,2},{6,4},{0,6},{3,1},{5,3},{7,5},{1,7},{10,8},{12,10},{14... | collective-permute-start | bytes 24584 | tf_op jit(solution)/shard_map/ppermute | solution.py:410
  98.2 3.2 %collective-permute-start.15 = (f32[1,5,8,128]{3,2,1,0:T(8,128)S(1)}, f32[1,5,8,128]{3,2,1,0:T(8,128)S(1)}, u32[]{:S(2)}, u32[]{:S(2)}) collective-permute-start(f32[1,5,8,128]{3,2,1,0:T(8,128)S(1)} %shard_map.111), channel_id=1, source_target_pairs={{8,0},{16,8},{24,16},{32,24},{40,32},{48,40},{56,48},{64,56},{72,6... | collective-permute-start | bytes 61448 | tf_op jit(solution)/shard_map/ppermute | solution.py:413
  98.9 6.0 %collective-permute-start.14 = (f32[1,5,8,128]{3,2,1,0:T(8,128)S(1)}, f32[1,5,8,128]{3,2,1,0:T(8,128)S(1)}, u32[]{:S(2)}, u32[]{:S(2)}) collective-permute-start(f32[1,5,8,128]{3,2,1,0:T(8,128)S(1)} %shard_map.111), channel_id=1, source_target_pairs={{0,8},{8,16},{16,24},{24,32},{32,40},{40,48},{48,56},{56,64},{64,7... | collective-permute-start | bytes 61448 | tf_op jit(solution)/shard_map/ppermute | solution.py:413
  107.8 3.7 %collective-permute-start.16 = (f32[2,128]{1,0:T(2,128)S(1)}, f32[2,128]{1,0:T(2,128)S(1)}, u32[]{:S(2)}, u32[]{:S(2)}) collective-permute-start(f32[2,128]{1,0:T(2,128)S(1)} %get-tuple-element.68.mine_ref), channel_id=1, source_target_pairs={{0,1},{1,0},{2,3},{3,2},{4,5},{5,4},{6,7},{7,6},{8,9},{9,8},{10,11... | collective-permute-start | bytes 3080 | tf_op jit(solution)/shard_map/ppermute | solution.py:393
  130.3 3.0 %collective-permute-start.17 = (f32[1,128]{1,0:T(1,128)S(1)}, f32[1,128]{1,0:T(1,128)S(1)}, u32[]{:S(2)}, u32[]{:S(2)}) collective-permute-start(f32[1,128]{1,0:T(1,128)S(1)} %get-tuple-element.71.mine_ref), channel_id=1, source_target_pairs={{0,1},{1,0},{2,3},{3,2},{4,5},{5,4},{6,7},{7,6},{8,9},{9,8},{10,11... | collective-permute-start | bytes 1544 | tf_op jit(solution)/shard_map/ppermute | solution.py:393

commit v7 on v6

--- a/solution.py
+++ b/solution.py
@@ -94,11 +94,9 @@
     packed_ref[0:8, :] = jnp.broadcast_to(project(basis_ref, residual_ref[...], part_ref, second_ref[0]), (8, SLOTS))
 
 
-def top_face_kernel(second_ref, field_ref, face_ref):
-    second = second_ref[0]
-    for f in range(field_ref.shape[0]):
-        for y in range(2):
-            face_ref[f, y : y + 1, :] = facing(field_ref[f, y], second)
+def put_face(face_ref, field, second):
+    for y in range(2):
+        face_ref[0, y : y + 1, :] = facing(field[y], second)
 
 
 def side_faces_kernel(field_ref, across_ref, up_ref, down_ref):
@@ -281,21 +279,28 @@
     return jnp.sum(jnp.where(lane == at, rows, 0.0))
 
 
-def first_smooth_kernel(gathered_ref, coarse_ref, basis_ref, live_ref, residual_ref, inverse_ref, smoothed_ref, part_ref):
+def first_smooth_kernel(
+    second_ref, gathered_ref, coarse_ref, basis_ref, live_ref, residual_ref, inverse_ref,
+    smoothed_ref, face_ref, part_ref,
+):
     lifted = coarse_lift(gathered_ref, coarse_ref, basis_ref, part_ref)
-    smoothed_ref[...] = residual_ref[...] * inverse_ref[...] + live_ref[...] * lifted
+    smoothed = residual_ref[...] * inverse_ref[...] + live_ref[...] * lifted
+    smoothed_ref[...] = smoothed
+    put_face(face_ref, smoothed, second_ref[0])
 
 
 def second_smooth_kernel(
-    gathered_ref, coefficient_ref, coarse_ref, basis_ref, live_ref, residual_ref, inverse_ref,
-    smoothed_ref, image_ref, new_coefficient_ref, new_residual_ref, new_smoothed_ref, part_ref,
+    second_ref, gathered_ref, coefficient_ref, coarse_ref, basis_ref, live_ref, residual_ref, inverse_ref,
+    smoothed_ref, image_ref, new_coefficient_ref, new_residual_ref, new_smoothed_ref, face_ref, part_ref,
 ):
     step = total_of(gathered_ref, 0) / total_of(gathered_ref, 1)
     new_coefficient_ref[...] = coefficient_ref[...] - step * gathered_ref[pl.ds(0, 128, stride=2), :]
     lifted = coarse_lift(new_coefficient_ref, coarse_ref, basis_ref, part_ref)
     residual = residual_ref[...] - step * image_ref[...]
     new_residual_ref[...] = residual
-    new_smoothed_ref[...] = residual * inverse_ref[...] + live_ref[...] * lifted
+    smoothed = residual * inverse_ref[...] + live_ref[...] * lifted
+    new_smoothed_ref[...] = smoothed
+    put_face(face_ref, smoothed, second_ref[0])
 
 
 def third_smooth_kernel(
@@ -399,10 +404,8 @@
     return up, [(j, i) for i, j in up]
 
 
-def around(field, second, gy_spot, across=None):
+def around(field, gy_spot, across):
     count = field.shape[0]
-    if across is None:
-        across = swap(call(top_face_kernel, f32(count, 2, SLOTS), [SM, VM])(second, field))
     side = f32(count, 2, 8, SLOTS)
     upper, lower = call(side_faces_kernel, (side, side), [VM] * 2)(field, across)
     up, down = turns("gy")
@@ -451,7 +454,7 @@
     counts, dirichlet, basis = onchip(counts), onchip(dirichlet), onchip(basis)
     theirs = swap(packed)
     coefficient = gather(packed, theirs, 1)
-    block, before, after = around(geometry, second, gy_spot, theirs)
+    block, before, after = around(geometry, gy_spot, theirs)
     coefficient, block, centre = lax.optimization_barrier((coefficient, block, geometry))
     mine = call(centre_kernel, f32(16, 4, SLOTS, SLOTS), [VM])(centre)
 
@@ -471,8 +474,8 @@
     )(second, gx_spot, counts, before, after, sums, mine, live, dirichlet, outside(coarse_inverse))
     weight_a, weight_b, weight_c, coarse = map(onchip, (weight_a, weight_b, weight_c, coarse))
 
-    def image_of(field, residual, *olds):
-        block, before, after = (piece[0] for piece in around(field[None], second, gy_spot))
+    def image_of(field, face, residual, *olds):
+        block, before, after = (piece[0] for piece in around(field[None], gy_spot, swap(face)))
         sums = call(middle_image_kernel, sums_shape, [SM, SM] + [VM] * 2, [vmem(1, 4, 10, 8, SLOTS)])(
             second, counts, weight_b, block
         )
@@ -486,15 +489,16 @@
             live, diagonal, residual, basis, *olds,
         )
 
-    smoothed = call(first_smooth_kernel, cells, [VM] * 6, [part])(
-        coefficient, coarse, basis, live, residual, inverse
-    )
-    image, payload = image_of(smoothed, residual)
+    face_shape = f32(1, 2, SLOTS)
+    smoothed, face = call(first_smooth_kernel, (cells, face_shape), [SM] + [VM] * 6, [part])(
+        second, coefficient, coarse, basis, live, residual, inverse
+    )
+    image, payload = image_of(smoothed, face, residual)
     gathered_first = gather(payload)
-    coefficient, residual, second_smoothed = call(
-        second_smooth_kernel, (f32(128, SLOTS), cells, cells), [VM] * 9, [part]
-    )(gathered_first, coefficient, coarse, basis, live, residual, inverse, smoothed, image)
-    second_image, payload = image_of(second_smoothed, residual, smoothed, image)
+    coefficient, residual, second_smoothed, face = call(
+        second_smooth_kernel, (f32(128, SLOTS), cells, cells, face_shape), [SM] + [VM] * 9, [part]
+    )(second, gathered_first, coefficient, coarse, basis, live, residual, inverse, smoothed, image)
+    second_image, payload = image_of(second_smoothed, face, residual, smoothed, image)
     gathered = gather(payload)
     pressure, residual, third_smoothed, direction, payload = call(
         third_smooth_kernel,

time: 150 us -> 151 us (level)
  starting transfers between devices: 46.4 us -> 48.8 us
  Pallas kernels: 33.5 us -> 31.4 us
    ppermute x6, starting transfers between devices: 13.6 us -> 15.2 us  [swap(): return lax.ppermute(x, 'gz', [(0, 1), (1, 0)])]
  transfers between devices with their start and end apart: 19 -> 19, of which waited for: 13 -> 12; matrix products, arithmetic and copies ran while one was open for 0% -> 0% of each run, Pallas kernels for 7% -> 7%
where the time goes in v7:
time: 151 us; the launch traced here: 150 us
  blocking collectives  51.4 us (34%)
  starting transfers between devices  48.8 us (32%)
  Pallas kernels  31.4 us (21%)
  waiting for transfers between devices  17.9 us (12%)
    all_to_all x3, blocking collectives, gather(): got = lax.all_to_all(spread, ('gx', 'gy'), 0, 0, tiled=True)  51.4 us
    ppermute x6, starting transfers between devices, swap(): return lax.ppermute(x, 'gz', [(0, 1), (1, 0)])  15.2 us
    all_to_all x1, starting transfers between devices, gather(): got = lax.all_to_all(spread, ('gx', 'gy'), 0, 0, tiled=True)  13.8 us
    pallas_call x1, Pallas kernels, per_device(): call(outer_weights_kernel, (weight_shape, weight_shape, cells, cells, vme...  10.2 us
    ppermute x3, starting transfers between devices, around(): lax.ppermute(block, 'gx', down)  9.72 us
    ppermute x3, waiting for transfers between devices, around(): lax.ppermute(block, 'gx', up)  7.77 us
    ppermute x3, starting transfers between devices, around(): above = lax.ppermute(lower, 'gy', down)  7.1 us
    pallas_call x1, Pallas kernels, per_device(): call(middle_weights_kernel, (weight_shape, sums_shape), [SM, SM] + [VM] *...  5.62 us
  transfers between devices with their start and end apart: 19, of which 12 were waited for; matrix products, arithmetic and copies ran while one was open for 0% of the time, Pallas kernels for 7%

profile of v7, /device:TPU:1, one launch (start us, length us, event | category | flops | bytes accessed | tf_op | source)
XLA Modules:
  0.0 150.3 jit_solution(16677882654941363562)
XLA Ops:
  0.6 1.4 shard_map.94
  2.1 3.3 %collective-permute-start = (f32[16,128]{1,0:T(8,128)S(1)}, f32[16,128]{1,0:T(8,128)S(1)}, u32[]{:S(2)}, u32[]{:S(2)}) collective-permute-start(f32[16,128]{1,0:T(8,128)S(1)} %get-tuple-element.46.mine_ref), channel_id=1, source_target_pairs={{0,1},{1,0},{2,3},{3,2},{4,5},{5,4},{6,7},{7,6},{8,9},{9,8},{10,11... | collective-permute-start | bytes 24584 | tf_op jit(solution)/shard_map/ppermute | solution.py:398
  5.4 0.8 collective-permute-done.across_ref.theirs_ref
  6.2 0.7 shard_map.97
  6.9 13.8 %all-to-all-start = ((f32[128,1,128]{2,1,0:T(1,128)}), f32[128,1,128]{2,1,0:T(1,128)S(1)}, u32[]{:S(2)}, u32[]{:S(2)}) async-start(f32[128,1,128]{2,1,0:T(1,128)} %shard_map.97), calls=%async_computation | async-start | bytes 131072 | tf_op jit(solution)/shard_map/all_to_all | solution.py:423
  20.7 0.7 collective-permute-start.1
  21.3 2.1 %collective-permute-start.2 = (f32[4,2,8,128]{3,2,1,0:T(8,128)S(1)}, f32[4,2,8,128]{3,2,1,0:T(8,128)S(1)}, u32[]{:S(2)}, u32[]{:S(2)}) collective-permute-start(f32[4,2,8,128]{3,2,1,0:T(8,128)S(1)} %get-tuple-element.48), channel_id=1, source_target_pairs={{2,0},{4,2},{6,4},{0,6},{3,1},{5,3},{7,5},{1,7},{10,8},{12,10},{14... | collective-permute-start | bytes 98312 | tf_op jit(solution)/shard_map/ppermute | solution.py:413
  23.4 1.6 %collective-permute-done.1.below_ref = f32[4,2,8,128]{3,2,1,0:T(8,128)S(1)} collective-permute-done((f32[4,2,8,128]{3,2,1,0:T(8,128)S(1)}, f32[4,2,8,128]{3,2,1,0:T(8,128)S(1)}, u32[]{:S(2)}, u32[]{:S(2)}) %collective-permute-start.1) | collective-permute-done | bytes 32800 | tf_op jit(solution)/shard_map/ppermute | solution.py:412
  25.0 0.0 collective-permute-done.2.above_ref
  25.1 4.7 %collective-permute-start.4 = (f32[4,5,8,128]{3,2,1,0:T(8,128)S(1)}, f32[4,5,8,128]{3,2,1,0:T(8,128)S(1)}, u32[]{:S(2)}, u32[]{:S(2)}) collective-permute-start(f32[4,5,8,128]{3,2,1,0:T(8,128)S(1)} %shard_map.96.block_ref), channel_id=1, source_target_pairs={{8,0},{16,8},{24,16},{32,24},{40,32},{48,40},{56,48},{64,56},{72,6... | collective-permute-start | bytes 245768 | tf_op jit(solution)/shard_map/ppermute | solution.py:416
  29.8 0.0 collective-permute-start.3
  29.8 1.5 all-to-all-done
  31.3 1.3 shard_map.98.mine_ref
  32.6 5.6 %shard_map.99 = (f32[16,16,9,8,128]{4,3,2,1,0:T(8,128)S(1)}, f32[16,128,128]{2,1,0:T(8,128)S(1)}) custom-call(s32[1]{0:T(128)} %bitcast.second_ref, s32[1,2,8]{2,1,0:T(2,128)S(1)} %get-tuple-element.44.counts_ref, f32[16,4,128,128]{3,2,1,0:T(8,128)S(1)} %shard_map.98.mine_ref, f32[4,5,8,128]{3,2,1,0:T(8,128)S(1)} %shard_map.96.block_ref), custom_call_target="tpu_custom_call" | custom-call | tf_op jit(solution)/shard_map/pallas_call | solution.py:463
  38.2 0.0 collective-permute-done.4.after_ref
  38.2 0.0 collective-permute-done.3.before_ref
  38.2 10.2 %shard_map.100 = (f32[16,16,9,8,128]{4,3,2,1,0:T(8,128)S(1)}, f32[16,16,9,8,128]{4,3,2,1,0:T(8,128)S(1)}, f32[2,8,128]{2,1,0:T(8,128)S(1)}, f32[2,8,128]{2,1,0:T(8,128)S(1)}, f32[64,16384]{1,0:T(8,128)S(1)}) custom-call(s32[1]{0:T(128)} %bitcast.second_ref, s32[1]{0:T(128)} %bitcast.6.spot_ref, s32[1,2,8]{2,1,0:T(2,128)S(1)} %get-tuple-element.44.counts_ref, ...), custom_call_target="tpu_custom_call" | custom-call | tf_op jit(solution)/shard_map/pallas_call | solution.py:469
  48.4 0.7 shard_map.101
  49.1 1.5 collective-permute-start.5
  50.6 0.8 collective-permute-done.5.across_ref
  51.4 1.5 collective-permute-start.6
  52.9 2.4 %collective-permute-start.7 = (f32[1,2,8,128]{3,2,1,0:T(8,128)S(1)}, f32[1,2,8,128]{3,2,1,0:T(8,128)S(1)}, u32[]{:S(2)}, u32[]{:S(2)}) collective-permute-start(f32[1,2,8,128]{3,2,1,0:T(8,128)S(1)} %get-tuple-element.64), channel_id=1, source_target_pairs={{2,0},{4,2},{6,4},{0,6},{3,1},{5,3},{7,5},{1,7},{10,8},{12,10},{14... | collective-permute-start | bytes 24584 | tf_op jit(solution)/shard_map/ppermute | solution.py:413
  55.3 1.0 collective-permute-done.6.below_ref
  56.3 0.0 collective-permute-done.7.above_ref
  56.3 4.3 %collective-permute-start.9 = (f32[1,5,8,128]{3,2,1,0:T(8,128)S(1)}, f32[1,5,8,128]{3,2,1,0:T(8,128)S(1)}, u32[]{:S(2)}, u32[]{:S(2)}) collective-permute-start(f32[1,5,8,128]{3,2,1,0:T(8,128)S(1)} %shard_map.103), channel_id=1, source_target_pairs={{8,0},{16,8},{24,16},{32,24},{40,32},{48,40},{56,48},{64,56},{72,6... | collective-permute-start | bytes 61448 | tf_op jit(solution)/shard_map/ppermute | solution.py:416
  60.6 0.0 collective-permute-start.8
  60.6 1.7 %shard_map.104.old_sums_ref = f32[16,128,128]{2,1,0:T(8,128)S(1)} custom-call(s32[1]{0:T(128)} %bitcast.second_ref, s32[1,2,8]{2,1,0:T(2,128)S(1)} %get-tuple-element.44.counts_ref, f32[16,16,9,8,128]{4,3,2,1,0:T(8,128)S(1)} %get-tuple-element.65.weight_ref, f32[5,8,128]{2,1,0:T(8,128)S(1)} %bitcast.34), custom_call_target="tpu_custom_call" | custom-call | tf_op jit(solution)/shard_map/pallas_call | solution.py:479
  62.3 0.0 collective-permute-done.9
  62.3 4.3 %collective-permute-done.8 = f32[1,5,8,128]{3,2,1,0:T(8,128)S(1)} collective-permute-done((f32[1,5,8,128]{3,2,1,0:T(8,128)S(1)}, f32[1,5,8,128]{3,2,1,0:T(8,128)S(1)}, u32[]{:S(2)}, u32[]{:S(2)}) %collective-permute-start.8) | collective-permute-done | bytes 20512 | tf_op jit(solution)/shard_map/ppermute | solution.py:416
  66.5 2.8 %shard_map.105 = (f32[2,8,128]{2,1,0:T(8,128)S(1)}, f32[2,128]{1,0:T(2,128)S(1)}) custom-call(s32[1]{0:T(128)} %bitcast.second_ref, s32[1,2,8]{2,1,0:T(2,128)S(1)} %get-tuple-element.44.counts_ref, f32[16,16,9,8,128]{4,3,2,1,0:T(8,128)S(1)} %get-tuple-element.54.weight_a, f32[16,16,9,8,128]{4,3,2,1,0:T(8,128)S(1)} %get-tuple-element.55.weight_c, ...), custom_call_target="tpu_custom_call" | custom-call | tf_op jit(solution)/shard_map/pallas_call | solution.py:482
  69.3 3.2 %collective-permute-start.10 = (f32[2,128]{1,0:T(2,128)S(1)}, f32[2,128]{1,0:T(2,128)S(1)}, u32[]{:S(2)}, u32[]{:S(2)}) collective-permute-start(f32[2,128]{1,0:T(2,128)S(1)} %get-tuple-element.67.mine_ref), channel_id=1, source_target_pairs={{0,1},{1,0},{2,3},{3,2},{4,5},{5,4},{6,7},{7,6},{8,9},{9,8},{10,11... | collective-permute-start | bytes 3080 | tf_op jit(solution)/shard_map/ppermute | solution.py:398
  72.5 0.8 collective-permute-done.10.theirs_ref
  73.4 17.2 %all_to_all.20 = f32[128,2,128]{2,1,0:T(2,128)S(1)} all-to-all(f32[128,2,128]{2,1,0:T(2,128)S(1)} %shard_map.106), channel_id=1, replica_groups=mesh['gx'=32,'gy'=4,'gz'=2] {'gx','gy'}, dimensions={0} | all-to-all | bytes 262144 | tf_op jit(solution)/shard_map/all_to_all | solution.py:423
  90.6 0.8 shard_map.107
  91.3 2.1 %collective-permute-start.11 = (f32[1,2,128]{2,1,0:T(2,128)S(1)}, f32[1,2,128]{2,1,0:T(2,128)S(1)}, u32[]{:S(2)}, u32[]{:S(2)}) collective-permute-start(f32[1,2,128]{2,1,0:T(2,128)S(1)} %get-tuple-element.70), channel_id=1, source_target_pairs={{0,1},{1,0},{2,3},{3,2},{4,5},{5,4},{6,7},{7,6},{8,9},{9,8},{10,11... | collective-permute-start | bytes 3080 | tf_op jit(solution)/shard_map/ppermute | solution.py:398
  93.5 0.8 collective-permute-done.11.across_ref
  94.3 0.1 collective-permute-start.12
  94.4 2.6 %collective-permute-start.13 = (f32[1,2,8,128]{3,2,1,0:T(8,128)S(1)}, f32[1,2,8,128]{3,2,1,0:T(8,128)S(1)}, u32[]{:S(2)}, u32[]{:S(2)}) collective-permute-start(f32[1,2,8,128]{3,2,1,0:T(8,128)S(1)} %get-tuple-element.72), channel_id=1, source_target_pairs={{2,0},{4,2},{6,4},{0,6},{3,1},{5,3},{7,5},{1,7},{10,8},{12,10},{14... | collective-permute-start | bytes 24584 | tf_op jit(solution)/shard_map/ppermute | solution.py:413
  97.0 1.0 collective-permute-done.12.below_ref
  98.0 0.0 collective-permute-done.13.above_ref
  98.0 0.7 collective-permute-start.15
  98.7 0.8 collective-permute-start.14
  99.5 1.7 %shard_map.110.old_sums_ref = f32[16,128,128]{2,1,0:T(8,128)S(1)} custom-call(s32[1]{0:T(128)} %bitcast.second_ref, s32[1,2,8]{2,1,0:T(2,128)S(1)} %get-tuple-element.44.counts_ref, f32[16,16,9,8,128]{4,3,2,1,0:T(8,128)S(1)} %get-tuple-element.65.weight_ref, f32[5,8,128]{2,1,0:T(8,128)S(1)} %bitcast.33), custom_call_target="tpu_custom_call" | custom-call | tf_op jit(solution)/shard_map/pallas_call | solution.py:479
  101.2 0.0 collective-permute-done.15
  101.2 3.5 %collective-permute-done.14 = f32[1,5,8,128]{3,2,1,0:T(8,128)S(1)} collective-permute-done((f32[1,5,8,128]{3,2,1,0:T(8,128)S(1)}, f32[1,5,8,128]{3,2,1,0:T(8,128)S(1)}, u32[]{:S(2)}, u32[]{:S(2)}) %collective-permute-start.14) | collective-permute-done | bytes 20512 | tf_op jit(solution)/shard_map/ppermute | solution.py:416
  104.7 2.8 %shard_map.111 = (f32[2,8,128]{2,1,0:T(8,128)S(1)}, f32[2,128]{1,0:T(2,128)S(1)}) custom-call(s32[1]{0:T(128)} %bitcast.second_ref, s32[1,2,8]{2,1,0:T(2,128)S(1)} %get-tuple-element.44.counts_ref, f32[16,16,9,8,128]{4,3,2,1,0:T(8,128)S(1)} %get-tuple-element.54.weight_a, f32[16,16,9,8,128]{4,3,2,1,0:T(8,128)S(1)} %get-tuple-element.55.weight_c, ...), custom_call_target="tpu_custom_call" | custom-call | tf_op jit(solution)/shard_map/pallas_call | solution.py:482
  107.5 3.0 %collective-permute-start.16 = (f32[2,128]{1,0:T(2,128)S(1)}, f32[2,128]{1,0:T(2,128)S(1)}, u32[]{:S(2)}, u32[]{:S(2)}) collective-permute-start(f32[2,128]{1,0:T(2,128)S(1)} %get-tuple-element.74.mine_ref), channel_id=1, source_target_pairs={{0,1},{1,0},{2,3},{3,2},{4,5},{5,4},{6,7},{7,6},{8,9},{9,8},{10,11... | collective-permute-start | bytes 3080 | tf_op jit(solution)/shard_map/ppermute | solution.py:398
  110.5 0.8 collective-permute-done.16.theirs_ref
  111.4 18.1 %all_to_all.21 = f32[128,2,128]{2,1,0:T(2,128)S(1)} all-to-all(f32[128,2,128]{2,1,0:T(2,128)S(1)} %shard_map.112), channel_id=1, replica_groups=mesh['gx'=32,'gy'=4,'gz'=2] {'gx','gy'}, dimensions={0} | all-to-all | bytes 262144 | tf_op jit(solution)/shard_map/all_to_all | solution.py:423
  129.5 0.9 shard_map.113
  130.4 2.1 %collective-permute-start.17 = (f32[1,128]{1,0:T(1,128)S(1)}, f32[1,128]{1,0:T(1,128)S(1)}, u32[]{:S(2)}, u32[]{:S(2)}) collective-permute-start(f32[1,128]{1,0:T(1,128)S(1)} %get-tuple-element.77.mine_ref), channel_id=1, source_target_pairs={{0,1},{1,0},{2,3},{3,2},{4,5},{5,4},{6,7},{7,6},{8,9},{9,8},{10,11... | collective-permute-start | bytes 1544 | tf_op jit(solution)/shard_map/ppermute | solution.py:398
  132.5 0.8 collective-permute-done.17.theirs_ref
  133.4 16.1 %all_to_all.22 = f32[128,1,128]{2,1,0:T(1,128)S(1)} all-to-all(f32[128,1,128]{2,1,0:T(1,128)S(1)} %shard_map.114), channel_id=1, replica_groups=mesh['gx'=32,'gy'=4,'gz'=2] {'gx','gy'}, dimensions={0} | all-to-all | bytes 131072 | tf_op jit(solution)/shard_map/all_to_all | solution.py:423
  149.5 0.8 shard_map.115
  (9 shorter events, 0.1 us)
Async XLA Ops:
  2.1 4.1 %collective-permute-start = (f32[16,128]{1,0:T(8,128)S(1)}, f32[16,128]{1,0:T(8,128)S(1)}, u32[]{:S(2)}, u32[]{:S(2)}) collective-permute-start(f32[16,128]{1,0:T(8,128)S(1)} %get-tuple-element.46.mine_ref), channel_id=1, source_target_pairs={{0,1},{1,0},{2,3},{3,2},{4,5},{5,4},{6,7},{7,6},{8,9},{9,8},{10,11... | collective-permute-start | bytes 24584 | tf_op jit(solution)/shard_map/ppermute | solution.py:398
  6.9 24.4 %all-to-all-start = ((f32[128,1,128]{2,1,0:T(1,128)}), f32[128,1,128]{2,1,0:T(1,128)S(1)}, u32[]{:S(2)}, u32[]{:S(2)}) async-start(f32[128,1,128]{2,1,0:T(1,128)} %shard_map.97), calls=%async_computation | async-start | bytes 131072 | tf_op jit(solution)/shard_map/all_to_all | solution.py:423
  20.7 4.4 %collective-permute-start.1 = (f32[4,2,8,128]{3,2,1,0:T(8,128)S(1)}, f32[4,2,8,128]{3,2,1,0:T(8,128)S(1)}, u32[]{:S(2)}, u32[]{:S(2)}) collective-permute-start(f32[4,2,8,128]{3,2,1,0:T(8,128)S(1)} %get-tuple-element.47), channel_id=1, source_target_pairs={{0,2},{2,4},{4,6},{6,0},{1,3},{3,5},{5,7},{7,1},{8,10},{10,12},{12... | collective-permute-start | bytes 98312 | tf_op jit(solution)/shard_map/ppermute | solution.py:412
  21.3 3.7 %collective-permute-start.2 = (f32[4,2,8,128]{3,2,1,0:T(8,128)S(1)}, f32[4,2,8,128]{3,2,1,0:T(8,128)S(1)}, u32[]{:S(2)}, u32[]{:S(2)}) collective-permute-start(f32[4,2,8,128]{3,2,1,0:T(8,128)S(1)} %get-tuple-element.48), channel_id=1, source_target_pairs={{2,0},{4,2},{6,4},{0,6},{3,1},{5,3},{7,5},{1,7},{10,8},{12,10},{14... | collective-permute-start | bytes 98312 | tf_op jit(solution)/shard_map/ppermute | solution.py:413
  25.1 13.2 %collective-permute-start.4 = (f32[4,5,8,128]{3,2,1,0:T(8,128)S(1)}, f32[4,5,8,128]{3,2,1,0:T(8,128)S(1)}, u32[]{:S(2)}, u32[]{:S(2)}) collective-permute-start(f32[4,5,8,128]{3,2,1,0:T(8,128)S(1)} %shard_map.96.block_ref), channel_id=1, source_target_pairs={{8,0},{16,8},{24,16},{32,24},{40,32},{48,40},{56,48},{64,56},{72,6... | collective-permute-start | bytes 245768 | tf_op jit(solution)/shard_map/ppermute | solution.py:416
  29.8 8.4 %collective-permute-start.3 = (f32[4,5,8,128]{3,2,1,0:T(8,128)S(1)}, f32[4,5,8,128]{3,2,1,0:T(8,128)S(1)}, u32[]{:S(2)}, u32[]{:S(2)}) collective-permute-start(f32[4,5,8,128]{3,2,1,0:T(8,128)S(1)} %shard_map.96.block_ref), channel_id=1, source_target_pairs={{0,8},{8,16},{16,24},{24,32},{32,40},{40,48},{48,56},{56,64},{64,7... | collective-permute-start | bytes 245768 | tf_op jit(solution)/shard_map/ppermute | solution.py:416
  49.1 2.3 %collective-permute-start.5 = (f32[1,2,128]{2,1,0:T(2,128)S(1)}, f32[1,2,128]{2,1,0:T(2,128)S(1)}, u32[]{:S(2)}, u32[]{:S(2)}) collective-permute-start(f32[1,2,128]{2,1,0:T(2,128)S(1)} %get-tuple-element.62), channel_id=1, source_target_pairs={{0,1},{1,0},{2,3},{3,2},{4,5},{5,4},{6,7},{7,6},{8,9},{9,8},{10,11... | collective-permute-start | bytes 3080 | tf_op jit(solution)/shard_map/ppermute | solution.py:398
  51.4 4.9 %collective-permute-start.6 = (f32[1,2,8,128]{3,2,1,0:T(8,128)S(1)}, f32[1,2,8,128]{3,2,1,0:T(8,128)S(1)}, u32[]{:S(2)}, u32[]{:S(2)}) collective-permute-start(f32[1,2,8,128]{3,2,1,0:T(8,128)S(1)} %get-tuple-element.63), channel_id=1, source_target_pairs={{0,2},{2,4},{4,6},{6,0},{1,3},{3,5},{5,7},{7,1},{8,10},{10,12},{12... | collective-permute-start | bytes 24584 | tf_op jit(solution)/shard_map/ppermute | solution.py:412
  52.9 3.4 %collective-permute-start.7 = (f32[1,2,8,128]{3,2,1,0:T(8,128)S(1)}, f32[1,2,8,128]{3,2,1,0:T(8,128)S(1)}, u32[]{:S(2)}, u32[]{:S(2)}) collective-permute-start(f32[1,2,8,128]{3,2,1,0:T(8,128)S(1)} %get-tuple-element.64), channel_id=1, source_target_pairs={{2,0},{4,2},{6,4},{0,6},{3,1},{5,3},{7,5},{1,7},{10,8},{12,10},{14... | collective-permute-start | bytes 24584 | tf_op jit(solution)/shard_map/ppermute | solution.py:413
  56.3 6.0 %collective-permute-start.9 = (f32[1,5,8,128]{3,2,1,0:T(8,128)S(1)}, f32[1,5,8,128]{3,2,1,0:T(8,128)S(1)}, u32[]{:S(2)}, u32[]{:S(2)}) collective-permute-start(f32[1,5,8,128]{3,2,1,0:T(8,128)S(1)} %shard_map.103), channel_id=1, source_target_pairs={{8,0},{16,8},{24,16},{32,24},{40,32},{48,40},{56,48},{64,56},{72,6... | collective-permute-start | bytes 61448 | tf_op jit(solution)/shard_map/ppermute | solution.py:416
  60.6 6.0 %collective-permute-start.8 = (f32[1,5,8,128]{3,2,1,0:T(8,128)S(1)}, f32[1,5,8,128]{3,2,1,0:T(8,128)S(1)}, u32[]{:S(2)}, u32[]{:S(2)}) collective-permute-start(f32[1,5,8,128]{3,2,1,0:T(8,128)S(1)} %shard_map.103), channel_id=1, source_target_pairs={{0,8},{8,16},{16,24},{24,32},{32,40},{40,48},{48,56},{56,64},{64,7... | collective-permute-start | bytes 61448 | tf_op jit(solution)/shard_map/ppermute | solution.py:416
  69.3 4.0 %collective-permute-start.10 = (f32[2,128]{1,0:T(2,128)S(1)}, f32[2,128]{1,0:T(2,128)S(1)}, u32[]{:S(2)}, u32[]{:S(2)}) collective-permute-start(f32[2,128]{1,0:T(2,128)S(1)} %get-tuple-element.67.mine_ref), channel_id=1, source_target_pairs={{0,1},{1,0},{2,3},{3,2},{4,5},{5,4},{6,7},{7,6},{8,9},{9,8},{10,11... | collective-permute-start | bytes 3080 | tf_op jit(solution)/shard_map/ppermute | solution.py:398
  91.3 2.9 %collective-permute-start.11 = (f32[1,2,128]{2,1,0:T(2,128)S(1)}, f32[1,2,128]{2,1,0:T(2,128)S(1)}, u32[]{:S(2)}, u32[]{:S(2)}) collective-permute-start(f32[1,2,128]{2,1,0:T(2,128)S(1)} %get-tuple-element.70), channel_id=1, source_target_pairs={{0,1},{1,0},{2,3},{3,2},{4,5},{5,4},{6,7},{7,6},{8,9},{9,8},{10,11... | collective-permute-start | bytes 3080 | tf_op jit(solution)/shard_map/ppermute | solution.py:398
  94.3 3.7 %collective-permute-start.12 = (f32[1,2,8,128]{3,2,1,0:T(8,128)S(1)}, f32[1,2,8,128]{3,2,1,0:T(8,128)S(1)}, u32[]{:S(2)}, u32[]{:S(2)}) collective-permute-start(f32[1,2,8,128]{3,2,1,0:T(8,128)S(1)} %get-tuple-element.71), channel_id=1, source_target_pairs={{0,2},{2,4},{4,6},{6,0},{1,3},{3,5},{5,7},{7,1},{8,10},{10,12},{12... | collective-permute-start | bytes 24584 | tf_op jit(solution)/shard_map/ppermute | solution.py:412
  94.4 3.6 %collective-permute-start.13 = (f32[1,2,8,128]{3,2,1,0:T(8,128)S(1)}, f32[1,2,8,128]{3,2,1,0:T(8,128)S(1)}, u32[]{:S(2)}, u32[]{:S(2)}) collective-permute-start(f32[1,2,8,128]{3,2,1,0:T(8,128)S(1)} %get-tuple-element.72), channel_id=1, source_target_pairs={{2,0},{4,2},{6,4},{0,6},{3,1},{5,3},{7,5},{1,7},{10,8},{12,10},{14... | collective-permute-start | bytes 24584 | tf_op jit(solution)/shard_map/ppermute | solution.py:413
  98.0 3.1 %collective-permute-start.15 = (f32[1,5,8,128]{3,2,1,0:T(8,128)S(1)}, f32[1,5,8,128]{3,2,1,0:T(8,128)S(1)}, u32[]{:S(2)}, u32[]{:S(2)}) collective-permute-start(f32[1,5,8,128]{3,2,1,0:T(8,128)S(1)} %shard_map.109), channel_id=1, source_target_pairs={{8,0},{16,8},{24,16},{32,24},{40,32},{48,40},{56,48},{64,56},{72,6... | collective-permute-start | bytes 61448 | tf_op jit(solution)/shard_map/ppermute | solution.py:416
  98.7 6.0 %collective-permute-start.14 = (f32[1,5,8,128]{3,2,1,0:T(8,128)S(1)}, f32[1,5,8,128]{3,2,1,0:T(8,128)S(1)}, u32[]{:S(2)}, u32[]{:S(2)}) collective-permute-start(f32[1,5,8,128]{3,2,1,0:T(8,128)S(1)} %shard_map.109), channel_id=1, source_target_pairs={{0,8},{8,16},{16,24},{24,32},{32,40},{40,48},{48,56},{56,64},{64,7... | collective-permute-start | bytes 61448 | tf_op jit(solution)/shard_map/ppermute | solution.py:416
  107.5 3.8 %collective-permute-start.16 = (f32[2,128]{1,0:T(2,128)S(1)}, f32[2,128]{1,0:T(2,128)S(1)}, u32[]{:S(2)}, u32[]{:S(2)}) collective-permute-start(f32[2,128]{1,0:T(2,128)S(1)} %get-tuple-element.74.mine_ref), channel_id=1, source_target_pairs={{0,1},{1,0},{2,3},{3,2},{4,5},{5,4},{6,7},{7,6},{8,9},{9,8},{10,11... | collective-permute-start | bytes 3080 | tf_op jit(solution)/shard_map/ppermute | solution.py:398
  130.4 3.0 %collective-permute-start.17 = (f32[1,128]{1,0:T(1,128)S(1)}, f32[1,128]{1,0:T(1,128)S(1)}, u32[]{:S(2)}, u32[]{:S(2)}) collective-permute-start(f32[1,128]{1,0:T(1,128)S(1)} %get-tuple-element.77.mine_ref), channel_id=1, source_target_pairs={{0,1},{1,0},{2,3},{3,2},{4,5},{5,4},{6,7},{7,6},{8,9},{9,8},{10,11... | collective-permute-start | bytes 1544 | tf_op jit(solution)/shard_map/ppermute | solution.py:398
